TPU v7x, 32 devices: a whole 2x2x4 slice. The times are simulated.
32 devices in a mesh: dp: 8 (over y, x, core), tensor: 4 (over z).
Axes of the slice: x: 2, y: 2, z: 4, core: 2. Of those that a mesh axis runs over, the one named last changes fastest.
Arguments:
- tokens: bfloat16 [32768, 768], P(('dp', 'tensor')), may hold values from -6 to 6
- qkv_weight: bfloat16 [768, 3, 768], P('dp', None, 'tensor'), may hold values from -0.3125 to 0.3125
- qv_bias: float32 [2, 768], replicated, may hold values from -3 to 3
- out_weight: bfloat16 [768, 768], P('dp', 'tensor'), may hold values from -0.875 to 0.875
- out_bias: float32 [768], replicated, may hold values from -2 to 2
- norm1_gain: float32 [768], replicated, may hold values from 0.1 to 1.9
- norm1_shift: float32 [768], replicated, may hold values from -2 to 2
- in_weight: bfloat16 [768, 2, 3072], P('dp', None, 'tensor'), may hold values from -0.21875 to 0.21875
- down_weight: bfloat16 [768, 3072], P('dp', 'tensor'), may hold values from -0.15625 to 0.15625
- down_bias: float32 [768], replicated, may hold values from -2 to 2
- norm2_gain: float32 [768], replicated, may hold values from 0.1 to 1.9
- norm2_shift: float32 [768], replicated, may hold values from -2 to 2
- cotangent: bfloat16 [32768, 768], P(('dp', 'tensor')), may hold values from -6 to 6
Outputs:
- layer_out: bfloat16 [32768, 768], P(('dp', 'tensor'))
- tokens_grad: bfloat16 [32768, 768], P(('dp', 'tensor'))
- qkv_weight_grad: float32 [768, 3, 768], P('dp', None, 'tensor')
- qv_bias_grad: float32 [2, 768], replicated
- out_weight_grad: float32 [768, 768], P('dp', 'tensor')
- out_bias_grad: float32 [768], replicated
- norm1_gain_grad: float32 [768], replicated
- norm1_shift_grad: float32 [768], replicated
- in_weight_grad: float32 [768, 2, 3072], P('dp', None, 'tensor')
- down_weight_grad: float32 [768, 3072], P('dp', 'tensor')
- down_bias_grad: float32 [768], replicated
- norm2_gain_grad: float32 [768], replicated
- norm2_shift_grad: float32 [768], replicated
All inputs are finite; a program needn't handle non-finite values.
Results may differ from a plain program's by a relative error of at most 0.02.
The roundings to bfloat16 on the way count: a program that leaves them out, or rounds other values in their place, can miss the bound.
Values may be sent and summed in bfloat16 or wider, within the bound.
No kernel may reach another device: no remote copies, remote signals or barrier semaphores. Data moves between devices by JAX's collectives and lax.ppermute only.
A program may use at most 192 MiB of HBM per device.

v0:
```python
import math

import jax
import jax.numpy as jnp
from jax import lax
from jax.sharding import PartitionSpec as P

HEAD = 64
SEQ = 1024


NORM_EPS = 1e-12
INV_ROOT_TWO = 0.7071067811865476
INV_ROOT_TWO_PI = 0.3989422804014327


def head_slopes(first_head, head_count):
    head_ids = first_head + jnp.arange(head_count, dtype=jnp.int32)
    powers = jnp.where(
        head_ids < 8, -(head_ids + 1).astype(jnp.float32), 7.5 - head_ids.astype(jnp.float32)
    )
    return jnp.exp2(powers)


def norm_forward(resid, gain, shift):
    center = resid - jnp.mean(resid, axis=1, keepdims=True)
    inverse = lax.rsqrt(jnp.mean(center * center, axis=1, keepdims=True) + NORM_EPS)
    normed = center * inverse
    return (normed * gain + shift, normed, inverse)


def norm_backward(grad_rows, normed, inverse, gain):
    scaled = grad_rows * gain
    first_mean = jnp.mean(scaled, axis=1, keepdims=True)
    second_mean = jnp.mean(scaled * normed, axis=1, keepdims=True)
    d_resid = inverse * (scaled - first_mean - normed * second_mean)
    return (d_resid, jnp.sum(grad_rows * normed, axis=0), jnp.sum(grad_rows, axis=0))


def make_scores(queries, key_rows, slope_value):
    length = queries.shape[0]
    position = jnp.arange(length, dtype=jnp.float32)
    distance = jnp.abs(position[:, None] - position[None, :])
    raw_scores = jnp.einsum("qd,kd->qk", queries, key_rows, preferred_element_type=jnp.float32)
    return raw_scores * (1.0 / math.sqrt(queries.shape[1])) - slope_value * distance


def attend_forward(item):
    queries, key_rows, value_rows, slope_value = item
    scores = make_scores(queries, key_rows, slope_value)
    row_max = jnp.max(scores, axis=1, keepdims=True)
    weights = jnp.exp(scores - row_max)
    row_sum = jnp.sum(weights, axis=1, keepdims=True)
    probs_low = (weights / row_sum).astype(jnp.bfloat16)
    context = jnp.dot(probs_low, value_rows, preferred_element_type=jnp.float32).astype(
        jnp.bfloat16
    )
    return (context, (row_max + jnp.log(row_sum))[:, 0])


def attend_backward(item):
    queries, key_rows, value_rows, log_total, d_context, slope_value = item
    scores = make_scores(queries, key_rows, slope_value)
    probs = jnp.exp(scores - log_total[:, None])
    probs_low = probs.astype(jnp.bfloat16)
    d_values = jnp.einsum("qk,qd->kd", probs_low, d_context, preferred_element_type=jnp.float32)
    d_probs = jnp.einsum("qd,kd->qk", d_context, value_rows, preferred_element_type=jnp.float32)
    inner_sum = jnp.sum(probs * d_probs, axis=1, keepdims=True)
    d_scores = (probs * (d_probs - inner_sum)).astype(jnp.bfloat16)
    scale_factor = 1.0 / math.sqrt(queries.shape[1])
    d_queries = jnp.dot(d_scores, key_rows, preferred_element_type=jnp.float32) * scale_factor
    d_keys = (
        jnp.einsum("qk,qd->kd", d_scores, queries, preferred_element_type=jnp.float32)
        * scale_factor
    )
    return (d_queries, d_keys, d_values)


def to_items(matrix, head_count):
    seq_count = matrix.shape[0] // SEQ
    each_width = matrix.shape[1] // head_count
    shaped = matrix.reshape(seq_count, SEQ, head_count, each_width).transpose(0, 2, 1, 3)
    return shaped.reshape(seq_count * head_count, SEQ, each_width)


def from_items(items, head_count):
    seq_count = items.shape[0] // head_count
    shaped = items.reshape(seq_count, head_count, SEQ, items.shape[2]).transpose(0, 2, 1, 3)
    return shaped.reshape(seq_count * SEQ, head_count * items.shape[2])


def fetch_weights(qkv_weight, in_weight, out_weight, down_weight):
    qkv_rows, in_rows, out_rows, down_rows = (
        lax.all_gather(qkv_weight, "dp", axis=0, tiled=True),
        lax.all_gather(in_weight, "dp", axis=0, tiled=True),
        lax.all_gather(out_weight, "dp", axis=0, tiled=True),
        lax.all_gather(down_weight, "dp", axis=0, tiled=True),
    )
    return (qkv_rows, in_rows, out_rows, down_rows)


def gelu_parts(gate_part):
    normal_cdf = 0.5 * (1.0 + lax.erf(gate_part * INV_ROOT_TWO))
    density = jnp.exp(-0.5 * gate_part * gate_part) * INV_ROOT_TWO_PI
    return (gate_part * normal_cdf, normal_cdf + gate_part * density)


def local(
    tokens,
    qkv_weight,
    qv_bias,
    out_weight,
    out_bias,
    norm1_gain,
    norm1_shift,
    in_weight,
    down_weight,
    down_bias,
    norm2_gain,
    norm2_shift,
    cotangent,
):
    model_width = tokens.shape[1]
    qkv_full, in_full, out_full, down_full = fetch_weights(
        qkv_weight, in_weight, out_weight, down_weight
    )
    local_width = qkv_full.shape[2]
    hidden_width = in_full.shape[2]
    head_count = local_width // HEAD
    col_start = lax.axis_index("tensor") * local_width
    group_rows = lax.all_gather(tokens, "tensor", axis=0, tiled=True)
    seq_count = group_rows.shape[0] // SEQ
    item_slopes = jnp.tile(head_slopes(col_start // HEAD, head_count), seq_count)
    bias_local = lax.dynamic_slice_in_dim(qv_bias, col_start, local_width, 1)
    projected = jnp.dot(
        group_rows,
        qkv_full.reshape(model_width, 3 * local_width),
        preferred_element_type=jnp.float32,
    )
    queries = (projected[:, :local_width] + bias_local[0]).astype(jnp.bfloat16)
    key_rows = projected[:, local_width : 2 * local_width].astype(jnp.bfloat16)
    value_rows = (projected[:, 2 * local_width :] + bias_local[1]).astype(jnp.bfloat16)
    query_items = to_items(queries, head_count)
    key_items = to_items(key_rows, head_count)
    value_items = to_items(value_rows, head_count)
    context_items, log_totals = lax.map(
        attend_forward, (query_items, key_items, value_items, item_slopes)
    )
    context = from_items(context_items, head_count)
    attn_partial = jnp.einsum("rc,oc->ro", context, out_full, preferred_element_type=jnp.float32)
    attention = lax.psum_scatter(attn_partial, "tensor", scatter_dimension=0, tiled=True)
    resid1 = tokens.astype(jnp.float32) + attention + out_bias
    hidden1, normed1, inverse1 = norm_forward(resid1, norm1_gain, norm1_shift)
    hidden1_low = hidden1.astype(jnp.bfloat16)
    group_hidden = lax.all_gather(hidden1_low, "tensor", axis=0, tiled=True)
    gate_up = jnp.dot(
        group_hidden,
        in_full.reshape(model_width, 2 * hidden_width),
        preferred_element_type=jnp.float32,
    )
    gate_part = gate_up[:, :hidden_width]
    up_part = gate_up[:, hidden_width:]
    activated, slope_gelu = gelu_parts(gate_part)
    gated = (activated * up_part).astype(jnp.bfloat16)
    ffn_partial = jnp.einsum("rf,of->ro", gated, down_full, preferred_element_type=jnp.float32)
    ffn_out = lax.psum_scatter(ffn_partial, "tensor", scatter_dimension=0, tiled=True)
    resid2 = hidden1 + ffn_out + down_bias
    result, normed2, inverse2 = norm_forward(resid2, norm2_gain, norm2_shift)
    d_resid2, norm2_gain_grad, norm2_shift_grad = norm_backward(
        cotangent.astype(jnp.float32), normed2, inverse2, norm2_gain
    )
    down_bias_grad = jnp.sum(d_resid2, axis=0)
    d_ffn_low = d_resid2.astype(jnp.bfloat16)
    group_d_ffn = lax.all_gather(d_ffn_low, "tensor", axis=0, tiled=True)
    qkv_full, in_full, out_full, down_full = fetch_weights(
        qkv_weight, in_weight, out_weight, down_weight
    )
    d_gated = jnp.dot(group_d_ffn, down_full, preferred_element_type=jnp.float32)
    down_grad = jnp.einsum("ro,rf->of", group_d_ffn, gated, preferred_element_type=jnp.float32)
    d_gate_up = jnp.concatenate(
        [d_gated * up_part * slope_gelu, d_gated * activated], axis=1
    ).astype(jnp.bfloat16)
    in_grad = jnp.einsum(
        "rd,rc->dc", group_hidden, d_gate_up, preferred_element_type=jnp.float32
    ).reshape(model_width, 2, hidden_width)
    d_group_hidden = jnp.einsum(
        "rc,dc->rd",
        d_gate_up,
        in_full.reshape(model_width, 2 * hidden_width),
        preferred_element_type=jnp.float32,
    )
    d_hidden_ffn = lax.psum_scatter(d_group_hidden, "tensor", scatter_dimension=0, tiled=True)
    d_hidden1 = d_resid2 + d_hidden_ffn
    d_resid1, norm1_gain_grad, norm1_shift_grad = norm_backward(
        d_hidden1, normed1, inverse1, norm1_gain
    )
    out_bias_grad = jnp.sum(d_resid1, axis=0)
    d_attn_low = d_resid1.astype(jnp.bfloat16)
    group_d_attn = lax.all_gather(d_attn_low, "tensor", axis=0, tiled=True)
    d_context = jnp.dot(group_d_attn, out_full, preferred_element_type=jnp.float32).astype(
        jnp.bfloat16
    )
    out_grad = jnp.einsum("ro,rc->oc", group_d_attn, context, preferred_element_type=jnp.float32)
    d_query_items, d_key_items, d_value_items = lax.map(
        attend_backward,
        (
            query_items,
            key_items,
            value_items,
            log_totals,
            to_items(d_context, head_count),
            item_slopes,
        ),
    )
    d_queries = from_items(d_query_items, head_count)
    d_keys = from_items(d_key_items, head_count)
    d_values = from_items(d_value_items, head_count)
    bias_local_grad = jnp.stack([jnp.sum(d_queries, axis=0), jnp.sum(d_values, axis=0)])
    qv_grad = lax.dynamic_update_slice(
        jnp.zeros((2, model_width), jnp.float32),
        bias_local_grad,
        (jnp.zeros((), jnp.int32), col_start),
    )
    d_projected = jnp.concatenate([d_queries, d_keys, d_values], axis=1).astype(jnp.bfloat16)
    qkv_grad = jnp.einsum(
        "rd,rc->dc", group_rows, d_projected, preferred_element_type=jnp.float32
    ).reshape(model_width, 3, local_width)
    d_group_rows = jnp.einsum(
        "rc,dc->rd",
        d_projected,
        qkv_full.reshape(model_width, 3 * local_width),
        preferred_element_type=jnp.float32,
    )
    d_tokens_attn = lax.psum_scatter(
        d_group_rows.astype(jnp.bfloat16), "tensor", scatter_dimension=0, tiled=True
    ).astype(jnp.float32)
    tokens_grad = (d_resid1 + d_tokens_attn).astype(jnp.bfloat16)
    qkv_grad, in_grad, out_grad, down_grad = (
        lax.psum_scatter(qkv_grad, "dp", scatter_dimension=0, tiled=True),
        lax.psum_scatter(in_grad, "dp", scatter_dimension=0, tiled=True),
        lax.psum_scatter(out_grad, "dp", scatter_dimension=0, tiled=True),
        lax.psum_scatter(down_grad, "dp", scatter_dimension=0, tiled=True),
    )
    (
        qv_grad,
        out_bias_grad,
        norm1_gain_grad,
        norm1_shift_grad,
        down_bias_grad,
        norm2_gain_grad,
        norm2_shift_grad,
    ) = lax.psum(
        (
            qv_grad,
            out_bias_grad,
            norm1_gain_grad,
            norm1_shift_grad,
            down_bias_grad,
            norm2_gain_grad,
            norm2_shift_grad,
        ),
        ("dp", "tensor"),
    )
    return (
        result.astype(jnp.bfloat16),
        tokens_grad,
        qkv_grad,
        qv_grad,
        out_grad,
        out_bias_grad,
        norm1_gain_grad,
        norm1_shift_grad,
        in_grad,
        down_grad,
        down_bias_grad,
        norm2_gain_grad,
        norm2_shift_grad,
    )


def solution(mesh):
    placed = (
        P(("dp", "tensor"), None),
        P("dp", None, "tensor"),
        P(),
        P("dp", "tensor"),
        P(),
        P(),
        P(),
        P("dp", None, "tensor"),
        P("dp", "tensor"),
        P(),
        P(),
        P(),
        P(("dp", "tensor"), None),
    )
    return jax.shard_map(
        local,
        mesh=mesh,
        in_specs=placed,
        out_specs=(
            P(("dp", "tensor"), None),
            P(("dp", "tensor"), None),
            P("dp", None, "tensor"),
            P(),
            P("dp", "tensor"),
            P(),
            P(),
            P(),
            P("dp", None, "tensor"),
            P("dp", "tensor"),
            P(),
            P(),
            P(),
        ),
        check_vma=False,
    )
```

profile of v0, /device:TPU:0, one launch (start us, length us, event | category | flops | bytes accessed | tf_op | source)
XLA Modules:
  0.0 1840.1 jit_solution(1177063377857514128)
XLA Ops:
  10.0 14.6 all_gather.29
  25.5 8.5 all_gather.30
  34.9 93.6 %all-gather.7.cloned.1.call-done = bf16[4096,768]{1,0:T(8,128)(2,1)} async-done(((bf16[1024,768]{1,0:T(8,128)(2,1)}), bf16[4096,768]{1,0:T(8,128)(2,1)}) %all-gather.7.cloned.1.call-update) | async-done | bytes 6291472 | tf_op jit(solution)/shard_map/all_gather | solution.py:131
  128.5 6.0 fusion.74
  143.4 3.9 reshape.186
  147.3 4.5 copy.45
  151.8 3.9 reshape.184
  155.6 4.4 copy.44
  160.1 131.6 %while.26 = (s32[]{:T(128)}, bf16[12,1024,64]{1,2,0:T(8,128)(2,1)}, f32[12,1024]{1,0:T(8,128)}, bf16[12,1024,64]{2,1,0:T(8,128)(2,1)S(1)}, bf16[12,1024,64]{2,1,...) while((s32[]{:T(128)}, bf16[12,1024,64]{1,2,0:T(8,128)(2,1)}, ...), condition=%wide.region_3.4_spmd, body=%wide.region_0.3_spmd.sunk | while | flops 280034304 | bytes 30321288 | solution.py:146
  167.3 3.7 fusion.124
  178.3 3.7 fusion.124
  189.2 3.7 fusion.124
  200.2 3.7 fusion.124
  211.2 3.7 fusion.124
  222.1 3.7 fusion.124
  233.1 3.7 fusion.124
  244.0 3.7 fusion.124
  255.0 3.7 fusion.124
  266.0 3.7 fusion.124
  276.9 3.7 fusion.124
  287.9 3.7 fusion.124
  291.6 3.8 copy.46
  297.2 6.4 fusion.75
  304.5 209.3 %reduce-scatter.8.cloned.1.call-done = f32[1024,768]{1,0:T(8,128)} async-done(((f32[4096,768]{1,0:T(8,128)}), f32[1024,768]{1,0:T(8,128)}) %reduce-scatter.8.cloned.1.call-update) | async-done | bytes 3145744 | tf_op jit(solution)/shard_map/reduce_scatter | solution.py:151
  519.8 3.7 copy.53
  523.5 112.0 %all-gather.9.cloned.1.call-done = bf16[4096,768]{1,0:T(8,128)(2,1)} async-done(((bf16[1024,768]{1,0:T(8,128)(2,1)}), bf16[4096,768]{1,0:T(8,128)(2,1)}) %all-gather.9.cloned.1.call-update) | async-done | bytes 6291472 | tf_op jit(solution)/shard_map/all_gather | solution.py:155
  635.5 17.3 fusion.76
  652.8 12.2 multiply_convert_fusion.2
  665.0 10.4 fusion.77
  675.4 10.0 all-gather.15.cloned.1.call-start
  685.4 200.3 %reduce-scatter.10.cloned.1.call-done = f32[1024,768]{1,0:T(8,128)} async-done(((f32[4096,768]{1,0:T(8,128)}), f32[1024,768]{1,0:T(8,128)}) %reduce-scatter.10.cloned.1.call-update) | async-done | bytes 3145744 | tf_op jit(solution)/shard_map/reduce_scatter | solution.py:166
  898.2 116.5 %all-gather.15.cloned.1.call-done = bf16[4096,768]{1,0:T(8,128)(2,1)} async-done(((bf16[1024,768]{1,0:T(8,128)(2,1)}), bf16[4096,768]{1,0:T(8,128)(2,1)}) %all-gather.15.cloned.1.call-update) | async-done | bytes 6291472 | tf_op jit(solution)/shard_map/all_gather | solution.py:174
  1014.7 22.1 %fusion.50 = (bf16[4096,768]{0,1:T(8,128)(2,1)}, bf16[4096,768]{0,1:T(8,128)(2,1)}) fusion(f32[4096,1536]{0,1:T(8,128)} %fusion.76, bf16[4096,768]{1,0:T(8,128)(2,1)} %all-gather.15.cloned.1.call-done, bf16[768,768]{1,0:T(8,128)(2,1)} %all-gather.13.cloned.1.call-done), kind=kOutput, calls=%fused_computation.57 | convolution fusion | flops 4875878400 | bytes 45219840 | tf_op jit(solution)/shard_map/dot_general | solution.py:178
  1036.9 16.1 fusion.52
  1053.1 210.0 %reduce-scatter.12.cloned.1.call-done = f32[1024,768]{1,0:T(8,128)} async-done(((f32[4096,768]{1,0:T(8,128)}), f32[1024,768]{1,0:T(8,128)}) %reduce-scatter.12.cloned.1.call-update) | async-done | bytes 3145744 | tf_op jit(solution)/shard_map/reduce_scatter | solution.py:192
  1263.1 4.4 multiply_reduce_fusion.1
  1272.7 16.5 fusion.51
  1289.3 6.7 reshape.200
  1296.0 92.8 %all-gather.17.cloned.1.call-done = bf16[4096,768]{1,0:T(8,128)(2,1)} async-done(((bf16[1024,768]{1,0:T(8,128)(2,1)}), bf16[4096,768]{1,0:T(8,128)(2,1)}) %all-gather.17.cloned.1.call-update) | async-done | bytes 6291472 | tf_op jit(solution)/shard_map/all_gather | solution.py:199
  1388.8 6.2 convolution_convert_fusion.1
  1395.0 3.8 reshape.191
  1398.8 4.4 copy.47
  1403.3 167.5 %while.27 = (s32[]{:T(128)}, f32[12,1024,64]{1,2,0:T(8,128)S(1)}, bf16[12,1024,64]{1,2,0:T(8,128)(2,1)}, f32[12,1024,64]{1,2,0:T(8,128)}, bf16[12,1024,64]{2,1,0...) while((s32[]{:T(128)}, f32[12,1024,64]{1,2,0:T(8,128)S(1)}, ...), condition=%wide.region_17.18_spmd, body=%wide.region_15.17_spmd.sunk | while | flops 683801600 | bytes 34104956 | solution.py:204
  1406.4 3.4 multiply_reduce_fusion.7
  1420.3 3.4 multiply_reduce_fusion.7
  1434.2 3.4 multiply_reduce_fusion.7
  1448.2 3.4 multiply_reduce_fusion.7
  1462.1 3.4 multiply_reduce_fusion.7
  1490.1 3.4 multiply_reduce_fusion.7
  1504.0 3.4 multiply_reduce_fusion.7
  1518.0 3.4 multiply_reduce_fusion.7
  1559.8 3.4 multiply_reduce_fusion.7
  1575.3 3.9 copy.61
  1582.4 7.0 convolution_convert_fusion
  1589.5 10.5 fusion.80
  1600.1 5.5 fusion.79
  1605.7 7.6 fusion.78
  1618.5 4.3 bitcast_reduce_fusion
  1622.8 4.2 bitcast_reduce_fusion.1
  1627.3 47.4 %all-reduce.1 = (f32[2,768]{1,0:T(2,128)}, f32[768]{0:T(1024)}, f32[768]{0:T(1024)}, f32[768]{0:T(1024)}, f32[768]{0:T(1024)}, /*index=5*/f32[768]{0:T(1024)}, f32[768]{0:T(1024)}) all-reduce(f32[2,768]{1,0:T(2,128)S(1)} %dynamic_update_slice.21, f32[768]{0:T(1024)S(1)} %copy-done.23, ...), channel_id=1, replica_groups=mesh['dp'=8,'tensor'=4] {'dp','tensor'}, use_global_device_ids=true, to_apply=%region_22.23 | all-reduce | flops 6144 | bytes 49152 | tf_op jit(solution)/shard_map/psum | solution.py:252
  1674.8 24.9 %reduce-scatter.14.cloned.1.call-done = bf16[1024,768]{1,0:T(8,128)(2,1)} async-done(((bf16[4096,768]{1,0:T(8,128)(2,1)}), bf16[1024,768]{1,0:T(8,128)(2,1)}) %reduce-scatter.14.cloned.1.call-update) | async-done | bytes 1572880 | tf_op jit(solution)/shard_map/reduce_scatter | solution.py:234
  1702.5 44.0 %reduce-scatter.20.cloned.1.call-done = f32[96,768]{1,0:T(8,128)} async-done(((f32[768,768]{1,0:T(8,128)}), f32[96,768]{1,0:T(8,128)}) %reduce-scatter.20.cloned.1.call-update) | async-done | bytes 294928 | tf_op jit(solution)/shard_map/reduce_scatter | solution.py:242
  1746.5 39.0 %reduce-scatter.18.cloned.1.call-done = f32[96,192]{1,0:T(8,128)} async-done(((f32[768,192]{1,0:T(8,128)}), f32[96,192]{1,0:T(8,128)}) %reduce-scatter.18.cloned.1.call-update) | async-done | bytes 73744 | tf_op jit(solution)/shard_map/reduce_scatter | solution.py:241
  1785.5 46.8 %reduce-scatter.16.cloned.1.call-done = f32[96,3,192]{2,0,1:T(8,128)} async-done(((f32[768,3,192]{2,0,1:T(8,128)}), f32[96,3,192]{2,0,1:T(8,128)}) %reduce-scatter.16.cloned.1.call-update) | async-done | bytes 221200 | tf_op jit(solution)/shard_map/reduce_scatter | solution.py:239
  (313 shorter events, 277.3 us)
Async XLA Ops:
  8.0 17.5 copy-start.17
  8.0 120.5 %all-gather.7.cloned.1.call-start = ((), (), s32[]{:S(2)}) async-start(), calls=%async_computation.7 | async-start | bytes 7864320 | tf_op jit(solution)/shard_map/all_gather | solution.py:131
  8.8 505.1 %reduce-scatter.8.cloned.1.call-start = ((), (), s32[]{:S(2)}) async-start(), calls=%async_computation.8 | async-start | bytes 15728640 | tf_op jit(solution)/shard_map/reduce_scatter | solution.py:151
  25.5 109.0 %copy-start.13 = (bf16[768,3,192]{0,2,1:T(8,128)(2,1)}, bf16[768,3,192]{0,2,1:T(8,128)(2,1)S(1)}, u32[]{:S(2)}) copy-start(bf16[768,3,192]{0,2,1:T(8,128)(2,1)S(1)} %copy.42) | copy-start | bytes 2654212
  34.1 262.0 %copy-start.9 = (bf16[768,192]{1,0:T(8,128)(2,1)}, bf16[768,192]{1,0:T(8,128)(2,1)S(1)}, u32[]{:S(2)}) copy-start(bf16[768,192]{1,0:T(8,128)(2,1)S(1)} %all_gather.30) | copy-start | bytes 884740
  163.3 1.9 copy-start
  174.3 1.9 copy-start
  185.3 1.9 copy-start
  196.2 1.9 copy-start
  207.2 1.9 copy-start
  218.2 1.9 copy-start
  229.1 1.9 copy-start
  240.1 1.9 copy-start
  251.0 1.9 copy-start
  262.0 1.9 copy-start
  273.0 1.9 copy-start
  283.9 1.9 copy-start
  291.6 4.4 copy-start.7
  291.6 4.4 copy-start.29
  296.1 1.1 copy-start.5
  303.6 210.3 %copy-start.27 = (f32[768]{0:T(1024)S(1)}, f32[768]{0:T(1024)}, u32[]{:S(2)}) copy-start(f32[768]{0:T(1024)} %param.21) | copy-start | bytes 9220
  303.7 216.1 %all-gather.11.cloned.1.call-start = ((), (), s32[]{:S(2)}) async-start(), calls=%async_computation.10 | async-start | bytes 2654208 | tf_op jit(solution)/shard_map/all_gather | solution.py:95
  304.2 331.3 %all-gather.9.cloned.1.call-start = ((), (), s32[]{:S(2)}) async-start(), calls=%async_computation.9 | async-start | bytes 7864320 | tf_op jit(solution)/shard_map/all_gather | solution.py:155
  516.7 0.7 copy-start.16
  516.7 0.7 copy-start.22
  519.1 145.8 %all-gather.13.cloned.1.call-start = ((), (), s32[]{:S(2)}) async-start(), calls=%async_computation.11 | async-start | bytes 1327104 | tf_op jit(solution)/shard_map/all_gather | solution.py:97
  519.7 365.9 %reduce-scatter.10.cloned.1.call-start = ((), (), s32[]{:S(2)}) async-start(), calls=%async_computation.12 | async-start | bytes 15728640 | tf_op jit(solution)/shard_map/reduce_scatter | solution.py:166
  675.3 210.3 %copy-start.28 = (f32[768]{0:T(1024)S(1)}, f32[768]{0:T(1024)}, u32[]{:S(2)}) copy-start(f32[768]{0:T(1024)} %param.26) | copy-start | bytes 9220
  675.4 339.4 %all-gather.15.cloned.1.call-start = ((), (), s32[]{:S(2)}) async-start(), calls=%async_computation.13 | async-start | bytes 7864320 | tf_op jit(solution)/shard_map/all_gather | solution.py:174
  888.6 1.4 copy-start.8
  888.6 1.4 copy-start.21
  889.1 3.2 copy-start.26
  895.2 1.6 copy-start.1
  898.2 364.9 %reduce-scatter.12.cloned.1.call-start = ((), (), s32[]{:S(2)}) async-start(), calls=%async_computation.14 | async-start | bytes 15728640 | tf_op jit(solution)/shard_map/reduce_scatter | solution.py:192
  1014.7 22.1 %copy-start.11 = (bf16[96,8,2,768]{3,1,2,0:T(8,128)(2,1)S(1)}, bf16[96,8,2,768]{3,1,2,0:T(8,128)(2,1)}, u32[]{:S(2)}) copy-start(bf16[96,8,2,768]{3,1,2,0:T(8,128)(2,1)} %copy.53) | copy-start | bytes 7077892
  1053.0 335.8 %all-gather.17.cloned.1.call-start = ((), (), s32[]{:S(2)}) async-start(), calls=%async_computation.15 | async-start | bytes 7864320 | tf_op jit(solution)/shard_map/all_gather | solution.py:199
  1269.2 1.7 copy-start.2
  1272.2 344.2 %all-reduce.4.cloned.1.call-start = ((), (), s32[]{:S(2)}) async-start(), calls=%async_computation.20 | async-start | bytes 9437184
  1295.9 92.9 %copy-start.10 = (bf16[768,192]{1,0:T(8,128)(2,1)S(1)}, bf16[768,192]{1,0:T(8,128)(2,1)}, u32[]{:S(2)}) copy-start(bf16[768,192]{1,0:T(8,128)(2,1)} %copy-done.9) | copy-start | bytes 884740
  1295.9 403.7 %reduce-scatter.14.cloned.1.call-start = ((), (), s32[]{:S(2)}) async-start(), calls=%async_computation.16 | async-start | bytes 7864320 | tf_op jit(solution)/shard_map/reduce_scatter | solution.py:234
  1398.8 4.5 copy-start.30
  1570.8 2.7 copy-start.4
  1570.8 2.7 copy-start.12
  1580.0 2.4 copy-start.14
  1580.3 2.1 copy-start.15
  1589.5 10.6 copy-start.6
  1589.5 157.0 %reduce-scatter.20.cloned.1.call-start = ((), (), s32[]{:S(2)}) async-start(), calls=%async_computation.19 | async-start | bytes 2654208 | tf_op jit(solution)/shard_map/reduce_scatter | solution.py:242
  1600.0 185.5 %reduce-scatter.18.cloned.1.call-start = ((), (), s32[]{:S(2)}) async-start(), calls=%async_computation.18 | async-start | bytes 884736 | tf_op jit(solution)/shard_map/reduce_scatter | solution.py:241
  1605.6 226.7 %reduce-scatter.16.cloned.1.call-start = ((), (), s32[]{:S(2)}) async-start(), calls=%async_computation.17 | async-start | bytes 2654208 | tf_op jit(solution)/shard_map/reduce_scatter | solution.py:239
  1613.2 2.0 copy-start.31
  1618.4 8.8 copy-start.18
  1618.4 8.8 copy-start.19
  1618.4 8.9 copy-start.20
  1618.4 8.9 copy-start.23
  1618.4 8.9 copy-start.24
  1618.4 8.9 copy-start.25
  1618.5 81.2 %copy-start.3 = (f32[1024,768]{1,0:T(8,128)S(1)}, f32[1024,768]{1,0:T(8,128)}, u32[]{:S(2)}) copy-start(f32[1024,768]{1,0:T(8,128)} %copy-done.2) | copy-start | bytes 9437188
Sparse Core Ops, SparseCore 0:
  10.4 118.0 all-gather.6
  303.8 210.0 reduce-scatter.7
  898.3 116.3 all-gather.14
  1272.4 116.3 all-gather.16
  1589.6 110.0 reduce-scatter.13
  1703.4 43.0 reduce-scatter.19
  1750.5 34.9 reduce-scatter.17
  1789.8 42.4 reduce-scatter.15
Sparse Core Ops, SparseCore 1:
  306.0 27.0 all-gather.10
  519.2 116.2 all-gather.8
  637.3 22.1 all-gather.12
  675.4 210.2 reduce-scatter.9
  1053.1 209.9 reduce-scatter.11
  1296.0 87.4 all-reduce.3
where the time goes:
time: 1850 us; the launch traced here: 1840 us
  waiting for transfers between devices  1190 us (64%)
  matrix products  346 us (19%)
  local copies, waits for them, and re-layouts  134 us (7%)
  blocking collectives  70.6 us (4%)
  other arithmetic  69.1 us (4%)
    reduce_scatter x1, waiting for transfers between devices, local(): lax.psum_scatter(d_group_hidden, 'tensor', scatter_dimension=0, tiled=True)  210 us
    reduce_scatter x1, waiting for transfers between devices, local(): lax.psum_scatter(attn_partial, 'tensor', scatter_dimension=0, tiled=True)  209 us
    reduce_scatter x1, waiting for transfers between devices, local(): lax.psum_scatter(ffn_partial, 'tensor', scatter_dimension=0, tiled=True)  200 us
    all_gather x1, waiting for transfers between devices, local(): group_d_ffn = lax.all_gather(d_ffn_low, 'tensor', axis=0, tiled=True)  116 us
    all_gather x1, waiting for transfers between devices, local(): group_hidden = lax.all_gather(hidden1_low, 'tensor', axis=0, tiled=True)  112 us
    all_gather x1, waiting for transfers between devices, local(): group_rows = lax.all_gather(tokens, 'tensor', axis=0, tiled=True)  93.6 us
    all_gather x1, waiting for transfers between devices, local(): group_d_attn = lax.all_gather(d_attn_low, 'tensor', axis=0, tiled=True)  92.8 us
    dot_general x24, matrix products, make_scores(): jnp.einsum('qd,kd->qk', queries, key_rows, preferred_element_type=jnp.flo...  73 us
  transfers between devices with their start and end apart: 14, of which 11 were waited for; matrix products, arithmetic and copies ran while one was open for 16% of the time, Pallas kernels for 0%

commit v1 on v0

v1 whole, which is shorter than its diff:
```python
import functools
import math

import jax
import jax.numpy as jnp
from jax import lax
from jax.experimental import pallas as pl
from jax.experimental.pallas import tpu as pltpu
from jax.sharding import PartitionSpec as P

HEAD = 64
SEQ = 1024
GROUP = 4
QB = 256
LOG2E = 1.4426950408889634
SCALE = LOG2E / math.sqrt(HEAD)
NT = (((1,), (1,)), ((), ()))
NN = (((1,), (0,)), ((), ()))


def mm(left, right, dims=NN):
    return lax.dot_general(left, right, dims, preferred_element_type=jnp.float32)


def fill_row_distance(dist_ref):
    shape = dist_ref.shape
    row = lax.broadcasted_iota(jnp.int32, shape, 0)
    col = lax.broadcasted_iota(jnp.int32, shape, 1)
    dist_ref[...] = jnp.abs(row - col + (SEQ - QB)).astype(jnp.float32) * LOG2E


def attend_kernel(slope_ref, qkv_ref, ctx_ref, lse_ref, dist_ref):
    hh = pl.program_id(0)
    width = GROUP * HEAD

    @pl.when(hh == 0)
    def _():
        fill_row_distance(dist_ref)

    lane = lax.broadcasted_iota(jnp.int32, (1, 128), 1)
    for pair in range(GROUP // 2):
        keys = qkv_ref[:, width + 128 * pair : width + 128 * pair + 128]
        values = qkv_ref[:, 2 * width + 128 * pair : 2 * width + 128 * pair + 128]
        for block in range(SEQ // QB):
            rows = slice(block * QB, (block + 1) * QB)
            q = qkv_ref[rows, 128 * pair : 128 * pair + 128]
            parts = []
            stats = []
            for side in range(2):
                own = (lane < HEAD) if side == 0 else (lane >= HEAD)
                slope = slope_ref[hh * GROUP + 2 * pair + side]
                s = mm(jnp.where(own, q, jnp.zeros_like(q)), keys, NT) * SCALE
                s = s - slope * dist_ref[:, SEQ - QB - block * QB : 2 * SEQ - QB - block * QB]
                top = jnp.max(s, axis=1, keepdims=True)
                w = jnp.exp2(s - top)
                total = jnp.sum(w, axis=1, keepdims=True)
                p = (w * (1.0 / total)).astype(jnp.bfloat16)
                parts.append(mm(p, values))
                stats.append(top + jnp.log2(total))
            ctx = jnp.where(lane < HEAD, parts[0], parts[1])
            ctx_ref[rows, 128 * pair : 128 * pair + 128] = ctx.astype(jnp.bfloat16)
            stat = jnp.where(lane < HEAD, stats[0], stats[1])
            flipped = stat.T
            lse_ref[2 * pair : 2 * pair + 1, rows] = flipped[0:1, :]
            lse_ref[2 * pair + 1 : 2 * pair + 2, rows] = flipped[HEAD : HEAD + 1, :]


def attend_forward(qkv, slopes):
    groups = qkv.shape[1] // (3 * GROUP * HEAD)
    return pl.pallas_call(
        attend_kernel,
        grid=(groups,),
        in_specs=[
            pl.BlockSpec(memory_space=pltpu.SMEM),
            pl.BlockSpec((SEQ, 3 * GROUP * HEAD), lambda g: (0, g)),
        ],
        out_specs=[
            pl.BlockSpec((SEQ, GROUP * HEAD), lambda g: (0, g)),
            pl.BlockSpec((None, GROUP, SEQ), lambda g: (g, 0, 0)),
        ],
        out_shape=[
            jax.ShapeDtypeStruct((SEQ, groups * GROUP * HEAD), jnp.bfloat16),
            jax.ShapeDtypeStruct((groups, GROUP, SEQ), jnp.float32),
        ],
        scratch_shapes=[pltpu.VMEM((QB, 2 * SEQ - QB), jnp.float32)],
        compiler_params=pltpu.CompilerParams(vmem_limit_bytes=40 << 20),
        name="attend_forward",
    )(slopes, qkv)


def fill_distance(dist_ref):
    row = lax.broadcasted_iota(jnp.int32, dist_ref.shape, 0)
    col = lax.broadcasted_iota(jnp.int32, dist_ref.shape, 1)
    dist_ref[...] = jnp.abs(row - col - (SEQ - QB)).astype(jnp.float32) * LOG2E


def attend_back_kernel(base, slope_ref, qkv_ref, lse_ref, dctx_ref, dqkv_ref, sums_ref, dist_ref, acc_ref, dqt_ref):
    width = GROUP * HEAD
    @pl.when(pl.program_id(0) == 0)
    def _():
        fill_distance(dist_ref)

    lane = lax.broadcasted_iota(jnp.int32, (1, 128), 1)
    for pair in range(GROUP // 2):
        cols = slice(128 * pair, 128 * pair + 128)
        keys = qkv_ref[:, width + 128 * pair : width + 128 * pair + 128]
        values = qkv_ref[:, 2 * width + 128 * pair : 2 * width + 128 * pair + 128]
        keys_t = keys.T
        for side in range(2):
            own = (lane < HEAD) if side == 0 else (lane >= HEAD)
            own_rows = slice(HEAD * side, HEAD * side + HEAD)
            slope = slope_ref[base + 2 * pair + side]
            for block in range(SEQ // QB):
                rows = slice(block * QB, (block + 1) * QB)
                q = qkv_ref[rows, 128 * pair : 128 * pair + 128]
                q = jnp.where(own, q, jnp.zeros_like(q))
                do = dctx_ref[rows, cols]
                do = jnp.where(own, do, jnp.zeros_like(do))
                s = mm(keys, q, NT) * SCALE
                start = SEQ - QB - block * QB
                s = s - slope * dist_ref[start : start + SEQ, :]
                p = jnp.exp2(s - lse_ref[2 * pair + side : 2 * pair + side + 1, rows])
                dp = mm(values, do, NT)
                inner = jnp.sum(p * dp, axis=0, keepdims=True)
                ds = (p * (dp - inner)).astype(jnp.bfloat16)
                p = p.astype(jnp.bfloat16)
                dv = mm(p, do)
                dk = mm(ds, q)
                if block == 0 and side == 0:
                    acc_ref[:, 0:128] = dk
                    acc_ref[:, 128:256] = dv
                else:
                    acc_ref[:, 0:128] += dk
                    acc_ref[:, 128:256] += dv
                dqt_ref[own_rows, rows] = mm(keys_t[own_rows], ds)
        dq = dqt_ref[...].T * (1.0 / math.sqrt(HEAD))
        dk = acc_ref[:, 0:128] * (1.0 / math.sqrt(HEAD))
        dv = acc_ref[:, 128:256]
        dqkv_ref[:, 128 * pair : 128 * pair + 128] = dq.astype(jnp.bfloat16)
        dqkv_ref[:, width + 128 * pair : width + 128 * pair + 128] = dk.astype(jnp.bfloat16)
        dqkv_ref[:, 2 * width + 128 * pair : 2 * width + 128 * pair + 128] = dv.astype(jnp.bfloat16)
        sums_ref[0:1, cols] = jnp.sum(dq, axis=0, keepdims=True)
        sums_ref[1:2, cols] = jnp.sum(dv, axis=0, keepdims=True)


def attend_backward(qkv, lse, dctx, slopes, group):
    width = GROUP * HEAD
    return pl.pallas_call(
        functools.partial(attend_back_kernel, group * GROUP),
        grid=(1,),
        in_specs=[
            pl.BlockSpec(memory_space=pltpu.SMEM),
            pl.BlockSpec((SEQ, 3 * width), lambda g: (0, group)),
            pl.BlockSpec((None, GROUP, SEQ), lambda g: (group, 0, 0)),
            pl.BlockSpec((SEQ, width), lambda g: (0, group)),
        ],
        out_specs=[
            pl.BlockSpec((SEQ, 3 * width), lambda g: (0, 0)),
            pl.BlockSpec((2, width), lambda g: (0, 0)),
        ],
        out_shape=[
            jax.ShapeDtypeStruct((SEQ, 3 * width), jnp.bfloat16),
            jax.ShapeDtypeStruct((2, width), jnp.float32),
        ],
        scratch_shapes=[
            pltpu.VMEM((2 * SEQ - QB, QB), jnp.float32),
            pltpu.VMEM((SEQ, 256), jnp.float32),
            pltpu.VMEM((128, SEQ), jnp.float32),
        ],
        compiler_params=pltpu.CompilerParams(vmem_limit_bytes=40 << 20),
        name="attend_backward",
    )(slopes, qkv, lse, dctx)


NORM_EPS = 1e-12
INV_ROOT_TWO = 0.7071067811865476
INV_ROOT_TWO_PI = 0.3989422804014327
FF_CHUNKS = 3


def norm_forward(resid, gain, shift):
    center = resid - jnp.mean(resid, axis=1, keepdims=True)
    inverse = lax.rsqrt(jnp.mean(center * center, axis=1, keepdims=True) + NORM_EPS)
    normed = center * inverse
    return (normed * gain + shift, normed, inverse)


def norm_backward(grad_rows, normed, inverse, gain):
    scaled = grad_rows * gain
    first_mean = jnp.mean(scaled, axis=1, keepdims=True)
    second_mean = jnp.mean(scaled * normed, axis=1, keepdims=True)
    d_resid = inverse * (scaled - first_mean - normed * second_mean)
    return (d_resid, jnp.sum(grad_rows * normed, axis=0), jnp.sum(grad_rows, axis=0))


def gelu_parts(gate_part):
    normal_cdf = 0.5 * (1.0 + lax.erf(gate_part * INV_ROOT_TWO))
    density = jnp.exp(-0.5 * gate_part * gate_part) * INV_ROOT_TWO_PI
    return (gate_part * normal_cdf, normal_cdf + gate_part * density)


class Links:
    def __init__(self, mesh_shape):
        self.dp = mesh_shape["dp"]
        self.tensor = mesh_shape["tensor"]
        self.paired = self.dp == 8 and self.tensor == 4

    def swap(self, value, axis, bit):
        size = self.dp if axis == "dp" else self.tensor
        return lax.ppermute(value, axis, [(i, i ^ bit) for i in range(size)])

    def tensor_order(self):
        places = jnp.arange(self.tensor, dtype=jnp.int32)
        return places ^ lax.axis_index("tensor") if self.paired else places

    def gather(self, piece, dp_bits):
        rows = piece.shape[0]
        if not self.paired:
            columns = lax.all_gather(piece, "tensor", axis=2)
            return lax.all_gather(columns, "dp", axis=0, tiled=True)
        second = self.swap(piece, "tensor", 2)
        pair = jnp.stack([piece, second])
        other = self.swap(pair, "tensor", 1)
        columns = jnp.stack([piece, other[0], second, other[1]], axis=2)
        held = {0: columns}
        for bit in dp_bits:
            for place in list(held):
                held[place | bit] = self.swap(held[place], "dp", bit)
        me = lax.axis_index("dp")
        whole = jnp.zeros((self.dp * rows,) + columns.shape[1:], piece.dtype)
        for place, value in held.items():
            whole = lax.dynamic_update_slice(whole, value, ((me ^ place) * rows, 0, 0, 0))
        return whole

    def scatter(self, grad, dp_bits):
        if not self.paired:
            mine = lax.psum_scatter(grad, "dp", scatter_dimension=0, tiled=True)
            return lax.psum_scatter(mine, "tensor", scatter_dimension=2, tiled=False).astype(jnp.float32)
        rows = grad.shape[0] // self.dp
        me = lax.axis_index("dp")
        held = {
            place: lax.dynamic_slice_in_dim(grad, (me ^ place) * rows, rows, 0)
            for place in range(self.dp)
        }
        for bit in dp_bits:
            for place in [p for p in held if p & bit]:
                arrived = self.swap(held.pop(place), "dp", bit)
                mine = held[place ^ bit].astype(jnp.float32) + arrived.astype(jnp.float32)
                held[place ^ bit] = mine.astype(jnp.bfloat16)
        mine = held[0]
        arrived = self.swap(mine[:, :, 1::2], "tensor", 1)
        mine = (mine[:, :, 0::2].astype(jnp.float32) + arrived.astype(jnp.float32)).astype(jnp.bfloat16)
        arrived = self.swap(mine[:, :, 1], "tensor", 2)
        return mine[:, :, 0].astype(jnp.float32) + arrived.astype(jnp.float32)

    def total(self, value):
        if not self.paired:
            return lax.psum(value, ("dp", "tensor"))
        for axis, bit in (("dp", 1), ("dp", 4), ("dp", 2), ("tensor", 1), ("tensor", 2)):
            value = value + self.swap(value, axis, bit)
        return value


def local(
    links,
    tokens,
    qkv_weight,
    qv_bias,
    out_weight,
    out_bias,
    norm1_gain,
    norm1_shift,
    in_weight,
    down_weight,
    down_bias,
    norm2_gain,
    norm2_shift,
    cotangent,
):
    width = tokens.shape[1]
    rows = qkv_weight.shape[0]
    n_tensor = links.tensor
    groups = qkv_weight.shape[2] // HEAD
    part = in_weight.shape[2] // FF_CHUNKS

    qkv_pieces = qkv_weight.reshape(rows, 3, groups, HEAD)
    qkv_full = [links.gather(qkv_pieces[:, :, g], (2, 4, 1)).reshape(width, -1) for g in range(groups)]
    qkv_full = jnp.concatenate(qkv_full, axis=1)
    out_full = links.gather(out_weight.reshape(rows, groups, HEAD), (4, 2, 1)).reshape(width, -1)
    in_full = []
    down_full = []
    for c in range(FF_CHUNKS):
        cols = slice(c * part, (c + 1) * part)
        piece = jnp.concatenate([in_weight[:, :, cols], down_weight[:, None, cols]], axis=1)
        full = links.gather(piece, (2, 4, 1) if c % 2 else (4, 2, 1))
        in_full.append(full[:, :2].reshape(width, -1))
        down_full.append(full[:, 2].reshape(width, -1))

    places = links.tensor_order()
    head_ids = (places[None, :] * groups + jnp.arange(groups, dtype=jnp.int32)[:, None]).reshape(-1)
    powers = jnp.where(
        head_ids < 8, -(head_ids + 1).astype(jnp.float32), 7.5 - head_ids.astype(jnp.float32)
    )
    slopes = jnp.exp2(powers)
    bias_cols = qv_bias.reshape(2, n_tensor, groups, HEAD)[:, places].transpose(0, 2, 1, 3)
    bias_cols = bias_cols.reshape(2, groups, n_tensor * HEAD)
    bias_row = jnp.stack([bias_cols[0], jnp.zeros_like(bias_cols[0]), bias_cols[1]], axis=1).reshape(-1)

    projected = jnp.dot(tokens, qkv_full, preferred_element_type=jnp.float32)
    qkv = (projected + bias_row).astype(jnp.bfloat16)
    context, lse = attend_forward(qkv, slopes)
    attention = jnp.einsum("rc,oc->ro", context, out_full, preferred_element_type=jnp.float32)
    resid1 = tokens.astype(jnp.float32) + attention + out_bias
    hidden1, normed1, inverse1 = norm_forward(resid1, norm1_gain, norm1_shift)
    hidden1_low = hidden1.astype(jnp.bfloat16)
    ffn_out = 0.0
    kept = []
    for c in range(FF_CHUNKS):
        gate_up = jnp.dot(hidden1_low, in_full[c], preferred_element_type=jnp.float32)
        gate_part = gate_up[:, : part * n_tensor]
        up_part = gate_up[:, part * n_tensor :]
        activated, slope_gelu = gelu_parts(gate_part)
        gated = (activated * up_part).astype(jnp.bfloat16)
        ffn_out = ffn_out + jnp.einsum(
            "rf,of->ro", gated, down_full[c], preferred_element_type=jnp.float32
        )
        kept.append((gated, (up_part * slope_gelu).astype(jnp.bfloat16), activated.astype(jnp.bfloat16)))
    resid2 = hidden1 + ffn_out + down_bias
    result, normed2, inverse2 = norm_forward(resid2, norm2_gain, norm2_shift)

    d_resid2, norm2_gain_grad, norm2_shift_grad = norm_backward(
        cotangent.astype(jnp.float32), normed2, inverse2, norm2_gain
    )
    down_bias_grad = jnp.sum(d_resid2, axis=0)
    d_ffn_low = d_resid2.astype(jnp.bfloat16)
    d_hidden1 = d_resid2
    in_grads = []
    down_grads = []
    for c in range(FF_CHUNKS):
        gated, slope_up, activated = kept[c]
        d_gated = jnp.dot(d_ffn_low, down_full[c], preferred_element_type=jnp.float32)
        d_gate_up = jnp.concatenate([d_gated * slope_up, d_gated * activated], axis=1)
        d_gate_up = d_gate_up.astype(jnp.bfloat16)
        down_grad = jnp.einsum("ro,rf->of", d_ffn_low, gated, preferred_element_type=jnp.float32)
        in_grad = jnp.einsum("rd,rc->dc", hidden1_low, d_gate_up, preferred_element_type=jnp.float32)
        d_hidden1 = d_hidden1 + jnp.einsum(
            "rc,dc->rd", d_gate_up, in_full[c], preferred_element_type=jnp.float32
        )
        grad = jnp.concatenate([in_grad, down_grad], axis=1).astype(jnp.bfloat16)
        mine = links.scatter(grad.reshape(width, 3, n_tensor, part), (1, 2, 4) if c % 2 else (1, 4, 2))
        in_grads.append(mine[:, :2])
        down_grads.append(mine[:, 2])
    d_resid1, norm1_gain_grad, norm1_shift_grad = norm_backward(
        d_hidden1, normed1, inverse1, norm1_gain
    )
    out_bias_grad = jnp.sum(d_resid1, axis=0)
    d_attn_low = d_resid1.astype(jnp.bfloat16)
    d_context = jnp.dot(d_attn_low, out_full, preferred_element_type=jnp.float32).astype(jnp.bfloat16)
    out_grad = jnp.einsum("ro,rc->oc", d_attn_low, context, preferred_element_type=jnp.float32)
    out_grad = links.scatter(
        out_grad.astype(jnp.bfloat16).reshape(width, groups, n_tensor, HEAD), (1, 2, 4)
    ).reshape(rows, -1)
    d_tokens = d_resid1
    qkv_grads = []
    bias_grads = []
    for g in range(groups):
        d_qkv, sums = attend_backward(qkv, lse, d_context, slopes, g)
        grad = jnp.einsum("rd,rc->dc", tokens, d_qkv, preferred_element_type=jnp.float32)
        grad = grad.astype(jnp.bfloat16).reshape(width, 3, n_tensor, HEAD)
        qkv_grads.append(links.scatter(grad, (1, 2, 4) if g % 2 else (1, 4, 2)))
        d_tokens = d_tokens + jnp.einsum(
            "rc,dc->rd",
            d_qkv,
            qkv_full[:, g * d_qkv.shape[1] : (g + 1) * d_qkv.shape[1]],
            preferred_element_type=jnp.float32,
        )
        bias_grads.append(sums.reshape(2, n_tensor, HEAD))
    tokens_grad = d_tokens.astype(jnp.bfloat16)
    qkv_grad = jnp.stack(qkv_grads, axis=2).reshape(rows, 3, -1)
    in_grad = jnp.concatenate(in_grads, axis=2)
    down_grad = jnp.concatenate(down_grads, axis=1)
    qv_grad = jnp.stack(bias_grads, axis=2)[:, places].reshape(2, width)
    sums = links.total(
        jnp.concatenate(
            [
                qv_grad,
                out_bias_grad[None],
                norm1_gain_grad[None],
                norm1_shift_grad[None],
                down_bias_grad[None],
                norm2_gain_grad[None],
                norm2_shift_grad[None],
            ]
        )
    )
    return (
        result.astype(jnp.bfloat16),
        tokens_grad,
        qkv_grad,
        sums[:2],
        out_grad,
        sums[2],
        sums[3],
        sums[4],
        in_grad,
        down_grad,
        sums[5],
        sums[6],
        sums[7],
    )


def solution(mesh):
    rows_all = P(("dp", "tensor"), None)
    return jax.shard_map(
        functools.partial(local, Links(mesh.shape)),
        mesh=mesh,
        in_specs=(
            rows_all,
            P("dp", None, "tensor"),
            P(),
            P("dp", "tensor"),
            P(),
            P(),
            P(),
            P("dp", None, "tensor"),
            P("dp", "tensor"),
            P(),
            P(),
            P(),
            rows_all,
        ),
        out_specs=(
            rows_all,
            rows_all,
            P("dp", None, "tensor"),
            P(),
            P("dp", "tensor"),
            P(),
            P(),
            P(),
            P("dp", None, "tensor"),
            P("dp", "tensor"),
            P(),
            P(),
            P(),
        ),
        check_vma=False,
    )
```

time: 1850 us -> 1100 us (0.59)
  waiting for transfers between devices: 1190 us -> 233 us
  local copies, waits for them, and re-layouts: 134 us -> 529 us
  matrix products: 346 us -> 118 us
  Pallas kernels: 0 us -> 77.9 us
  starting transfers between devices: 11.2 us -> 86.8 us
  blocking collectives: 70.6 us -> 0 us
  other arithmetic: 69.1 us -> 37.2 us
    reduce_scatter x7 -> x0, waiting for transfers between devices: 774 us -> none  [the longest x1 210 us: local(): lax.psum_scatter(d_group_hidden, 'tensor', scatter_dimension=0, tiled=True)]
    all_gather x6 -> x0, waiting for transfers between devices: 415 us -> none  [the longest x1 116 us: local(): group_d_ffn = lax.all_gather(d_ffn_low, 'tensor', axis=0, tiled=True)]
    dynamic_update_slice x13 -> x56, local copies, waits for them, and re-layouts: 16.9 us -> 360 us  [gather(): lax.dynamic_update_slice(whole, value, ((me ^ place) * rows, 0, 0, 0))]
    ppermute x0 -> x131, waiting for transfers between devices: none -> 233 us  [swap(): return lax.ppermute(value, axis, [(i, i ^ bit) for i in range(size)])]
    dot_general x95 -> x27, matrix products: 339 us -> 114 us  [the longest x3 20.4 us: local(): jnp.dot(d_ffn_low, down_full[c], preferred_element_type=jnp.float32)]
    ppermute x0 -> x131, starting transfers between devices: none -> 86.8 us  [swap(): return lax.ppermute(value, axis, [(i, i ^ bit) for i in range(size)])]
    pallas_call x0 -> x4, Pallas kernels: none -> 77.9 us  [the longest x3 44.5 us: attend_backward(): pl.pallas_call(functools.partial(attend_back_kernel, group * GROUP), grid...]
    psum x1 -> x0, blocking collectives: 47.4 us -> none  [local(): lax.psum((qv_grad, out_bias_grad, norm1_gain_grad, norm1_shift_grad, down...]
  transfers between devices with their start and end apart: 14 -> 131, of which waited for: 11 -> 52; matrix products, arithmetic and copies ran while one was open for 16% -> 49% of each run, Pallas kernels for 0% -> 3%
where the time goes in v1:
time: 1100 us; the launch traced here: 1080 us
  local copies, waits for them, and re-layouts  529 us (48%)
  waiting for transfers between devices  233 us (21%)
  matrix products  118 us (11%)
  starting transfers between devices  86.8 us (8%)
  Pallas kernels  77.9 us (7%)
  other arithmetic  37.2 us (3%)
    dynamic_update_slice x56, local copies, waits for them, and re-layouts, gather(): lax.dynamic_update_slice(whole, value, ((me ^ place) * rows, 0, 0, 0))  360 us
    ppermute x131, waiting for transfers between devices, swap(): return lax.ppermute(value, axis, [(i, i ^ bit) for i in range(size)])  233 us
    ppermute x131, starting transfers between devices, swap(): return lax.ppermute(value, axis, [(i, i ^ bit) for i in range(size)])  86.8 us
    unnamed x317, local copies, waits for them, and re-layouts  44.5 us
    pallas_call x3, Pallas kernels, attend_backward(): pl.pallas_call(functools.partial(attend_back_kernel, group * GROUP), grid...  44.5 us
    ppermute x21, local copies, waits for them, and re-layouts, swap(): return lax.ppermute(value, axis, [(i, i ^ bit) for i in range(size)])  35.3 us
    pallas_call x1, Pallas kernels, attend_forward(): pl.pallas_call(attend_kernel, grid=(groups,), in_specs=[pl.BlockSpec(memo...  33.4 us
    convert_element_type x3, local copies, waits for them, and re-layouts, local(): grad = jnp.concatenate([in_grad, down_grad], axis=1).astype(jnp.bfloat16)  29.5 us
  transfers between devices with their start and end apart: 131, of which 52 were waited for; matrix products, arithmetic and copies ran while one was open for 49% of the time, Pallas kernels for 3%

profile of v1, /device:TPU:0, one launch (start us, length us, event | category | flops | bytes accessed | tf_op | source)
XLA Modules:
  0.0 1084.3 jit_solution(7536447437291022450)
XLA Ops:
  19.0 10.5 collective-permute-done.18
  31.6 12.0 %collective-permute-done.28 = bf16[2,96,3,64]{1,3,2,0:T(8,128)(2,1)S(1)} collective-permute-done((bf16[2,96,3,64]{1,3,2,0:T(8,128)(2,1)S(1)}, bf16[2,96,3,64]{1,3,2,0:T(8,128)(2,1)S(1)}, u32[]{:S(2)}, u32[]{:S(2)}) %collective-permute-start.28) | collective-permute-done | bytes 73760 | tf_op jit(solution)/shard_map/ppermute | solution.py:210
  96.8 6.5 collective-permute-done.37
  194.4 4.8 dynamic_update_slice.173
  237.0 4.9 dynamic_update_slice.198
  249.9 8.4 dynamic_update_slice.200
  260.9 8.0 dynamic_update_slice.216
  271.4 8.0 dynamic_update_slice.208
  298.9 6.3 fusion.qkv_ref
  305.3 33.4 %attend_forward.1 = (bf16[1024,768]{1,0:T(8,128)(2,1)S(1)}, f32[3,4,1024]{2,1,0:T(4,128)S(1)}) custom-call(f32[12]{0:T(128)S(1)} %reshape.214.slope_ref, bf16[1024,2304]{1,0:T(8,128)(2,1)S(1)} %fusion.qkv_ref), custom_call_target="tpu_custom_call" | custom-call | tf_op jit(solution)/shard_map/attend_forward/pallas_call | solution.py:70
  353.1 8.7 collective-permute-done.58
  364.2 10.1 collective-permute-done.40
  377.9 8.0 dynamic_update_slice.201
  387.4 9.5 dynamic_update_slice.202
  398.4 8.0 dynamic_update_slice.217
  408.0 9.5 dynamic_update_slice.218
  419.0 9.5 dynamic_update_slice.209
  430.0 8.0 dynamic_update_slice.210
  445.6 9.9 dynamic_update_slice.203
  455.5 10.0 dynamic_update_slice.204
  467.7 9.9 dynamic_update_slice.205
  479.8 9.9 dynamic_update_slice.206
  492.0 9.9 dynamic_update_slice.219
  501.9 9.7 dynamic_update_slice.220
  513.1 9.6 dynamic_update_slice.221
  524.2 9.5 dynamic_update_slice.222
  535.2 9.5 dynamic_update_slice.211
  544.7 9.5 dynamic_update_slice.212
  555.7 9.5 dynamic_update_slice.213
  566.8 9.5 dynamic_update_slice.214
  577.8 8.8 dynamic_update_slice.207
  594.5 8.8 dynamic_update_slice.223
  611.4 8.8 dynamic_update_slice.215
  652.1 4.8 fusion.63
  661.5 6.8 multiply_convert_fusion.1
  668.3 8.1 multiply_convert_fusion.5
  676.4 5.4 multiply_convert_fusion.3
  690.0 5.3 fusion.34
  695.3 5.4 convolution_convert_fusion.2
  700.8 5.2 fusion.33
  706.0 5.0 convolution_convert_fusion.1
  711.1 5.0 convolution_convert_fusion
  716.1 8.7 multiply_reduce_fusion
  730.5 14.8 %attend_backward.5 = (bf16[1024,768]{1,0:T(8,128)(2,1)S(1)}, f32[2,256]{1,0:T(2,128)S(1)}) custom-call(f32[12]{0:T(128)S(1)} %copy-done.2, bf16[1024,2304]{1,0:T(8,128)(2,1)S(1)} %bitcast.245, f32[3,4,1024]{2,1,0:T(4,128)S(1)} %get-tuple-element.22.lse_ref, bf16[1024,768]{1,0:T(8,128)(2,1)S(1)} %convolution_convert_fusion.6.dctx_ref), custom_call_target="tpu_custom_call" | custom-call | tf_op jit(solution)/shard_map/attend_backward/pallas_call | solution.py:148
  745.3 15.0 %attend_backward.4 = (bf16[1024,768]{1,0:T(8,128)(2,1)S(1)}, f32[2,256]{1,0:T(2,128)S(1)}) custom-call(f32[12]{0:T(128)S(1)} %copy-done.2, bf16[1024,2304]{1,0:T(8,128)(2,1)S(1)} %bitcast.245, f32[3,4,1024]{2,1,0:T(4,128)S(1)} %get-tuple-element.22.lse_ref, bf16[1024,768]{1,0:T(8,128)(2,1)S(1)} %convolution_convert_fusion.6.dctx_ref), custom_call_target="tpu_custom_call" | custom-call | tf_op jit(solution)/shard_map/attend_backward/pallas_call | solution.py:148
  760.3 14.8 %attend_backward.3 = (bf16[1024,768]{1,0:T(8,128)(2,1)S(1)}, f32[2,256]{1,0:T(2,128)S(1)}) custom-call(f32[12]{0:T(128)S(1)} %copy-done.2, bf16[1024,2304]{1,0:T(8,128)(2,1)S(1)} %bitcast.245, f32[3,4,1024]{2,1,0:T(4,128)S(1)} %get-tuple-element.22.lse_ref, bf16[1024,768]{1,0:T(8,128)(2,1)S(1)} %convolution_convert_fusion.6.dctx_ref), custom_call_target="tpu_custom_call" | custom-call | tf_op jit(solution)/shard_map/attend_backward/pallas_call | solution.py:148
  783.3 10.0 convert_element_type.830
  793.4 5.3 constant_dynamic-slice_fusion.23
  823.5 9.6 convert_element_type.858
  833.2 9.8 convert_element_type.886
  851.9 7.3 constant_dynamic-slice_fusion.7
  894.2 6.4 collective-permute-done.86
  907.6 5.0 collective-permute-done.68
  947.8 5.1 collective-permute-done.88
  967.9 5.3 collective-permute-done.89
  973.2 5.1 collective-permute-done.103
  978.4 5.0 collective-permute-done.71
  995.5 11.4 %collective-permute-done.109 = bf16[96,3,4,256]{3,0,1,2:T(8,128)(2,1)S(1)} collective-permute-done((bf16[96,3,4,256]{3,0,1,2:T(8,128)(2,1)S(1)}, bf16[96,3,4,256]{3,0,1,2:T(8,128)(2,1)S(1)}, u32[]{:S(2)}, u32[]{:S(2)}) %collective-permute-start.109) | collective-permute-done | bytes 589856 | tf_op jit(solution)/shard_map/ppermute | solution.py:210
  1013.0 10.2 collective-permute-done.127
  1023.9 11.9 %collective-permute-done.106 = bf16[96,3,4,256]{3,0,1,2:T(8,128)(2,1)S(1)} collective-permute-done((bf16[96,3,4,256]{3,0,1,2:T(8,128)(2,1)S(1)}, bf16[96,3,4,256]{3,0,1,2:T(8,128)(2,1)S(1)}, u32[]{:S(2)}, u32[]{:S(2)}) %collective-permute-start.106) | collective-permute-done | bytes 589856 | tf_op jit(solution)/shard_map/ppermute | solution.py:210
  1039.5 8.9 collective-permute-done.119
  1048.9 10.8 collective-permute-done.124
  1063.4 9.4 collective-permute-done.129
  1073.1 6.7 collective-permute-done.121
  (799 shorter events, 515.8 us)
Async XLA Ops:
  1.6 14.3 %collective-permute-start.27 = (bf16[96,3,64]{0,2,1:T(8,128)(2,1)S(1)}, bf16[96,3,64]{0,2,1:T(8,128)(2,1)S(1)}, u32[]{:S(2)}, u32[]{:S(2)}) collective-permute-start(bf16[96,3,64]{0,2,1:T(8,128)(2,1)S(1)} %bitcast.278), channel_id=1, source_target_pairs={{0,2},{1,3},{2,0},{3,1},{4,6},{5,7},{6,4},{7,5},{8,10},{9,11},{10,... | collective-permute-start | bytes 110600 | tf_op jit(solution)/shard_map/ppermute | solution.py:210
  6.9 22.6 %collective-permute-start.9 = (bf16[96,3,64]{0,2,1:T(8,128)(2,1)S(1)}, bf16[96,3,64]{0,2,1:T(8,128)(2,1)S(1)}, u32[]{:S(2)}, u32[]{:S(2)}) collective-permute-start(bf16[96,3,64]{0,2,1:T(8,128)(2,1)S(1)} %get-tuple-element.174), channel_id=1, source_target_pairs={{0,2},{1,3},{2,0},{3,1},{4,6},{5,7},{6,4},{7,5},{8,10},{9,11},{10,... | collective-permute-start | bytes 110600 | tf_op jit(solution)/shard_map/ppermute | solution.py:210
  9.8 19.7 %collective-permute-start.18 = (bf16[96,3,64]{0,2,1:T(8,128)(2,1)S(1)}, bf16[96,3,64]{0,2,1:T(8,128)(2,1)S(1)}, u32[]{:S(2)}, u32[]{:S(2)}) collective-permute-start(bf16[96,3,64]{0,2,1:T(8,128)(2,1)S(1)} %get-tuple-element.176), channel_id=1, source_target_pairs={{0,2},{1,3},{2,0},{3,1},{4,6},{5,7},{6,4},{7,5},{8,10},{9,11},{10,... | collective-permute-start | bytes 110600 | tf_op jit(solution)/shard_map/ppermute | solution.py:210
  12.3 42.3 %collective-permute-start.36 = (bf16[96,3,256]{0,2,1:T(8,128)(2,1)S(1)}, bf16[96,3,256]{0,2,1:T(8,128)(2,1)S(1)}, u32[]{:S(2)}, u32[]{:S(2)}) collective-permute-start(bf16[96,3,256]{0,2,1:T(8,128)(2,1)S(1)} %get-tuple-element.166), channel_id=1, source_target_pairs={{0,2},{1,3},{2,0},{3,1},{4,6},{5,7},{6,4},{7,5},{8,10},{9,11},{10,... | collective-permute-start | bytes 442376 | tf_op jit(solution)/shard_map/ppermute | solution.py:210
  15.9 40.3 %collective-permute-start.45 = (bf16[96,3,256]{0,2,1:T(8,128)(2,1)S(1)}, bf16[96,3,256]{0,2,1:T(8,128)(2,1)S(1)}, u32[]{:S(2)}, u32[]{:S(2)}) collective-permute-start(bf16[96,3,256]{0,2,1:T(8,128)(2,1)S(1)} %get-tuple-element.163), channel_id=1, source_target_pairs={{0,2},{1,3},{2,0},{3,1},{4,6},{5,7},{6,4},{7,5},{8,10},{9,11},{10,... | collective-permute-start | bytes 442376 | tf_op jit(solution)/shard_map/ppermute | solution.py:210
  16.1 40.2 %collective-permute-start.54 = (bf16[96,3,256]{0,2,1:T(8,128)(2,1)S(1)}, bf16[96,3,256]{0,2,1:T(8,128)(2,1)S(1)}, u32[]{:S(2)}, u32[]{:S(2)}) collective-permute-start(bf16[96,3,256]{0,2,1:T(8,128)(2,1)S(1)} %get-tuple-element.160), channel_id=1, source_target_pairs={{0,2},{1,3},{2,0},{3,1},{4,6},{5,7},{6,4},{7,5},{8,10},{9,11},{10,... | collective-permute-start | bytes 442376 | tf_op jit(solution)/shard_map/ppermute | solution.py:210
  29.5 14.2 %collective-permute-start.28 = (bf16[2,96,3,64]{1,3,2,0:T(8,128)(2,1)S(1)}, bf16[2,96,3,64]{1,3,2,0:T(8,128)(2,1)S(1)}, u32[]{:S(2)}, u32[]{:S(2)}) collective-permute-start(bf16[2,96,3,64]{1,3,2,0:T(8,128)(2,1)S(1)} %pad_maximum_fusion.33), channel_id=1, source_target_pairs={{0,1},{1,0},{2,3},{3,2},{4,5},{5,4},{6,7},{7,6},{8,9},{9,8},{10,11... | collective-permute-start | bytes 221192 | tf_op jit(solution)/shard_map/ppermute | solution.py:210
  29.5 23.5 %collective-permute-start.19 = (bf16[2,96,3,64]{1,3,2,0:T(8,128)(2,1)S(1)}, bf16[2,96,3,64]{1,3,2,0:T(8,128)(2,1)S(1)}, u32[]{:S(2)}, u32[]{:S(2)}) collective-permute-start(bf16[2,96,3,64]{1,3,2,0:T(8,128)(2,1)S(1)} %pad_maximum_fusion.32), channel_id=1, source_target_pairs={{0,1},{1,0},{2,3},{3,2},{4,5},{5,4},{6,7},{7,6},{8,9},{9,8},{10,11... | collective-permute-start | bytes 221192 | tf_op jit(solution)/shard_map/ppermute | solution.py:210
  71.1 11.8 %collective-permute-start.55 = (bf16[2,96,3,256]{1,3,2,0:T(8,128)(2,1)S(1)}, bf16[2,96,3,256]{1,3,2,0:T(8,128)(2,1)S(1)}, u32[]{:S(2)}, u32[]{:S(2)}) collective-permute-start(bf16[2,96,3,256]{1,3,2,0:T(8,128)(2,1)S(1)} %pad_maximum_fusion.20), channel_id=1, source_target_pairs={{0,1},{1,0},{2,3},{3,2},{4,5},{5,4},{6,7},{7,6},{8,9},{9,8},{10,11... | collective-permute-start | bytes 884744 | tf_op jit(solution)/shard_map/ppermute | solution.py:210
  84.4 12.4 %collective-permute-start.46 = (bf16[2,96,3,256]{1,3,2,0:T(8,128)(2,1)}, bf16[2,96,3,256]{1,3,2,0:T(8,128)(2,1)}, u32[]{:S(2)}, u32[]{:S(2)}) collective-permute-start(bf16[2,96,3,256]{1,3,2,0:T(8,128)(2,1)} %pad_maximum_fusion.19), channel_id=1, source_target_pairs={{0,1},{1,0},{2,3},{3,2},{4,5},{5,4},{6,7},{7,6},{8,9},{9,8},{10,11... | collective-permute-start | bytes 884744 | tf_op jit(solution)/shard_map/ppermute | solution.py:210
  84.7 18.6 %collective-permute-start.37 = (bf16[2,96,3,256]{1,3,2,0:T(8,128)(2,1)}, bf16[2,96,3,256]{1,3,2,0:T(8,128)(2,1)}, u32[]{:S(2)}, u32[]{:S(2)}) collective-permute-start(bf16[2,96,3,256]{1,3,2,0:T(8,128)(2,1)} %pad_maximum_fusion.18), channel_id=1, source_target_pairs={{0,1},{1,0},{2,3},{3,2},{4,5},{5,4},{6,7},{7,6},{8,9},{9,8},{10,11... | collective-permute-start | bytes 884744 | tf_op jit(solution)/shard_map/ppermute | solution.py:210
  90.3 18.8 %collective-permute-start.59 = (bf16[96,3,4,256]{3,0,2,1:T(8,128)(2,1)}, bf16[96,3,4,256]{3,0,2,1:T(8,128)(2,1)S(1)}, u32[]{:S(2)}, u32[]{:S(2)}) collective-permute-start(bf16[96,3,4,256]{3,0,2,1:T(8,128)(2,1)} %copy.286), channel_id=1, source_target_pairs={{0,4},{4,0},{8,12},{12,8},{16,20},{20,16},{24,28},{28,24},{1,5},{5... | collective-permute-start | bytes 1769480 | tf_op jit(solution)/shard_map/ppermute | solution.py:210
  90.6 15.1 %collective-permute-start.35 = (bf16[96,3,4,64]{0,3,2,1:T(8,128)(2,1)}, bf16[96,3,4,64]{0,3,2,1:T(8,128)(2,1)S(1)}, u32[]{:S(2)}, u32[]{:S(2)}) collective-permute-start(bf16[96,3,4,64]{0,3,2,1:T(8,128)(2,1)} %copy-done.109), channel_id=1, source_target_pairs={{0,4},{4,0},{8,12},{12,8},{16,20},{20,16},{24,28},{28,24},{1,5},{5... | collective-permute-start | bytes 442376 | tf_op jit(solution)/shard_map/ppermute | solution.py:210
  95.6 11.4 %collective-permute-start.8 = (bf16[96,3,4,64]{0,3,2,1:T(8,128)(2,1)}, bf16[96,3,4,64]{0,3,2,1:T(8,128)(2,1)}, u32[]{:S(2)}, u32[]{:S(2)}) collective-permute-start(bf16[96,3,4,64]{0,3,2,1:T(8,128)(2,1)} %copy-done.116), channel_id=1, source_target_pairs={{0,4},{4,0},{8,12},{12,8},{16,20},{20,16},{24,28},{28,24},{1,5},{5... | collective-permute-start | bytes 442376 | tf_op jit(solution)/shard_map/ppermute | solution.py:210
  96.8 11.7 %collective-permute-start.17 = (bf16[96,3,4,64]{0,3,2,1:T(8,128)(2,1)}, bf16[96,3,4,64]{0,3,2,1:T(8,128)(2,1)}, u32[]{:S(2)}, u32[]{:S(2)}) collective-permute-start(bf16[96,3,4,64]{0,3,2,1:T(8,128)(2,1)} %collective-permute-done.13), channel_id=1, source_target_pairs={{0,4},{4,0},{8,12},{12,8},{16,20},{20,16},{24,28},{28,24},{1,5},{5... | collective-permute-start | bytes 442376 | tf_op jit(solution)/shard_map/ppermute | solution.py:210
  105.7 185.9 %collective-permute-start.57 = (bf16[96,3,4,256]{3,0,2,1:T(8,128)(2,1)}, bf16[96,3,4,256]{3,0,2,1:T(8,128)(2,1)}, u32[]{:S(2)}, u32[]{:S(2)}) collective-permute-start(bf16[96,3,4,256]{3,0,2,1:T(8,128)(2,1)} %copy.286), channel_id=1, source_target_pairs={{0,8},{4,12},{8,0},{12,4},{16,24},{20,28},{24,16},{28,20},{1,9},{5... | collective-permute-start | bytes 1769480 | tf_op jit(solution)/shard_map/ppermute | solution.py:210
  107.0 188.7 %collective-permute-start.56 = (bf16[96,3,4,256]{3,0,2,1:T(8,128)(2,1)}, bf16[96,3,4,256]{3,0,2,1:T(8,128)(2,1)}, u32[]{:S(2)}, u32[]{:S(2)}) collective-permute-start(bf16[96,3,4,256]{3,0,2,1:T(8,128)(2,1)} %copy.286), channel_id=1, source_target_pairs={{0,16},{4,20},{8,24},{12,28},{16,0},{20,4},{24,8},{28,12},{1,17},{... | collective-permute-start | bytes 1769480 | tf_op jit(solution)/shard_map/ppermute | solution.py:210
  108.5 189.3 %collective-permute-start.50 = (bf16[96,3,4,256]{3,0,2,1:T(8,128)(2,1)}, bf16[96,3,4,256]{3,0,2,1:T(8,128)(2,1)}, u32[]{:S(2)}, u32[]{:S(2)}) collective-permute-start(bf16[96,3,4,256]{3,0,2,1:T(8,128)(2,1)} %copy.269), channel_id=1, source_target_pairs={{0,4},{4,0},{8,12},{12,8},{16,20},{20,16},{24,28},{28,24},{1,5},{5... | collective-permute-start | bytes 1769480 | tf_op jit(solution)/shard_map/ppermute | solution.py:210
  108.5 189.9 %collective-permute-start.48 = (bf16[96,3,4,256]{3,0,2,1:T(8,128)(2,1)}, bf16[96,3,4,256]{3,0,2,1:T(8,128)(2,1)}, u32[]{:S(2)}, u32[]{:S(2)}) collective-permute-start(bf16[96,3,4,256]{3,0,2,1:T(8,128)(2,1)} %copy.269), channel_id=1, source_target_pairs={{0,16},{4,20},{8,24},{12,28},{16,0},{20,4},{24,8},{28,12},{1,17},{... | collective-permute-start | bytes 1769480 | tf_op jit(solution)/shard_map/ppermute | solution.py:210
  109.1 189.3 %collective-permute-start.47 = (bf16[96,3,4,256]{3,0,2,1:T(8,128)(2,1)}, bf16[96,3,4,256]{3,0,2,1:T(8,128)(2,1)}, u32[]{:S(2)}, u32[]{:S(2)}) collective-permute-start(bf16[96,3,4,256]{3,0,2,1:T(8,128)(2,1)} %copy.269), channel_id=1, source_target_pairs={{0,8},{4,12},{8,0},{12,4},{16,24},{20,28},{24,16},{28,20},{1,9},{5... | collective-permute-start | bytes 1769480 | tf_op jit(solution)/shard_map/ppermute | solution.py:210
  291.6 53.6 %collective-permute-start.41 = (bf16[96,3,4,256]{3,0,2,1:T(8,128)(2,1)}, bf16[96,3,4,256]{3,0,2,1:T(8,128)(2,1)}, u32[]{:S(2)}, u32[]{:S(2)}) collective-permute-start(bf16[96,3,4,256]{3,0,2,1:T(8,128)(2,1)} %copy.254), channel_id=1, source_target_pairs={{0,4},{4,0},{8,12},{12,8},{16,20},{20,16},{24,28},{28,24},{1,5},{5... | collective-permute-start | bytes 1769480 | tf_op jit(solution)/shard_map/ppermute | solution.py:210
  295.7 51.1 %collective-permute-start.39 = (bf16[96,3,4,256]{3,0,2,1:T(8,128)(2,1)}, bf16[96,3,4,256]{3,0,2,1:T(8,128)(2,1)}, u32[]{:S(2)}, u32[]{:S(2)}) collective-permute-start(bf16[96,3,4,256]{3,0,2,1:T(8,128)(2,1)} %copy.254), channel_id=1, source_target_pairs={{0,8},{4,12},{8,0},{12,4},{16,24},{20,28},{24,16},{28,20},{1,9},{5... | collective-permute-start | bytes 1769480 | tf_op jit(solution)/shard_map/ppermute | solution.py:210
  297.8 49.0 %collective-permute-start.38 = (bf16[96,3,4,256]{3,0,2,1:T(8,128)(2,1)}, bf16[96,3,4,256]{3,0,2,1:T(8,128)(2,1)}, u32[]{:S(2)}, u32[]{:S(2)}) collective-permute-start(bf16[96,3,4,256]{3,0,2,1:T(8,128)(2,1)} %copy.254), channel_id=1, source_target_pairs={{0,16},{4,20},{8,24},{12,28},{16,0},{20,4},{24,8},{28,12},{1,17},{... | collective-permute-start | bytes 1769480 | tf_op jit(solution)/shard_map/ppermute | solution.py:210
  298.4 49.4 %collective-permute-start.61 = (bf16[96,3,4,256]{3,0,2,1:T(8,128)(2,1)}, bf16[96,3,4,256]{3,0,2,1:T(8,128)(2,1)}, u32[]{:S(2)}, u32[]{:S(2)}) collective-permute-start(bf16[96,3,4,256]{3,0,2,1:T(8,128)(2,1)} %collective-permute-done.57), channel_id=1, source_target_pairs={{0,4},{4,0},{8,12},{12,8},{16,20},{20,16},{24,28},{28,24},{1,5},{5... | collective-permute-start | bytes 1769480 | tf_op jit(solution)/shard_map/ppermute | solution.py:210
  298.4 51.2 %collective-permute-start.60 = (bf16[96,3,4,256]{3,0,2,1:T(8,128)(2,1)}, bf16[96,3,4,256]{3,0,2,1:T(8,128)(2,1)}, u32[]{:S(2)}, u32[]{:S(2)}) collective-permute-start(bf16[96,3,4,256]{3,0,2,1:T(8,128)(2,1)} %collective-permute-done.56), channel_id=1, source_target_pairs={{0,4},{4,0},{8,12},{12,8},{16,20},{20,16},{24,28},{28,24},{1,5},{5... | collective-permute-start | bytes 1769480 | tf_op jit(solution)/shard_map/ppermute | solution.py:210
  345.2 16.6 %collective-permute-start.58 = (bf16[96,3,4,256]{3,0,2,1:T(8,128)(2,1)}, bf16[96,3,4,256]{3,0,2,1:T(8,128)(2,1)}, u32[]{:S(2)}, u32[]{:S(2)}) collective-permute-start(bf16[96,3,4,256]{3,0,2,1:T(8,128)(2,1)} %collective-permute-done.56), channel_id=1, source_target_pairs={{0,8},{4,12},{8,0},{12,4},{16,24},{20,28},{24,16},{28,20},{1,9},{5... | collective-permute-start | bytes 1769480 | tf_op jit(solution)/shard_map/ppermute | solution.py:210
  346.8 17.3 %collective-permute-start.42 = (bf16[96,3,4,256]{3,0,2,1:T(8,128)(2,1)}, bf16[96,3,4,256]{3,0,2,1:T(8,128)(2,1)S(1)}, u32[]{:S(2)}, u32[]{:S(2)}) collective-permute-start(bf16[96,3,4,256]{3,0,2,1:T(8,128)(2,1)} %collective-permute-done.38), channel_id=1, source_target_pairs={{0,4},{4,0},{8,12},{12,8},{16,20},{20,16},{24,28},{28,24},{1,5},{5... | collective-permute-start | bytes 1769480 | tf_op jit(solution)/shard_map/ppermute | solution.py:210
  346.8 27.4 %collective-permute-start.40 = (bf16[96,3,4,256]{3,0,2,1:T(8,128)(2,1)}, bf16[96,3,4,256]{3,0,2,1:T(8,128)(2,1)}, u32[]{:S(2)}, u32[]{:S(2)}) collective-permute-start(bf16[96,3,4,256]{3,0,2,1:T(8,128)(2,1)} %collective-permute-done.38), channel_id=1, source_target_pairs={{0,8},{4,12},{8,0},{12,4},{16,24},{20,28},{24,16},{28,20},{1,9},{5... | collective-permute-start | bytes 1769480 | tf_op jit(solution)/shard_map/ppermute | solution.py:210
  347.8 15.7 %collective-permute-start.49 = (bf16[96,3,4,256]{3,0,2,1:T(8,128)(2,1)}, bf16[96,3,4,256]{3,0,2,1:T(8,128)(2,1)}, u32[]{:S(2)}, u32[]{:S(2)}) collective-permute-start(bf16[96,3,4,256]{3,0,2,1:T(8,128)(2,1)} %collective-permute-done.47), channel_id=1, source_target_pairs={{0,16},{4,20},{8,24},{12,28},{16,0},{20,4},{24,8},{28,12},{1,17},{... | collective-permute-start | bytes 1769480 | tf_op jit(solution)/shard_map/ppermute | solution.py:210
  349.6 14.0 %collective-permute-start.43 = (bf16[96,3,4,256]{3,0,2,1:T(8,128)(2,1)}, bf16[96,3,4,256]{3,0,2,1:T(8,128)(2,1)S(1)}, u32[]{:S(2)}, u32[]{:S(2)}) collective-permute-start(bf16[96,3,4,256]{3,0,2,1:T(8,128)(2,1)} %collective-permute-done.39), channel_id=1, source_target_pairs={{0,4},{4,0},{8,12},{12,8},{16,20},{20,16},{24,28},{28,24},{1,5},{5... | collective-permute-start | bytes 1769480 | tf_op jit(solution)/shard_map/ppermute | solution.py:210
  361.8 192.4 %collective-permute-start.51 = (bf16[96,3,4,256]{3,0,2,1:T(8,128)(2,1)}, bf16[96,3,4,256]{3,0,2,1:T(8,128)(2,1)}, u32[]{:S(2)}, u32[]{:S(2)}) collective-permute-start(bf16[96,3,4,256]{3,0,2,1:T(8,128)(2,1)} %collective-permute-done.47), channel_id=1, source_target_pairs={{0,4},{4,0},{8,12},{12,8},{16,20},{20,16},{24,28},{28,24},{1,5},{5... | collective-permute-start | bytes 1769480 | tf_op jit(solution)/shard_map/ppermute | solution.py:210
  363.6 201.7 %collective-permute-start.52 = (bf16[96,3,4,256]{3,0,2,1:T(8,128)(2,1)}, bf16[96,3,4,256]{3,0,2,1:T(8,128)(2,1)}, u32[]{:S(2)}, u32[]{:S(2)}) collective-permute-start(bf16[96,3,4,256]{3,0,2,1:T(8,128)(2,1)} %collective-permute-done.48), channel_id=1, source_target_pairs={{0,4},{4,0},{8,12},{12,8},{16,20},{20,16},{24,28},{28,24},{1,5},{5... | collective-permute-start | bytes 1769480 | tf_op jit(solution)/shard_map/ppermute | solution.py:210
  363.6 229.5 %collective-permute-start.62 = (bf16[96,3,4,256]{3,0,2,1:T(8,128)(2,1)}, bf16[96,3,4,256]{3,0,2,1:T(8,128)(2,1)}, u32[]{:S(2)}, u32[]{:S(2)}) collective-permute-start(bf16[96,3,4,256]{3,0,2,1:T(8,128)(2,1)} %collective-permute-done.58), channel_id=1, source_target_pairs={{0,4},{4,0},{8,12},{12,8},{16,20},{20,16},{24,28},{28,24},{1,5},{5... | collective-permute-start | bytes 1769480 | tf_op jit(solution)/shard_map/ppermute | solution.py:210
  364.1 245.8 %collective-permute-start.53 = (bf16[96,3,4,256]{3,0,2,1:T(8,128)(2,1)}, bf16[96,3,4,256]{3,0,2,1:T(8,128)(2,1)}, u32[]{:S(2)}, u32[]{:S(2)}) collective-permute-start(bf16[96,3,4,256]{3,0,2,1:T(8,128)(2,1)} %collective-permute-done.49), channel_id=1, source_target_pairs={{0,4},{4,0},{8,12},{12,8},{16,20},{20,16},{24,28},{28,24},{1,5},{5... | collective-permute-start | bytes 1769480 | tf_op jit(solution)/shard_map/ppermute | solution.py:210
  374.3 202.0 %collective-permute-start.44 = (bf16[96,3,4,256]{3,0,2,1:T(8,128)(2,1)}, bf16[96,3,4,256]{3,0,2,1:T(8,128)(2,1)}, u32[]{:S(2)}, u32[]{:S(2)}) collective-permute-start(bf16[96,3,4,256]{3,0,2,1:T(8,128)(2,1)} %collective-permute-done.40), channel_id=1, source_target_pairs={{0,4},{4,0},{8,12},{12,8},{16,20},{20,16},{24,28},{28,24},{1,5},{5... | collective-permute-start | bytes 1769480 | tf_op jit(solution)/shard_map/ppermute | solution.py:210
  799.7 193.0 %collective-permute-start.104 = (bf16[96,3,4,256]{3,0,1,2:T(8,128)(2,1)}, bf16[96,3,4,256]{3,0,1,2:T(8,128)(2,1)}, u32[]{:S(2)}, u32[]{:S(2)}) collective-permute-start(bf16[96,3,4,256]{3,0,1,2:T(8,128)(2,1)} %copy.427), channel_id=1, source_target_pairs={{0,4},{4,0},{8,12},{12,8},{16,20},{20,16},{24,28},{28,24},{1,5},{5... | collective-permute-start | bytes 1769480 | tf_op jit(solution)/shard_map/ppermute | solution.py:210
  804.7 14.5 %collective-permute-start.90 = (f32[8,768]{1,0:T(8,128)S(1)}, f32[8,768]{1,0:T(8,128)S(1)}, u32[]{:S(2)}, u32[]{:S(2)}) collective-permute-start(f32[8,768]{1,0:T(8,128)S(1)} %concatenate.52), channel_id=1, source_target_pairs={{0,4},{4,0},{8,12},{12,8},{16,20},{20,16},{24,28},{28,24},{1,5},{5... | collective-permute-start | bytes 73736 | tf_op jit(solution)/shard_map/ppermute | solution.py:210
  819.2 32.7 %collective-permute-start.91 = (f32[8,768]{1,0:T(8,128)S(1)}, f32[8,768]{1,0:T(8,128)S(1)}, u32[]{:S(2)}, u32[]{:S(2)}) collective-permute-start(f32[8,768]{1,0:T(8,128)S(1)} %add.538), channel_id=1, source_target_pairs={{0,16},{4,20},{8,24},{12,28},{16,0},{20,4},{24,8},{28,12},{1,17},{... | collective-permute-start | bytes 73736 | tf_op jit(solution)/shard_map/ppermute | solution.py:210
  844.9 144.4 %collective-permute-start.108 = (bf16[96,3,4,256]{3,0,1,2:T(8,128)(2,1)}, bf16[96,3,4,256]{3,0,1,2:T(8,128)(2,1)}, u32[]{:S(2)}, u32[]{:S(2)}) collective-permute-start(bf16[96,3,4,256]{3,0,1,2:T(8,128)(2,1)} %copy.433), channel_id=1, source_target_pairs={{0,4},{4,0},{8,12},{12,8},{16,20},{20,16},{24,28},{28,24},{1,5},{5... | collective-permute-start | bytes 1769480 | tf_op jit(solution)/shard_map/ppermute | solution.py:210
  851.3 32.0 %collective-permute-start.82 = (bf16[96,3,4,64]{0,3,1,2:T(8,128)(2,1)}, bf16[96,3,4,64]{0,3,1,2:T(8,128)(2,1)}, u32[]{:S(2)}, u32[]{:S(2)}) collective-permute-start(bf16[96,3,4,64]{0,3,1,2:T(8,128)(2,1)} %copy.413), channel_id=1, source_target_pairs={{0,4},{4,0},{8,12},{12,8},{16,20},{20,16},{24,28},{28,24},{1,5},{5... | collective-permute-start | bytes 442376 | tf_op jit(solution)/shard_map/ppermute | solution.py:210
  859.3 15.9 %collective-permute-start.93 = (f32[8,768]{1,0:T(8,128)S(1)}, f32[8,768]{1,0:T(8,128)S(1)}, u32[]{:S(2)}, u32[]{:S(2)}) collective-permute-start(f32[8,768]{1,0:T(8,128)S(1)} %add.540), channel_id=1, source_target_pairs={{0,1},{1,0},{2,3},{3,2},{4,5},{5,4},{6,7},{7,6},{8,9},{9,8},{10,11... | collective-permute-start | bytes 73736 | tf_op jit(solution)/shard_map/ppermute | solution.py:210
  875.2 18.8 %collective-permute-start.84 = (bf16[96,3,4,64]{0,3,1,2:T(8,128)(2,1)}, bf16[96,3,4,64]{0,3,1,2:T(8,128)(2,1)}, u32[]{:S(2)}, u32[]{:S(2)}) collective-permute-start(bf16[96,3,4,64]{0,3,1,2:T(8,128)(2,1)} %copy.415), channel_id=1, source_target_pairs={{0,4},{4,0},{8,12},{12,8},{16,20},{20,16},{24,28},{28,24},{1,5},{5... | collective-permute-start | bytes 442376 | tf_op jit(solution)/shard_map/ppermute | solution.py:210
  881.9 39.3 %collective-permute-start.81 = (bf16[96,3,4,64]{0,3,1,2:T(8,128)(2,1)S(1)}, bf16[96,3,4,64]{0,3,1,2:T(8,128)(2,1)S(1)}, u32[]{:S(2)}, u32[]{:S(2)}) collective-permute-start(bf16[96,3,4,64]{0,3,1,2:T(8,128)(2,1)S(1)} %copy-done.117), channel_id=1, source_target_pairs={{0,4},{4,0},{8,12},{12,8},{16,20},{20,16},{24,28},{28,24},{1,5},{5... | collective-permute-start | bytes 442376 | tf_op jit(solution)/shard_map/ppermute | solution.py:210
  941.8 49.3 %collective-permute-start.105 = (bf16[96,3,4,256]{3,0,1,2:T(8,128)(2,1)}, bf16[96,3,4,256]{3,0,1,2:T(8,128)(2,1)S(1)}, u32[]{:S(2)}, u32[]{:S(2)}) collective-permute-start(bf16[96,3,4,256]{3,0,1,2:T(8,128)(2,1)} %copy.429), channel_id=1, source_target_pairs={{0,4},{4,0},{8,12},{12,8},{16,20},{20,16},{24,28},{28,24},{1,5},{5... | collective-permute-start | bytes 1769480 | tf_op jit(solution)/shard_map/ppermute | solution.py:210
  944.2 48.9 %collective-permute-start.107 = (bf16[96,3,4,256]{3,0,1,2:T(8,128)(2,1)}, bf16[96,3,4,256]{3,0,1,2:T(8,128)(2,1)}, u32[]{:S(2)}, u32[]{:S(2)}) collective-permute-start(bf16[96,3,4,256]{3,0,1,2:T(8,128)(2,1)} %copy.431), channel_id=1, source_target_pairs={{0,4},{4,0},{8,12},{12,8},{16,20},{20,16},{24,28},{28,24},{1,5},{5... | collective-permute-start | bytes 1769480 | tf_op jit(solution)/shard_map/ppermute | solution.py:210
  991.2 15.7 %collective-permute-start.109 = (bf16[96,3,4,256]{3,0,1,2:T(8,128)(2,1)S(1)}, bf16[96,3,4,256]{3,0,1,2:T(8,128)(2,1)S(1)}, u32[]{:S(2)}, u32[]{:S(2)}) collective-permute-start(bf16[96,3,4,256]{3,0,1,2:T(8,128)(2,1)S(1)} %add_convert_fusion.19), channel_id=1, source_target_pairs={{0,16},{4,20},{8,24},{12,28},{16,0},{20,4},{24,8},{28,12},{1,17},{... | collective-permute-start | bytes 1769480 | tf_op jit(solution)/shard_map/ppermute | solution.py:210
  992.7 16.0 %collective-permute-start.116 = (bf16[96,3,4,256]{3,0,1,2:T(8,128)(2,1)S(1)}, bf16[96,3,4,256]{3,0,1,2:T(8,128)(2,1)S(1)}, u32[]{:S(2)}, u32[]{:S(2)}) collective-permute-start(bf16[96,3,4,256]{3,0,1,2:T(8,128)(2,1)S(1)} %copy-done.94), channel_id=1, source_target_pairs={{0,4},{4,0},{8,12},{12,8},{16,20},{20,16},{24,28},{28,24},{1,5},{5... | collective-permute-start | bytes 1769480 | tf_op jit(solution)/shard_map/ppermute | solution.py:210
  993.2 15.6 %collective-permute-start.123 = (bf16[96,3,4,256]{3,0,1,2:T(8,128)(2,1)S(1)}, bf16[96,3,4,256]{3,0,1,2:T(8,128)(2,1)S(1)}, u32[]{:S(2)}, u32[]{:S(2)}) collective-permute-start(bf16[96,3,4,256]{3,0,1,2:T(8,128)(2,1)S(1)} %copy-done.93), channel_id=1, source_target_pairs={{0,4},{4,0},{8,12},{12,8},{16,20},{20,16},{24,28},{28,24},{1,5},{5... | collective-permute-start | bytes 1769480 | tf_op jit(solution)/shard_map/ppermute | solution.py:210
  993.3 17.3 %collective-permute-start.118 = (bf16[96,3,4,256]{3,0,1,2:T(8,128)(2,1)S(1)}, bf16[96,3,4,256]{3,0,1,2:T(8,128)(2,1)S(1)}, u32[]{:S(2)}, u32[]{:S(2)}) collective-permute-start(bf16[96,3,4,256]{3,0,1,2:T(8,128)(2,1)S(1)} %add_convert_fusion.12), channel_id=1, source_target_pairs={{0,8},{4,12},{8,0},{12,4},{16,24},{20,28},{24,16},{28,20},{1,9},{5... | collective-permute-start | bytes 1769480 | tf_op jit(solution)/shard_map/ppermute | solution.py:210
  995.5 17.3 %collective-permute-start.125 = (bf16[96,3,4,256]{3,0,1,2:T(8,128)(2,1)S(1)}, bf16[96,3,4,256]{3,0,1,2:T(8,128)(2,1)S(1)}, u32[]{:S(2)}, u32[]{:S(2)}) collective-permute-start(bf16[96,3,4,256]{3,0,1,2:T(8,128)(2,1)S(1)} %copy-done.92), channel_id=1, source_target_pairs={{0,4},{4,0},{8,12},{12,8},{16,20},{20,16},{24,28},{28,24},{1,5},{5... | collective-permute-start | bytes 1769480 | tf_op jit(solution)/shard_map/ppermute | solution.py:210
  1006.9 16.2 %collective-permute-start.127 = (bf16[96,3,4,256]{3,0,1,2:T(8,128)(2,1)S(1)}, bf16[96,3,4,256]{3,0,1,2:T(8,128)(2,1)S(1)}, u32[]{:S(2)}, u32[]{:S(2)}) collective-permute-start(bf16[96,3,4,256]{3,0,1,2:T(8,128)(2,1)S(1)} %add_convert_fusion.5), channel_id=1, source_target_pairs={{0,16},{4,20},{8,24},{12,28},{16,0},{20,4},{24,8},{28,12},{1,17},{... | collective-permute-start | bytes 1769480 | tf_op jit(solution)/shard_map/ppermute | solution.py:210
  1008.7 15.1 %collective-permute-start.113 = (bf16[96,3,4,256]{3,0,1,2:T(8,128)(2,1)S(1)}, bf16[96,3,4,256]{3,0,1,2:T(8,128)(2,1)S(1)}, u32[]{:S(2)}, u32[]{:S(2)}) collective-permute-start(bf16[96,3,4,256]{3,0,1,2:T(8,128)(2,1)S(1)} %copy-done.91), channel_id=1, source_target_pairs={{0,4},{4,0},{8,12},{12,8},{16,20},{20,16},{24,28},{28,24},{1,5},{5... | collective-permute-start | bytes 1769480 | tf_op jit(solution)/shard_map/ppermute | solution.py:210
  1008.8 27.0 %collective-permute-start.106 = (bf16[96,3,4,256]{3,0,1,2:T(8,128)(2,1)S(1)}, bf16[96,3,4,256]{3,0,1,2:T(8,128)(2,1)S(1)}, u32[]{:S(2)}, u32[]{:S(2)}) collective-permute-start(bf16[96,3,4,256]{3,0,1,2:T(8,128)(2,1)S(1)} %add_convert_fusion.22), channel_id=1, source_target_pairs={{0,16},{4,20},{8,24},{12,28},{16,0},{20,4},{24,8},{28,12},{1,17},{... | collective-permute-start | bytes 1769480 | tf_op jit(solution)/shard_map/ppermute | solution.py:210
  1010.6 25.4 %collective-permute-start.110 = (bf16[96,3,4,256]{3,0,1,2:T(8,128)(2,1)S(1)}, bf16[96,3,4,256]{3,0,1,2:T(8,128)(2,1)S(1)}, u32[]{:S(2)}, u32[]{:S(2)}) collective-permute-start(bf16[96,3,4,256]{3,0,1,2:T(8,128)(2,1)S(1)} %add_convert_fusion.18), channel_id=1, source_target_pairs={{0,8},{4,12},{8,0},{12,4},{16,24},{20,28},{24,16},{28,20},{1,9},{5... | collective-permute-start | bytes 1769480 | tf_op jit(solution)/shard_map/ppermute | solution.py:210
  1012.8 26.7 %collective-permute-start.115 = (bf16[96,3,4,256]{3,0,1,2:T(8,128)(2,1)S(1)}, bf16[96,3,4,256]{3,0,1,2:T(8,128)(2,1)S(1)}, u32[]{:S(2)}, u32[]{:S(2)}) collective-permute-start(bf16[96,3,4,256]{3,0,1,2:T(8,128)(2,1)S(1)} %add_convert_fusion.15), channel_id=1, source_target_pairs={{0,8},{4,12},{8,0},{12,4},{16,24},{20,28},{24,16},{28,20},{1,9},{5... | collective-permute-start | bytes 1769480 | tf_op jit(solution)/shard_map/ppermute | solution.py:210
  1023.2 25.3 %collective-permute-start.119 = (bf16[96,3,4,256]{3,0,1,2:T(8,128)(2,1)S(1)}, bf16[96,3,4,256]{3,0,1,2:T(8,128)(2,1)S(1)}, u32[]{:S(2)}, u32[]{:S(2)}) collective-permute-start(bf16[96,3,4,256]{3,0,1,2:T(8,128)(2,1)S(1)} %add_convert_fusion.11), channel_id=1, source_target_pairs={{0,16},{4,20},{8,24},{12,28},{16,0},{20,4},{24,8},{28,12},{1,17},{... | collective-permute-start | bytes 1769480 | tf_op jit(solution)/shard_map/ppermute | solution.py:210
  1023.8 25.1 %collective-permute-start.122 = (bf16[96,3,4,256]{3,0,1,2:T(8,128)(2,1)S(1)}, bf16[96,3,4,256]{3,0,1,2:T(8,128)(2,1)S(1)}, u32[]{:S(2)}, u32[]{:S(2)}) collective-permute-start(bf16[96,3,4,256]{3,0,1,2:T(8,128)(2,1)S(1)} %copy-done.90), channel_id=1, source_target_pairs={{0,4},{4,0},{8,12},{12,8},{16,20},{20,16},{24,28},{28,24},{1,5},{5... | collective-permute-start | bytes 1769480 | tf_op jit(solution)/shard_map/ppermute | solution.py:210
  1035.8 23.9 %collective-permute-start.124 = (bf16[96,3,4,256]{3,0,1,2:T(8,128)(2,1)S(1)}, bf16[96,3,4,256]{3,0,1,2:T(8,128)(2,1)S(1)}, u32[]{:S(2)}, u32[]{:S(2)}) collective-permute-start(bf16[96,3,4,256]{3,0,1,2:T(8,128)(2,1)S(1)} %add_convert_fusion.8), channel_id=1, source_target_pairs={{0,16},{4,20},{8,24},{12,28},{16,0},{20,4},{24,8},{28,12},{1,17},{... | collective-permute-start | bytes 1769480 | tf_op jit(solution)/shard_map/ppermute | solution.py:210
  1036.0 23.7 %collective-permute-start.128 = (bf16[96,3,4,256]{3,0,1,2:T(8,128)(2,1)S(1)}, bf16[96,3,4,256]{3,0,1,2:T(8,128)(2,1)S(1)}, u32[]{:S(2)}, u32[]{:S(2)}) collective-permute-start(bf16[96,3,4,256]{3,0,1,2:T(8,128)(2,1)S(1)} %add_convert_fusion.4), channel_id=1, source_target_pairs={{0,8},{4,12},{8,0},{12,4},{16,24},{20,28},{24,16},{28,20},{1,9},{5... | collective-permute-start | bytes 1769480 | tf_op jit(solution)/shard_map/ppermute | solution.py:210
  1039.4 20.7 %collective-permute-start.111 = (bf16[96,3,2,256]{3,0,1,2:T(8,128)(2,1)S(1)}, bf16[96,3,2,256]{3,0,1,2:T(8,128)(2,1)S(1)}, u32[]{:S(2)}, u32[]{:S(2)}) collective-permute-start(bf16[96,3,2,256]{3,0,1,2:T(8,128)(2,1)S(1)} %slice.294), channel_id=1, source_target_pairs={{0,1},{1,0},{2,3},{3,2},{4,5},{5,4},{6,7},{7,6},{8,9},{9,8},{10,11... | collective-permute-start | bytes 884744 | tf_op jit(solution)/shard_map/ppermute | solution.py:210
  1048.8 13.9 %collective-permute-start.120 = (bf16[96,3,2,256]{3,0,1,2:T(8,128)(2,1)S(1)}, bf16[96,3,2,256]{3,0,1,2:T(8,128)(2,1)S(1)}, u32[]{:S(2)}, u32[]{:S(2)}) collective-permute-start(bf16[96,3,2,256]{3,0,1,2:T(8,128)(2,1)S(1)} %slice.299), channel_id=1, source_target_pairs={{0,1},{1,0},{2,3},{3,2},{4,5},{5,4},{6,7},{7,6},{8,9},{9,8},{10,11... | collective-permute-start | bytes 884744 | tf_op jit(solution)/shard_map/ppermute | solution.py:210
  1060.1 12.8 %collective-permute-start.129 = (bf16[96,3,2,256]{3,0,1,2:T(8,128)(2,1)S(1)}, bf16[96,3,2,256]{3,0,1,2:T(8,128)(2,1)S(1)}, u32[]{:S(2)}, u32[]{:S(2)}) collective-permute-start(bf16[96,3,2,256]{3,0,1,2:T(8,128)(2,1)S(1)} %slice.304), channel_id=1, source_target_pairs={{0,1},{1,0},{2,3},{3,2},{4,5},{5,4},{6,7},{7,6},{8,9},{9,8},{10,11... | collective-permute-start | bytes 884744 | tf_op jit(solution)/shard_map/ppermute | solution.py:210
  1060.3 12.7 %collective-permute-start.112 = (bf16[96,3,256]{2,0,1:T(8,128)(2,1)S(1)}, bf16[96,3,256]{2,0,1:T(8,128)(2,1)S(1)}, u32[]{:S(2)}, u32[]{:S(2)}) collective-permute-start(bf16[96,3,256]{2,0,1:T(8,128)(2,1)S(1)} %slice_bitcast_fusion.10), channel_id=1, source_target_pairs={{0,2},{1,3},{2,0},{3,1},{4,6},{5,7},{6,4},{7,5},{8,10},{9,11},{10,... | collective-permute-start | bytes 442376 | tf_op jit(solution)/shard_map/ppermute | solution.py:210
  1062.8 17.0 %collective-permute-start.121 = (bf16[96,3,256]{2,0,1:T(8,128)(2,1)S(1)}, bf16[96,3,256]{2,0,1:T(8,128)(2,1)S(1)}, u32[]{:S(2)}, u32[]{:S(2)}) collective-permute-start(bf16[96,3,256]{2,0,1:T(8,128)(2,1)S(1)} %slice_bitcast_fusion.8), channel_id=1, source_target_pairs={{0,2},{1,3},{2,0},{3,1},{4,6},{5,7},{6,4},{7,5},{8,10},{9,11},{10,... | collective-permute-start | bytes 442376 | tf_op jit(solution)/shard_map/ppermute | solution.py:210
  (204 other events, 2239.2 us)

commit v2 on v1

v2 whole, which is shorter than its diff:
```python
import functools
import math

import jax
import jax.numpy as jnp
from jax import lax
from jax.experimental import pallas as pl
from jax.experimental.pallas import tpu as pltpu
from jax.sharding import PartitionSpec as P

HEAD = 64
SEQ = 1024
GROUP = 4
QB = 256
BLOCKS = 8
LOG2E = 1.4426950408889634
INV_ROOT_HEAD = 1.0 / math.sqrt(HEAD)
SCALE = LOG2E * INV_ROOT_HEAD
NORM_EPS = 1e-12
INV_ROOT_TWO = 0.7071067811865476
INV_ROOT_TWO_PI = 0.3989422804014327
FF_CHUNKS = 3
NT = (((1,), (1,)), ((), ()))
NN = (((1,), (0,)), ((), ()))
BF16 = jnp.bfloat16
F32 = jnp.float32


def mm(left, right, dims=NN):
    return lax.dot_general(left, right, dims, preferred_element_type=F32)


def params(**more):
    return pltpu.CompilerParams(vmem_limit_bytes=56 << 20, **more)


def cost(flops, nbytes, exps=0):
    return pl.CostEstimate(flops=flops, bytes_accessed=nbytes, transcendentals=exps)


SMEM = pl.BlockSpec(memory_space=pltpu.SMEM)


def whole(*shape):
    return pl.BlockSpec(shape, lambda *_: (0,) * len(shape))


def shaped(dtype, *shape):
    return jax.ShapeDtypeStruct(shape, dtype)


def assemble(place_ref, piece_refs, full_ref):
    rows = piece_refs[0].shape[0]
    for k, piece_ref in enumerate(piece_refs):
        start = pl.multiple_of(place_ref[k] * rows, rows)
        full_ref[pl.ds(start, rows), :] = piece_ref[...]


def deal(place_ref, full_ref, even_ref, odd_ref):
    rows = full_ref.shape[0] // BLOCKS
    for k in range(BLOCKS):
        start = pl.multiple_of(place_ref[k] * rows, rows)
        target = odd_ref if k % 2 else even_ref
        target[k // 2] = full_ref[pl.ds(start, rows), :]


def fill_row_distance(dist_ref):
    row = lax.broadcasted_iota(jnp.int32, dist_ref.shape, 0)
    col = lax.broadcasted_iota(jnp.int32, dist_ref.shape, 1)
    dist_ref[...] = jnp.abs(row - col + (SEQ - QB)).astype(F32) * LOG2E


def fill_distance(dist_ref):
    row = lax.broadcasted_iota(jnp.int32, dist_ref.shape, 0)
    col = lax.broadcasted_iota(jnp.int32, dist_ref.shape, 1)
    dist_ref[...] = jnp.abs(row - col - (SEQ - QB)).astype(F32) * LOG2E


def attend_kernel(base, place_ref, slope_ref, x_ref, bias_ref, *rest):
    piece_refs = rest[:BLOCKS]
    qkv_ref, ctx_ref, lse_ref, full_ref, dist_ref = rest[BLOCKS:]
    width = GROUP * HEAD
    assemble(place_ref, piece_refs, full_ref)
    fill_row_distance(dist_ref)
    for block in range(SEQ // QB):
        rows = slice(block * QB, (block + 1) * QB)
        qkv_ref[rows, :] = (mm(x_ref[rows, :], full_ref[...]) + bias_ref[...]).astype(BF16)
    lane = lax.broadcasted_iota(jnp.int32, (1, 128), 1)
    for pair in range(GROUP // 2):
        keys = qkv_ref[:, width + 128 * pair : width + 128 * pair + 128]
        values = qkv_ref[:, 2 * width + 128 * pair : 2 * width + 128 * pair + 128]
        for block in range(SEQ // QB):
            rows = slice(block * QB, (block + 1) * QB)
            start = SEQ - QB - block * QB
            q = qkv_ref[rows, 128 * pair : 128 * pair + 128]
            parts = []
            stats = []
            for side in range(2):
                own = (lane < HEAD) if side == 0 else (lane >= HEAD)
                slope = slope_ref[base + 2 * pair + side]
                s = mm(jnp.where(own, q, jnp.zeros_like(q)), keys, NT) * SCALE
                s = s - slope * dist_ref[:, start : start + SEQ]
                top = jnp.max(s, axis=1, keepdims=True)
                w = jnp.exp2(s - top)
                total = jnp.sum(w, axis=1, keepdims=True)
                p = (w * (1.0 / total)).astype(BF16)
                parts.append(mm(p, values))
                stats.append(top + jnp.log2(total))
            ctx = jnp.where(lane < HEAD, parts[0], parts[1])
            ctx_ref[rows, 128 * pair : 128 * pair + 128] = ctx.astype(BF16)
            flipped = jnp.where(lane < HEAD, stats[0], stats[1]).T
            lse_ref[2 * pair : 2 * pair + 1, rows] = flipped[0:1, :]
            lse_ref[2 * pair + 1 : 2 * pair + 2, rows] = flipped[HEAD : HEAD + 1, :]


def attend_forward(group, place, slopes, x, bias, pieces):
    width = GROUP * HEAD
    depth = x.shape[1]
    return pl.pallas_call(
        functools.partial(attend_kernel, group * GROUP),
        grid=(1,),
        in_specs=[SMEM, SMEM, whole(SEQ, depth), whole(1, 3 * width)]
        + [whole(depth // BLOCKS, 3 * width)] * BLOCKS,
        out_specs=[whole(SEQ, 3 * width), whole(SEQ, width), whole(GROUP, SEQ)],
        out_shape=[
            shaped(BF16, SEQ, 3 * width),
            shaped(BF16, SEQ, width),
            shaped(F32, GROUP, SEQ),
        ],
        scratch_shapes=[
            pltpu.VMEM((depth, 3 * width), BF16),
            pltpu.VMEM((QB, 2 * SEQ - QB), F32),
        ],
        compiler_params=params(),
        cost_estimate=cost(13_000_000_000, 8 << 20, 4 << 20),
        name="attend_forward",
    )(place, slopes, x, bias, *pieces)


def attend_back_kernel(
    base, last, place_ref, slope_ref, qkv_ref, lse_ref, dctx_ref, x_t_ref, acc_in_ref, *rest
):
    piece_refs = rest[:BLOCKS]
    (even_ref, odd_ref, sums_ref, acc_out_ref, full_ref, dist_ref, acc_ref, dqt_ref, dqkv_ref) = rest[
        BLOCKS:
    ]
    width = GROUP * HEAD
    fill_distance(dist_ref)
    assemble(place_ref, piece_refs, full_ref)
    lane = lax.broadcasted_iota(jnp.int32, (1, 128), 1)
    for pair in range(GROUP // 2):
        cols = slice(128 * pair, 128 * pair + 128)
        keys = qkv_ref[:, width + 128 * pair : width + 128 * pair + 128]
        values = qkv_ref[:, 2 * width + 128 * pair : 2 * width + 128 * pair + 128]
        keys_t = keys.T
        for side in range(2):
            own = (lane < HEAD) if side == 0 else (lane >= HEAD)
            own_rows = slice(HEAD * side, HEAD * side + HEAD)
            slope = slope_ref[base + 2 * pair + side]
            for block in range(SEQ // QB):
                rows = slice(block * QB, (block + 1) * QB)
                start = SEQ - QB - block * QB
                q = qkv_ref[rows, cols]
                q = jnp.where(own, q, jnp.zeros_like(q))
                do = dctx_ref[rows, cols]
                do = jnp.where(own, do, jnp.zeros_like(do))
                s = mm(keys, q, NT) * SCALE
                s = s - slope * dist_ref[start : start + SEQ, :]
                p = jnp.exp2(s - lse_ref[2 * pair + side : 2 * pair + side + 1, rows])
                dp = mm(values, do, NT)
                inner = jnp.sum(p * dp, axis=0, keepdims=True)
                ds = (p * (dp - inner)).astype(BF16)
                p = p.astype(BF16)
                dv = mm(p, do)
                dk = mm(ds, q)
                if block == 0 and side == 0:
                    acc_ref[:, 0:128] = dk
                    acc_ref[:, 128:256] = dv
                else:
                    acc_ref[:, 0:128] += dk
                    acc_ref[:, 128:256] += dv
                dqt_ref[own_rows, rows] = mm(keys_t[own_rows], ds)
        dq = dqt_ref[...].T * INV_ROOT_HEAD
        dk = acc_ref[:, 0:128] * INV_ROOT_HEAD
        dv = acc_ref[:, 128:256]
        dqkv_ref[:, 128 * pair : 128 * pair + 128] = dq.astype(BF16)
        dqkv_ref[:, width + 128 * pair : width + 128 * pair + 128] = dk.astype(BF16)
        dqkv_ref[:, 2 * width + 128 * pair : 2 * width + 128 * pair + 128] = dv.astype(BF16)
        sums_ref[0:1, cols] = jnp.sum(dq, axis=0, keepdims=True)
        sums_ref[1:2, cols] = jnp.sum(dv, axis=0, keepdims=True)
    for block in range(SEQ // QB):
        rows = slice(block * QB, (block + 1) * QB)
        d_rows = acc_in_ref[rows, :] + mm(dqkv_ref[rows, :], full_ref[...], NT)
        acc_out_ref[rows, :] = d_rows.astype(acc_out_ref.dtype)
    full_ref[...] = mm(x_t_ref[...], dqkv_ref[...]).astype(BF16)
    deal(place_ref, full_ref, even_ref, odd_ref)


def attend_backward(group, last, place, slopes, qkv, lse, d_context, x_t, d_tokens, pieces):
    width = GROUP * HEAD
    depth = x_t.shape[0]
    rows = depth // BLOCKS
    return pl.pallas_call(
        functools.partial(attend_back_kernel, group * GROUP, last),
        grid=(1,),
        in_specs=[
            SMEM,
            SMEM,
            whole(SEQ, 3 * width),
            whole(GROUP, SEQ),
            pl.BlockSpec((SEQ, width), lambda _: (0, group)),
            whole(depth, SEQ),
            whole(SEQ, depth),
        ]
        + [whole(rows, 3 * width)] * BLOCKS,
        out_specs=[
            whole(BLOCKS // 2, rows, 3 * width),
            whole(BLOCKS // 2, rows, 3 * width),
            whole(2, width),
            whole(SEQ, depth),
        ],
        out_shape=[
            shaped(BF16, BLOCKS // 2, rows, 3 * width),
            shaped(BF16, BLOCKS // 2, rows, 3 * width),
            shaped(F32, 2, width),
            shaped(BF16 if last else F32, SEQ, depth),
        ],
        scratch_shapes=[
            pltpu.VMEM((depth, 3 * width), BF16),
            pltpu.VMEM((2 * SEQ - QB, QB), F32),
            pltpu.VMEM((SEQ, 256), F32),
            pltpu.VMEM((128, SEQ), F32),
            pltpu.VMEM((SEQ, 3 * width), BF16),
        ],
        compiler_params=params(),
        cost_estimate=cost(19_000_000_000, 8 << 20, 4 << 20),
        name="attend_backward",
    )(place, slopes, qkv, lse, d_context, x_t, d_tokens, *pieces)


def row_mean(value):
    return jnp.mean(value, axis=1, keepdims=True)


def normalize(resid):
    center = resid - row_mean(resid)
    inverse = lax.rsqrt(row_mean(center * center) + NORM_EPS)
    return center * inverse, inverse


def norm_pull(grad_rows, normed, inverse, gain):
    scaled = grad_rows * gain
    return inverse * (scaled - row_mean(scaled) - normed * row_mean(scaled * normed))


def add_sums(sums_ref, values, first):
    for place, value in enumerate(values):
        row = jnp.sum(value, axis=0, keepdims=True)
        if first:
            sums_ref[place : place + 1, :] = row
        else:
            sums_ref[place : place + 1, :] += row


def join_kernel(place_ref, x_ref, vec_ref, *rest):
    ctx_refs = rest[:3]
    piece_refs = rest[3 : 3 + BLOCKS]
    normed_ref, inverse_ref, low_ref, low_t_ref, full_ref = rest[3 + BLOCKS :]
    assemble(place_ref, piece_refs, full_ref)
    width = ctx_refs[0].shape[1]
    for block in range(SEQ // QB):
        rows = slice(block * QB, (block + 1) * QB)
        total = x_ref[rows, :].astype(F32) + vec_ref[0:1, :]
        for g, ctx_ref in enumerate(ctx_refs):
            total += mm(ctx_ref[rows, :], full_ref[:, g * width : (g + 1) * width], NT)
        normed, inverse = normalize(total)
        normed_ref[rows, :] = normed
        inverse_ref[rows, :] = jnp.broadcast_to(inverse, (QB, 128))
        low = normed * vec_ref[1:2, :] + vec_ref[2:3, :]
        low_ref[rows, :] = low.astype(BF16)
        low_t_ref[:, rows] = low.T.astype(BF16)


def join(place, x, vec, ctx, pieces):
    depth = x.shape[1]
    rows = depth // BLOCKS
    return pl.pallas_call(
        join_kernel,
        grid=(1,),
        in_specs=[SMEM, whole(SEQ, depth), whole(8, depth)]
        + [whole(SEQ, ctx[0].shape[1])] * 3
        + [whole(rows, depth)] * BLOCKS,
        out_specs=[whole(SEQ, depth), whole(SEQ, 128), whole(SEQ, depth), whole(depth, SEQ)],
        out_shape=[
            shaped(F32, SEQ, depth),
            shaped(F32, SEQ, 128),
            shaped(BF16, SEQ, depth),
            shaped(BF16, depth, SEQ),
        ],
        scratch_shapes=[pltpu.VMEM((depth, depth), BF16)],
        compiler_params=params(),
        cost_estimate=cost(4_000_000_000, 10 << 20),
        name="join",
    )(place, x, vec, *ctx, *pieces)


def turn_kernel(ffn_ref, normed1_ref, cot_ref, vec_ref, out_ref, d_ref, low_ref, low_t_ref, sums_ref):
    for block in range(SEQ // QB):
        rows = slice(block * QB, (block + 1) * QB)
        hidden = normed1_ref[rows, :] * vec_ref[1:2, :] + vec_ref[2:3, :]
        normed, inverse = normalize(hidden + ffn_ref[rows, :] + vec_ref[3:4, :])
        out_ref[rows, :] = (normed * vec_ref[4:5, :] + vec_ref[5:6, :]).astype(BF16)
        grad = cot_ref[rows, :].astype(F32)
        d_resid = norm_pull(grad, normed, inverse, vec_ref[4:5, :])
        d_ref[rows, :] = d_resid
        low_ref[rows, :] = d_resid.astype(BF16)
        low_t_ref[:, rows] = d_resid.T.astype(BF16)
        add_sums(sums_ref, (grad * normed, grad, d_resid), block == 0)


def turn(ffn, normed1, cot, vec):
    depth = cot.shape[1]
    return pl.pallas_call(
        turn_kernel,
        grid=(1,),
        in_specs=[whole(SEQ, depth)] * 3 + [whole(8, depth)],
        out_specs=[whole(SEQ, depth)] * 3 + [whole(depth, SEQ), whole(3, depth)],
        out_shape=[
            shaped(BF16, SEQ, depth),
            shaped(F32, SEQ, depth),
            shaped(BF16, SEQ, depth),
            shaped(BF16, depth, SEQ),
            shaped(F32, 3, depth),
        ],
        compiler_params=params(),
        cost_estimate=cost(4_000_000_000, 16 << 20),
        name="turn",
    )(ffn, normed1, cot, vec)


def rejoin_kernel(place_ref, d_hidden_ref, normed_ref, inverse_ref, vec_ref, *rest):
    ctx_refs = rest[:3]
    piece_refs = rest[3 : 3 + BLOCKS]
    d_ref, dctx_ref, even_ref, odd_ref, sums_ref, full_ref, low_t_ref = rest[3 + BLOCKS :]
    width = ctx_refs[0].shape[1]
    assemble(place_ref, piece_refs, full_ref)
    for block in range(SEQ // QB):
        rows = slice(block * QB, (block + 1) * QB)
        normed = normed_ref[rows, :]
        grad = d_hidden_ref[rows, :]
        d_resid = norm_pull(grad, normed, inverse_ref[rows, 0:1], vec_ref[1:2, :])
        d_ref[rows, :] = d_resid
        low = d_resid.astype(BF16)
        low_t_ref[:, rows] = d_resid.T.astype(BF16)
        dctx_ref[rows, :] = mm(low, full_ref[...]).astype(BF16)
        add_sums(sums_ref, (grad * normed, grad, d_resid), block == 0)
    for g, ctx_ref in enumerate(ctx_refs):
        full_ref[:, g * width : (g + 1) * width] = mm(low_t_ref[...], ctx_ref[...]).astype(BF16)
    deal(place_ref, full_ref, even_ref, odd_ref)


def rejoin(place, d_hidden, normed, inverse, vec, ctx, pieces):
    depth = d_hidden.shape[1]
    rows = depth // BLOCKS
    return pl.pallas_call(
        rejoin_kernel,
        grid=(1,),
        in_specs=[SMEM, whole(SEQ, depth), whole(SEQ, depth), whole(SEQ, 128), whole(8, depth)]
        + [whole(SEQ, ctx[0].shape[1])] * 3
        + [whole(rows, depth)] * BLOCKS,
        out_specs=[
            whole(SEQ, depth),
            whole(SEQ, depth),
            whole(BLOCKS // 2, rows, depth),
            whole(BLOCKS // 2, rows, depth),
            whole(3, depth),
        ],
        out_shape=[
            shaped(F32, SEQ, depth),
            shaped(BF16, SEQ, depth),
            shaped(BF16, BLOCKS // 2, rows, depth),
            shaped(BF16, BLOCKS // 2, rows, depth),
            shaped(F32, 3, depth),
        ],
        scratch_shapes=[pltpu.VMEM((depth, depth), BF16), pltpu.VMEM((depth, SEQ), BF16)],
        compiler_params=params(),
        cost_estimate=cost(6_000_000_000, 14 << 20),
        name="rejoin",
    )(place, d_hidden, normed, inverse, vec, *ctx, *pieces)


def gelu_parts(gate):
    normal_cdf = 0.5 * (1.0 + lax.erf(gate * INV_ROOT_TWO))
    density = jnp.exp(-0.5 * gate * gate) * INV_ROOT_TWO_PI
    return gate * normal_cdf, normal_cdf + gate * density


def feed_kernel(first, place_ref, low_ref, *rest):
    if not first:
        acc_in_ref, *rest = rest
    piece_refs = rest[:BLOCKS]
    acc_ref, gated_ref, slope_ref, active_ref, full_ref = rest[BLOCKS:]
    part = gated_ref.shape[1]
    assemble(place_ref, piece_refs, full_ref)
    step = pl.program_id(0)
    for block in range(SEQ // QB):
        rows = slice(block * QB, (block + 1) * QB)
        both = mm(low_ref[rows, :], full_ref[:, : 2 * part])
        up = both[:, part:]
        active, slope = gelu_parts(both[:, :part])
        gated = (active * up).astype(BF16)
        gated_ref[rows, :] = gated
        slope_ref[rows, :] = (slope * up).astype(BF16)
        active_ref[rows, :] = active.astype(BF16)
        more = mm(gated, full_ref[:, 2 * part :], NT)

        @pl.when(step == 0)
        def _():
            acc_ref[rows, :] = more if first else acc_in_ref[rows, :] + more

        @pl.when(step > 0)
        def _():
            acc_ref[rows, :] += more


def feed(place, low, acc, pieces):
    depth = low.shape[1]
    steps, rows, lanes = pieces[0].shape
    part = lanes // 3
    columns = pl.BlockSpec((SEQ, part), lambda m: (0, m))
    first = acc is None
    return pl.pallas_call(
        functools.partial(feed_kernel, first),
        grid=(steps,),
        in_specs=[SMEM, whole(SEQ, depth)]
        + ([] if first else [whole(SEQ, depth)])
        + [pl.BlockSpec((None, rows, lanes), lambda m: (m, 0, 0))] * BLOCKS,
        out_specs=[whole(SEQ, depth), columns, columns, columns],
        out_shape=[shaped(F32, SEQ, depth)] + [shaped(BF16, SEQ, steps * part)] * 3,
        scratch_shapes=[pltpu.VMEM((depth, lanes), BF16)],
        compiler_params=params(),
        cost_estimate=cost(10_000_000_000, 16 << 20),
        name="feed",
    )(place, low, *([] if first else [acc]), *pieces)


def feed_back_kernel(
    place_ref, d_ref, d_t_ref, low_t_ref, acc_in_ref, gated_ref, slope_ref, active_ref, *rest
):
    piece_refs = rest[:BLOCKS]
    acc_ref, even_ref, odd_ref, full_ref, gate_up_ref = rest[BLOCKS:]
    part = gated_ref.shape[1]
    assemble(place_ref, piece_refs, full_ref)
    step = pl.program_id(0)
    for block in range(SEQ // QB):
        rows = slice(block * QB, (block + 1) * QB)
        d_gated = mm(d_ref[rows, :], full_ref[:, 2 * part :])
        gate_up_ref[rows, :part] = (d_gated * slope_ref[rows, :].astype(F32)).astype(BF16)
        gate_up_ref[rows, part:] = (d_gated * active_ref[rows, :].astype(F32)).astype(BF16)
        more = mm(gate_up_ref[rows, :], full_ref[:, : 2 * part], NT)

        @pl.when(step == 0)
        def _():
            acc_ref[rows, :] = acc_in_ref[rows, :] + more

        @pl.when(step > 0)
        def _():
            acc_ref[rows, :] += more

    full_ref[:, : 2 * part] = mm(low_t_ref[...], gate_up_ref[...]).astype(BF16)
    full_ref[:, 2 * part :] = mm(d_t_ref[...], gated_ref[...]).astype(BF16)
    deal(place_ref, full_ref, even_ref, odd_ref)


def feed_back(place, d_low, d_low_t, low_t, acc, gated, slope, active, pieces):
    depth = d_low.shape[1]
    steps, rows, lanes = pieces[0].shape
    part = lanes // 3
    columns = pl.BlockSpec((SEQ, part), lambda m: (0, m))
    dealt = pl.BlockSpec((BLOCKS // 2, None, rows, lanes), lambda m: (0, m, 0, 0))
    return pl.pallas_call(
        feed_back_kernel,
        grid=(steps,),
        in_specs=[SMEM, whole(SEQ, depth), whole(depth, SEQ), whole(depth, SEQ), whole(SEQ, depth)]
        + [columns] * 3
        + [pl.BlockSpec((None, rows, lanes), lambda m: (m, 0, 0))] * BLOCKS,
        out_specs=[whole(SEQ, depth), dealt, dealt],
        out_shape=[shaped(F32, SEQ, depth)] + [shaped(BF16, BLOCKS // 2, steps, rows, lanes)] * 2,
        scratch_shapes=[pltpu.VMEM((depth, lanes), BF16), pltpu.VMEM((SEQ, 2 * part), BF16)],
        compiler_params=params(),
        cost_estimate=cost(12_000_000_000, 30 << 20),
        name="feed_back",
    )(place, d_low, d_low_t, low_t, acc, gated, slope, active, *pieces)


class Links:
    def __init__(self, mesh_shape):
        self.dp = mesh_shape["dp"]
        self.tensor = mesh_shape["tensor"]
        self.paired = self.dp == 8 and self.tensor == 4

    def swap(self, value, axis, bit):
        size = self.dp if axis == "dp" else self.tensor
        return lax.ppermute(value, axis, [(i, i ^ bit) for i in range(size)])

    def tensor_order(self):
        if self.paired:
            return jnp.array([0, 2, 1, 3], jnp.int32) ^ lax.axis_index("tensor")
        return jnp.arange(self.tensor, dtype=jnp.int32)

    def tensor_places(self):
        index = jnp.arange(self.tensor, dtype=jnp.int32)
        if self.paired:
            index = index ^ lax.axis_index("tensor")
            return (index & 1) * 2 + (index >> 1)
        return index

    def row_order(self):
        blocks = jnp.arange(BLOCKS, dtype=jnp.int32)
        return blocks ^ lax.axis_index("dp") if self.paired else blocks

    def spread(self, value, bits):
        if not self.paired:
            gathered = lax.all_gather(value, "dp", axis=value.ndim - 2, tiled=True)
            return jnp.split(gathered, BLOCKS, axis=value.ndim - 2)
        held = {0: value}
        for bit in bits:
            for place in list(held):
                held[place | bit] = self.swap(held[place], "dp", bit)
        return [held[place] for place in range(BLOCKS)]

    def columns_of_heads(self, piece):
        rows, lanes = piece.shape
        if not self.paired:
            gathered = lax.all_gather(piece.reshape(rows, lanes // HEAD, 1, HEAD), "tensor", axis=2, tiled=True)
            return gathered.reshape(rows, -1)
        far = self.swap(piece, "tensor", 2)
        pair = jnp.concatenate(
            [part[:, i : i + HEAD] for i in range(0, lanes, HEAD) for part in (piece, far)], axis=1
        )
        near = self.swap(pair, "tensor", 1)
        return jnp.concatenate(
            [part[:, i : i + 128] for i in range(0, 2 * lanes, 128) for part in (pair, near)], axis=1
        )

    def columns_of_units(self, piece):
        if not self.paired:
            return lax.all_gather(piece, "tensor", axis=0)
        pair = jnp.stack([piece, self.swap(piece, "tensor", 2)])
        return jnp.concatenate([pair, self.swap(pair, "tensor", 1)])

    def sum_rows(self, even, odd, x_first):
        if not self.paired:
            whole_rows = jnp.stack([even, odd], axis=1)
            whole_rows = whole_rows.reshape((BLOCKS,) + even.shape[1:]).astype(F32)
            whole_rows = jnp.moveaxis(whole_rows, 0, -3)
            whole_rows = whole_rows.reshape(whole_rows.shape[:-3] + (-1, whole_rows.shape[-1]))
            return lax.psum_scatter(
                whole_rows, "dp", scatter_dimension=whole_rows.ndim - 2, tiled=True
            )
        arrived = self.swap(odd, "dp", 1)
        first, second = (2, 4) if x_first else (4, 2)
        out = (1, 3) if x_first else (2, 3)
        stay = (0, 2) if x_first else (0, 1)
        sent = add_low(
            jnp.stack([even[i] for i in out]), jnp.stack([arrived[i] for i in out])
        )
        mine = add_low(
            jnp.stack([even[i] for i in stay]), jnp.stack([arrived[i] for i in stay])
        )
        arrived = self.swap(sent, "dp", first)
        sent = add_low(mine[1], arrived[1])
        mine = add_low(mine[0], arrived[0])
        return add_low(mine, self.swap(sent, "dp", second))

    def sum_units(self, mine):
        if not self.paired:
            return lax.psum_scatter(mine, "tensor", scatter_dimension=0, tiled=False)
        arrived = self.swap(mine[2:], "tensor", 1)
        sent = add_low(mine[1], arrived[1])
        mine = add_low(mine[0], arrived[0])
        return mine.astype(F32) + self.swap(sent, "tensor", 2).astype(F32)

    def sum_heads(self, mine):
        rows, lanes = mine.shape
        if not self.paired:
            mine = mine.reshape(rows, lanes // 256, 4, HEAD)
            return lax.psum_scatter(mine, "tensor", scatter_dimension=2, tiled=True).reshape(rows, -1)

        def take(value, size, at):
            return jnp.concatenate(
                [value[:, i + at : i + at + size] for i in range(0, value.shape[1], 2 * size)], axis=1
            )

        arrived = self.swap(take(mine, 128, 128), "tensor", 1)
        mine = add_low(take(mine, 128, 0), arrived)
        arrived = self.swap(take(mine, HEAD, HEAD), "tensor", 2)
        return take(mine, HEAD, 0).astype(F32) + arrived.astype(F32)

    def total(self, value):
        if not self.paired:
            return lax.psum(value, ("dp", "tensor"))
        for axis, bit in (("dp", 1), ("dp", 4), ("dp", 2), ("tensor", 1), ("tensor", 2)):
            value = value + self.swap(value, axis, bit)
        return value


def add_low(left, right):
    return (left.astype(F32) + right.astype(F32)).astype(BF16)


def local(
    links,
    tokens,
    qkv_weight,
    qv_bias,
    out_weight,
    out_bias,
    norm1_gain,
    norm1_shift,
    in_weight,
    down_weight,
    down_bias,
    norm2_gain,
    norm2_shift,
    cotangent,
):
    depth = tokens.shape[1]
    rows = qkv_weight.shape[0]
    n_tensor = links.tensor
    groups = qkv_weight.shape[2] // HEAD
    part = in_weight.shape[2] // FF_CHUNKS
    place = links.row_order()

    heads = [
        qkv_weight[:, c, g * HEAD : (g + 1) * HEAD] for g in range(groups) for c in range(3)
    ]
    columns = links.columns_of_heads(jnp.concatenate(heads + [out_weight], axis=1))
    pieces = [columns[:, i * depth : (i + 1) * depth] for i in range(groups + 1)]
    qkv_pieces = [links.spread(pieces[g], (4, 2, 1) if g % 2 else (2, 4, 1)) for g in range(groups)]
    out_pieces = links.spread(pieces[groups], (4, 2, 1))
    ff_pieces = []
    for c in range(FF_CHUNKS):
        cols = slice(c * part, (c + 1) * part)
        piece = jnp.concatenate(
            [in_weight[:, 0, cols], in_weight[:, 1, cols], down_weight[:, cols]], axis=1
        )
        ff_pieces.append(
            links.spread(links.columns_of_units(piece), (4, 2, 1) if c % 2 else (2, 4, 1))
        )

    order = links.tensor_order()
    head_ids = (order[None, :] * groups + jnp.arange(groups, dtype=jnp.int32)[:, None]).reshape(-1)
    powers = jnp.where(head_ids < 8, -(head_ids + 1).astype(F32), 7.5 - head_ids.astype(F32))
    slopes = jnp.exp2(powers)
    bias = qv_bias.reshape(2, n_tensor, groups, HEAD)[:, order].transpose(2, 0, 1, 3)
    bias = bias.reshape(groups, 2, n_tensor * HEAD)
    bias = jnp.concatenate([bias[:, 0], jnp.zeros_like(bias[:, 0]), bias[:, 1]], axis=1)
    vec = jnp.stack(
        [out_bias, norm1_gain, norm1_shift, down_bias, norm2_gain, norm2_shift, out_bias, out_bias]
    )
    tokens_t = tokens.T

    qkv, ctx, lse = [], [], []
    for g in range(groups):
        got = attend_forward(g, place, slopes, tokens, bias[g : g + 1], qkv_pieces[g])
        qkv.append(got[0])
        ctx.append(got[1])
        lse.append(got[2])
    normed1, inverse1, low, low_t = join(place, tokens, vec, ctx, out_pieces)
    acc = None
    kept = []
    for c in range(FF_CHUNKS):
        acc, *saved = feed(place, low, acc, ff_pieces[c])
        kept.append(saved)
    result, d_hidden, d_low, d_low_t, sums2 = turn(acc, normed1, cotangent, vec)

    ff_grads = []
    for c in range(FF_CHUNKS):
        d_hidden, even, odd = feed_back(
            place, d_low, d_low_t, low_t, d_hidden, *kept[c], ff_pieces[c]
        )
        ff_grads.append(links.sum_units(links.sum_rows(even, odd, c % 2 == 0)))
    d_tokens, d_context, even, odd, sums1 = rejoin(
        place, d_hidden, normed1, inverse1, vec, ctx, out_pieces
    )
    out_grad = links.sum_heads(links.sum_rows(even, odd, True))
    qkv_grads = []
    bias_grads = []
    for g in range(groups):
        even, odd, sums, d_tokens = attend_backward(
            g,
            g == groups - 1,
            place,
            slopes,
            qkv[g],
            lse[g],
            d_context,
            tokens_t,
            d_tokens,
            qkv_pieces[g],
        )
        qkv_grads.append(links.sum_heads(links.sum_rows(even, odd, g % 2 == 0)).reshape(rows, 3, HEAD))
        bias_grads.append(sums.reshape(2, n_tensor, HEAD))
    qkv_grad = jnp.concatenate(qkv_grads, axis=2)
    in_grad = jnp.stack(
        [
            jnp.concatenate([g[:, i * part : (i + 1) * part] for g in ff_grads], axis=1)
            for i in range(2)
        ],
        axis=1,
    )
    down_grad = jnp.concatenate([g[:, 2 * part :] for g in ff_grads], axis=1)
    back = links.tensor_places()
    qv_grad = jnp.stack(bias_grads, axis=2)[:, back].reshape(2, depth)
    sums = links.total(jnp.concatenate([qv_grad, sums1, sums2]))
    return (
        result,
        d_tokens,
        qkv_grad,
        sums[:2],
        out_grad,
        sums[4],
        sums[2],
        sums[3],
        in_grad,
        down_grad,
        sums[7],
        sums[5],
        sums[6],
    )


def solution(mesh):
    rows_all = P(("dp", "tensor"), None)
    columns_3d = P("dp", None, "tensor")
    columns_2d = P("dp", "tensor")
    return jax.shard_map(
        functools.partial(local, Links(mesh.shape)),
        mesh=mesh,
        in_specs=(
            rows_all,
            columns_3d,
            P(),
            columns_2d,
            P(),
            P(),
            P(),
            columns_3d,
            columns_2d,
            P(),
            P(),
            P(),
            rows_all,
        ),
        out_specs=(
            rows_all,
            rows_all,
            columns_3d,
            P(),
            columns_2d,
            P(),
            P(),
            P(),
            columns_3d,
            columns_2d,
            P(),
            P(),
            P(),
        ),
        check_vma=False,
    )
```

time: 1100 us -> 570 us (0.52)
  local copies, waits for them, and re-layouts: 529 us -> 37.3 us
  Pallas kernels: 77.9 us -> 260 us
  matrix products: 118 us -> 0 us
  waiting for transfers between devices: 233 us -> 157 us
    dynamic_update_slice x56 -> x0, local copies, waits for them, and re-layouts: 360 us -> none  [gather(): lax.dynamic_update_slice(whole, value, ((me ^ place) * rows, 0, 0, 0))]
    pallas_call x4 -> x15, Pallas kernels: 77.9 us -> 260 us  [the longest x3 73.8 us: feed_back(): pl.pallas_call(feed_back_kernel, grid=(steps,), in_specs=[SMEM, whole(SEQ...]
    dot_general x28 -> x0, matrix products: 118 us -> none  [the longest x3 20.4 us: local(): jnp.dot(d_ffn_low, down_full[c], preferred_element_type=jnp.float32)]
    ppermute x131 -> x97, waiting for transfers between devices: 233 us -> 157 us  [swap(): return lax.ppermute(value, axis, [(i, i ^ bit) for i in range(size)])]
    ppermute x21 -> x0, local copies, waits for them, and re-layouts: 35.3 us -> none  [swap(): return lax.ppermute(value, axis, [(i, i ^ bit) for i in range(size)])]
    unnamed x317 -> x159, local copies, waits for them, and re-layouts: 44.5 us -> 10.9 us
    convert_element_type x3 -> x0, local copies, waits for them, and re-layouts: 29.5 us -> none  [local(): grad = jnp.concatenate([in_grad, down_grad], axis=1).astype(jnp.bfloat16)]
    dynamic_slice x4 -> x0, local copies, waits for them, and re-layouts: 18.4 us -> none  [scatter(): lax.dynamic_slice_in_dim(grad, (me ^ place) * rows, rows, 0)]
  transfers between devices with their start and end apart: 131 -> 97, of which waited for: 52 -> 40; matrix products, arithmetic and copies ran while one was open for 49% -> 10% of each run, Pallas kernels for 3% -> 15%
where the time goes in v2:
time: 570 us; the launch traced here: 565 us
  Pallas kernels  260 us (46%)
  waiting for transfers between devices  157 us (28%)
  starting transfers between devices  79.5 us (14%)
  local copies, waits for them, and re-layouts  37.3 us (7%)
  other arithmetic  28.6 us (5%)
    ppermute x97, waiting for transfers between devices, swap(): return lax.ppermute(value, axis, [(i, i ^ bit) for i in range(size)])  157 us
    ppermute x97, starting transfers between devices, swap(): return lax.ppermute(value, axis, [(i, i ^ bit) for i in range(size)])  79.5 us
    pallas_call x3, Pallas kernels, feed_back(): pl.pallas_call(feed_back_kernel, grid=(steps,), in_specs=[SMEM, whole(SEQ...  73.8 us
    pallas_call x3, Pallas kernels, attend_backward(): pl.pallas_call(functools.partial(attend_back_kernel, group * GROUP, last)...  64.3 us
    pallas_call x3, Pallas kernels, feed(): pl.pallas_call(functools.partial(feed_kernel, first), grid=(steps,), in_s...  51.1 us
    pallas_call x3, Pallas kernels, attend_forward(): pl.pallas_call(functools.partial(attend_kernel, group * GROUP), grid=(1,)...  44.7 us
    convert_element_type x33, other arithmetic, add_low(): return (left.astype(F32) + right.astype(F32)).astype(BF16)  18.2 us
  transfers between devices with their start and end apart: 97, of which 40 were waited for; matrix products, arithmetic and copies ran while one was open for 10% of the time, Pallas kernels for 15%

profile of v2, /device:TPU:0, one launch (start us, length us, event | category | flops | bytes accessed | tf_op | source)
XLA Modules:
  0.0 565.2 jit_solution(2873623140555378668)
XLA Ops:
  2.6 4.1 collective-permute-start
  8.2 3.0 collective-permute-start.39
  13.4 10.7 %collective-permute-done = bf16[96,768]{1,0:T(8,128)(2,1)S(1)} collective-permute-done((bf16[96,768]{1,0:T(8,128)(2,1)S(1)}, bf16[96,768]{1,0:T(8,128)(2,1)S(1)}, u32[]{:S(2)}, u32[]{:S(2)}) %collective-permute-start) | collective-permute-done | bytes 147488 | tf_op jit(solution)/shard_map/ppermute | solution.py:504
  24.5 2.8 collective-permute-done.30
  27.4 3.0 collective-permute-done.39
  31.2 1.6 collective-permute-done.48
  34.2 4.9 collective-permute-done.1
  40.7 1.6 collective-permute-start.3
  43.2 2.3 collective-permute-done.31
  45.5 1.6 collective-permute-start.5
  47.1 4.7 collective-permute-done.40
  51.8 6.2 %collective-permute-done.49 = bf16[2,96,768]{2,1,0:T(8,128)(2,1)} collective-permute-done((bf16[2,96,768]{2,1,0:T(8,128)(2,1)}, bf16[2,96,768]{2,1,0:T(8,128)(2,1)}, u32[]{:S(2)}, u32[]{:S(2)}) %collective-permute-start.49) | collective-permute-done | bytes 294944 | tf_op jit(solution)/shard_map/ppermute | solution.py:504
  62.1 1.6 collective-permute-start.12
  65.4 2.7 collective-permute-done.12.rest_4_
  68.2 2.3 collective-permute-start.26
  71.4 1.8 collective-permute-start.7
  74.7 1.9 collective-permute-start.14
  82.5 2.1 copy.49
  86.4 2.7 collective-permute-start.21
  96.2 15.0 %attend_forward.3 = (bf16[1024,768]{1,0:T(8,128)(2,1)}, bf16[1024,256]{1,0:T(8,128)(2,1)}, f32[4,1024]{1,0:T(4,128)}) custom-call(s32[8]{0:T(128)} %iota_xor_fusion.place_ref, f32[12]{0:T(128)} %reshape.206.slope_ref, bf16[1024,768]{1,0:T(8,128)(2,1)} %x_ref.7, f32[1,768]{1,0:T(1,128)} %get-tuple-element.311.bias_ref, bf16[96,768]{1,0:T(8,128)(2,1)} %copy-done.23, ...), custom_call_target="tpu_custom_call" | custom-call | flops 12999999488 | bytes 8388608 | tf_op jit(solution)/shard_map/attend_forward/pallas_call | solution.py:119
  115.9 14.8 %attend_forward.4 = (bf16[1024,768]{1,0:T(8,128)(2,1)}, bf16[1024,256]{1,0:T(8,128)(2,1)}, f32[4,1024]{1,0:T(4,128)}) custom-call(s32[8]{0:T(128)} %iota_xor_fusion.place_ref, f32[12]{0:T(128)} %reshape.206.slope_ref, bf16[1024,768]{1,0:T(8,128)(2,1)} %x_ref.7, f32[1,768]{1,0:T(1,128)} %get-tuple-element.310.bias_ref, bf16[96,768]{1,0:T(8,128)(2,1)} %copy-done.24, ...), custom_call_target="tpu_custom_call" | custom-call | flops 12999999488 | bytes 8388608 | tf_op jit(solution)/shard_map/attend_forward/pallas_call | solution.py:119
  132.5 7.6 %collective-permute-done.44.rest_5_.rest_4_ = bf16[4,96,768]{2,1,0:T(8,128)(2,1)S(1)} collective-permute-done((bf16[4,96,768]{2,1,0:T(8,128)(2,1)S(1)}, bf16[4,96,768]{2,1,0:T(8,128)(2,1)S(1)}, u32[]{:S(2)}, u32[]{:S(2)}) %collective-permute-start.44) | collective-permute-done | bytes 589856 | tf_op jit(solution)/shard_map/ppermute | solution.py:504
  141.2 11.2 %collective-permute-done.37.rest_6_ = bf16[4,96,768]{2,1,0:T(8,128)(2,1)S(1)} collective-permute-done((bf16[4,96,768]{2,1,0:T(8,128)(2,1)S(1)}, bf16[4,96,768]{2,1,0:T(8,128)(2,1)S(1)}, u32[]{:S(2)}, u32[]{:S(2)}) %collective-permute-start.37) | collective-permute-done | bytes 589856 | tf_op jit(solution)/shard_map/ppermute | solution.py:504
  152.6 14.9 %attend_forward.5 = (bf16[1024,768]{1,0:T(8,128)(2,1)}, bf16[1024,256]{1,0:T(8,128)(2,1)}, f32[4,1024]{1,0:T(4,128)}) custom-call(s32[8]{0:T(128)} %iota_xor_fusion.place_ref, f32[12]{0:T(128)} %reshape.206.slope_ref, bf16[1024,768]{1,0:T(8,128)(2,1)} %x_ref.7, f32[1,768]{1,0:T(1,128)} %get-tuple-element.309.bias_ref, bf16[96,768]{1,0:T(8,128)(2,1)} %copy-done.25, ...), custom_call_target="tpu_custom_call" | custom-call | flops 12999999488 | bytes 8388608 | tf_op jit(solution)/shard_map/attend_forward/pallas_call | solution.py:119
  167.5 7.7 %join.1 = (f32[1024,768]{1,0:T(8,128)}, f32[1024,128]{1,0:T(8,128)}, bf16[1024,768]{1,0:T(8,128)(2,1)}, bf16[768,1024]{1,0:T(8,128)(2,1)}) custom-call(s32[8]{0:T(128)} %iota_xor_fusion.place_ref, bf16[1024,768]{1,0:T(8,128)(2,1)} %x_ref.7, f32[8,768]{1,0:T(8,128)} %stack.152.vec_ref, bf16[1024,256]{1,0:T(8,128)(2,1)} %get-tuple-element.69.rest_0_, ...), custom_call_target="tpu_custom_call" | custom-call | flops 4000000000 | bytes 10485760 | tf_op jit(solution)/shard_map/join/pallas_call | solution.py:287
  178.7 16.2 %feed.3 = (f32[1024,768]{1,0:T(8,128)}, bf16[1024,1024]{1,0:T(8,128)(2,1)}, bf16[1024,1024]{1,0:T(8,128)(2,1)}, bf16[1024,1024]{1,0:T(8,128)(2,1)}) custom-call(s32[8]{0:T(128)} %iota_xor_fusion.place_ref, bf16[1024,768]{1,0:T(8,128)(2,1)} %get-tuple-element.72.low_ref, bf16[4,96,768]{2,1,0:T(8,128)(2,1)} %copy-done.10, bf16[4,96,768]{2,1,0:T(8,128)(2,1)} %copy-done.39, ...), custom_call_target="tpu_custom_call" | custom-call | flops 10000000000 | bytes 16777216 | tf_op jit(solution)/shard_map/feed/pallas_call | solution.py:432
  195.7 7.9 %collective-permute-done.55.rest_7_.rest_6_ = bf16[4,96,768]{2,1,0:T(8,128)(2,1)S(1)} collective-permute-done((bf16[4,96,768]{2,1,0:T(8,128)(2,1)S(1)}, bf16[4,96,768]{2,1,0:T(8,128)(2,1)S(1)}, u32[]{:S(2)}, u32[]{:S(2)}) %collective-permute-start.55) | collective-permute-done | bytes 589856 | tf_op jit(solution)/shard_map/ppermute | solution.py:504
  204.5 17.4 %feed.4 = (f32[1024,768]{1,0:T(8,128)}, bf16[1024,1024]{1,0:T(8,128)(2,1)}, bf16[1024,1024]{1,0:T(8,128)(2,1)}, bf16[1024,1024]{1,0:T(8,128)(2,1)}) custom-call(s32[8]{0:T(128)} %iota_xor_fusion.place_ref, bf16[1024,768]{1,0:T(8,128)(2,1)} %get-tuple-element.72.low_ref, f32[1024,768]{1,0:T(8,128)} %get-tuple-element.73.rest_0_, ...), custom_call_target="tpu_custom_call" | custom-call | flops 10000000000 | bytes 16777216 | tf_op jit(solution)/shard_map/feed/pallas_call | solution.py:432
  223.4 17.5 %feed.5 = (f32[1024,768]{1,0:T(8,128)}, bf16[1024,1024]{1,0:T(8,128)(2,1)}, bf16[1024,1024]{1,0:T(8,128)(2,1)}, bf16[1024,1024]{1,0:T(8,128)(2,1)}) custom-call(s32[8]{0:T(128)} %iota_xor_fusion.place_ref, bf16[1024,768]{1,0:T(8,128)(2,1)} %get-tuple-element.72.low_ref, f32[1024,768]{1,0:T(8,128)} %get-tuple-element.74.rest_0_, ...), custom_call_target="tpu_custom_call" | custom-call | flops 10000000000 | bytes 16777216 | tf_op jit(solution)/shard_map/feed/pallas_call | solution.py:432
  240.9 9.8 %turn.1 = (bf16[1024,768]{1,0:T(8,128)(2,1)}, f32[1024,768]{1,0:T(8,128)}, bf16[1024,768]{1,0:T(8,128)(2,1)}, bf16[768,1024]{1,0:T(8,128)(2,1)}, f32[3,768]{1,0:T(4,128)}) custom-call(f32[1024,768]{1,0:T(8,128)} %get-tuple-element.75.ffn_ref, f32[1024,768]{1,0:T(8,128)} %get-tuple-element.76.normed1_ref.normed_ref, bf16[1024,768]{1,0:T(8,128)(2,1)} %cot_ref.1, ...), custom_call_target="tpu_custom_call" | custom-call | flops 4000000000 | bytes 16777216 | tf_op jit(solution)/shard_map/turn/pallas_call | solution.py:323
  250.7 24.4 %feed_back.3 = (f32[1024,768]{1,0:T(8,128)}, bf16[4,4,96,768]{3,2,1,0:T(8,128)(2,1)}, bf16[4,4,96,768]{3,2,1,0:T(8,128)(2,1)}) custom-call(s32[8]{0:T(128)} %iota_xor_fusion.place_ref, bf16[1024,768]{1,0:T(8,128)(2,1)} %get-tuple-element.80.d_ref, bf16[768,1024]{1,0:T(8,128)(2,1)} %get-tuple-element.81.d_t_ref, ...), custom_call_target="tpu_custom_call" | custom-call | flops 12000000000 | bytes 31457280 | tf_op jit(solution)/shard_map/feed_back/pallas_call | solution.py:481
  275.1 24.6 %feed_back.4 = (f32[1024,768]{1,0:T(8,128)}, bf16[4,4,96,768]{3,2,1,0:T(8,128)(2,1)}, bf16[4,4,96,768]{3,2,1,0:T(8,128)(2,1)}) custom-call(s32[8]{0:T(128)} %iota_xor_fusion.place_ref, bf16[1024,768]{1,0:T(8,128)(2,1)} %get-tuple-element.80.d_ref, bf16[768,1024]{1,0:T(8,128)(2,1)} %get-tuple-element.81.d_t_ref, ...), custom_call_target="tpu_custom_call" | custom-call | flops 12000000000 | bytes 31457280 | tf_op jit(solution)/shard_map/feed_back/pallas_call | solution.py:481
  299.7 24.8 %feed_back.5 = (f32[1024,768]{1,0:T(8,128)}, bf16[4,4,96,768]{3,2,1,0:T(8,128)(2,1)}, bf16[4,4,96,768]{3,2,1,0:T(8,128)(2,1)}) custom-call(s32[8]{0:T(128)} %iota_xor_fusion.place_ref, bf16[1024,768]{1,0:T(8,128)(2,1)} %get-tuple-element.80.d_ref, bf16[768,1024]{1,0:T(8,128)(2,1)} %get-tuple-element.81.d_t_ref, ...), custom_call_target="tpu_custom_call" | custom-call | flops 12000000000 | bytes 31457280 | tf_op jit(solution)/shard_map/feed_back/pallas_call | solution.py:481
  324.5 8.8 %rejoin.1 = (f32[1024,768]{1,0:T(8,128)}, bf16[1024,768]{1,0:T(8,128)(2,1)}, bf16[4,96,768]{2,1,0:T(8,128)(2,1)}, bf16[4,96,768]{2,1,0:T(8,128)(2,1)}, f32[3,768]{1,0:T(4,128)}) custom-call(s32[8]{0:T(128)} %iota_xor_fusion.place_ref, f32[1024,768]{1,0:T(8,128)} %get-tuple-element.95.d_hidden_ref, f32[1024,768]{1,0:T(8,128)} %get-tuple-element.76.normed1_ref.normed_ref, ...), custom_call_target="tpu_custom_call" | custom-call | flops 6000000000 | bytes 14680064 | tf_op jit(solution)/shard_map/rejoin/pallas_call | solution.py:365
  333.3 21.1 %attend_backward.3 = (bf16[4,96,768]{2,1,0:T(8,128)(2,1)}, bf16[4,96,768]{2,1,0:T(8,128)(2,1)}, f32[2,256]{1,0:T(2,128)}, f32[1024,768]{1,0:T(8,128)}) custom-call(s32[8]{0:T(128)} %iota_xor_fusion.place_ref, f32[12]{0:T(128)} %reshape.206.slope_ref, bf16[1024,768]{1,0:T(8,128)(2,1)} %get-tuple-element.100.qkv_ref, f32[4,1024]{1,0:T(4,128)} %get-tuple-element.101.lse_ref, ...), custom_call_target="tpu_custom_call" | custom-call | flops 19000000512 | bytes 8388608 | tf_op jit(solution)/shard_map/attend_backward/pallas_call | solution.py:203
  354.5 21.2 %attend_backward.4 = (bf16[4,96,768]{2,1,0:T(8,128)(2,1)}, bf16[4,96,768]{2,1,0:T(8,128)(2,1)}, f32[2,256]{1,0:T(2,128)}, f32[1024,768]{1,0:T(8,128)}) custom-call(s32[8]{0:T(128)} %iota_xor_fusion.place_ref, f32[12]{0:T(128)} %reshape.206.slope_ref, bf16[1024,768]{1,0:T(8,128)(2,1)} %get-tuple-element.98.qkv_ref, f32[4,1024]{1,0:T(4,128)} %get-tuple-element.99.lse_ref, ...), custom_call_target="tpu_custom_call" | custom-call | flops 19000000512 | bytes 8388608 | tf_op jit(solution)/shard_map/attend_backward/pallas_call | solution.py:203
  375.8 21.9 %attend_backward.5 = (bf16[4,96,768]{2,1,0:T(8,128)(2,1)}, bf16[4,96,768]{2,1,0:T(8,128)(2,1)}, f32[2,256]{1,0:T(2,128)}, bf16[1024,768]{1,0:T(8,128)(2,1)}) custom-call(s32[8]{0:T(128)} %iota_xor_fusion.place_ref, f32[12]{0:T(128)} %reshape.206.slope_ref, bf16[1024,768]{1,0:T(8,128)(2,1)} %get-tuple-element.78.qkv_ref, ...), custom_call_target="tpu_custom_call" | custom-call | flops 19000000512 | bytes 8388608 | tf_op jit(solution)/shard_map/attend_backward/pallas_call | solution.py:203
  403.2 2.6 collective-permute-done.73
  407.0 2.6 collective-permute-done.74
  409.8 3.7 collective-permute-done.75
  413.5 2.0 collective-permute-start.76
  424.4 6.8 %collective-permute-done.68 = bf16[2,96,768]{2,1,0:T(8,128)(2,1)S(1)} collective-permute-done((bf16[2,96,768]{2,1,0:T(8,128)(2,1)S(1)}, bf16[2,96,768]{2,1,0:T(8,128)(2,1)S(1)}, u32[]{:S(2)}, u32[]{:S(2)}) %collective-permute-start.68) | collective-permute-done | bytes 294944 | tf_op jit(solution)/shard_map/ppermute | solution.py:504
  433.5 7.7 %collective-permute-done.58 = bf16[2,96,768]{2,1,0:T(8,128)(2,1)S(1)} collective-permute-done((bf16[2,96,768]{2,1,0:T(8,128)(2,1)S(1)}, bf16[2,96,768]{2,1,0:T(8,128)(2,1)S(1)}, u32[]{:S(2)}, u32[]{:S(2)}) %collective-permute-start.58) | collective-permute-done | bytes 294944 | tf_op jit(solution)/shard_map/ppermute | solution.py:504
  442.3 3.9 collective-permute-done.78
  448.5 2.9 collective-permute-done.64
  455.0 1.6 collective-permute-done.79
  463.0 2.7 collective-permute-start.71
  466.2 1.6 collective-permute-start.66
  468.1 2.5 collective-permute-start.61
  471.2 1.6 collective-permute-start.81
  476.5 1.8 add_convert_fusion.3
  486.0 1.7 add_convert_fusion.1
  488.2 16.5 %collective-permute-done.93 = bf16[2,4,96,768]{3,2,1,0:T(8,128)(2,1)} collective-permute-done((bf16[2,4,96,768]{3,2,1,0:T(8,128)(2,1)}, bf16[2,4,96,768]{3,2,1,0:T(8,128)(2,1)}, u32[]{:S(2)}, u32[]{:S(2)}) %collective-permute-start.93) | collective-permute-done | bytes 1179680 | tf_op jit(solution)/shard_map/ppermute | solution.py:504
  504.7 2.0 fusion.8
  507.8 2.1 fusion.6
  510.9 19.0 %collective-permute-done.83 = bf16[2,4,96,768]{3,2,1,0:T(8,128)(2,1)} collective-permute-done((bf16[2,4,96,768]{3,2,1,0:T(8,128)(2,1)}, bf16[2,4,96,768]{3,2,1,0:T(8,128)(2,1)}, u32[]{:S(2)}, u32[]{:S(2)}) %collective-permute-start.83) | collective-permute-done | bytes 1179680 | tf_op jit(solution)/shard_map/ppermute | solution.py:504
  529.9 2.1 fusion.4
  533.8 1.8 copy.57
  537.1 2.0 collective-permute-start.95
  543.6 2.0 collective-permute-start.85
  547.5 5.4 collective-permute-done.90
  553.1 3.0 collective-permute-done.85
  556.4 3.2 collective-permute-done.91
  559.6 3.2 collective-permute-done.86
  (450 shorter events, 106.3 us)
Async XLA Ops:
  2.6 21.4 %collective-permute-start = (bf16[96,768]{1,0:T(8,128)(2,1)S(1)}, bf16[96,768]{1,0:T(8,128)(2,1)S(1)}, u32[]{:S(2)}, u32[]{:S(2)}) collective-permute-start(bf16[96,768]{1,0:T(8,128)(2,1)S(1)} %concatenate.130), channel_id=1, source_target_pairs={{0,2},{1,3},{2,0},{3,1},{4,6},{5,7},{6,4},{7,5},{8,10},{9,11},{10,... | collective-permute-start | bytes 442376 | tf_op jit(solution)/shard_map/ppermute | solution.py:504
  8.1 19.2 %collective-permute-start.30 = (bf16[96,768]{1,0:T(8,128)(2,1)S(1)}, bf16[96,768]{1,0:T(8,128)(2,1)S(1)}, u32[]{:S(2)}, u32[]{:S(2)}) collective-permute-start(bf16[96,768]{1,0:T(8,128)(2,1)S(1)} %get-tuple-element.260), channel_id=1, source_target_pairs={{0,2},{1,3},{2,0},{3,1},{4,6},{5,7},{6,4},{7,5},{8,10},{9,11},{10,... | collective-permute-start | bytes 442376 | tf_op jit(solution)/shard_map/ppermute | solution.py:504
  8.2 22.2 %collective-permute-start.39 = (bf16[96,768]{1,0:T(8,128)(2,1)S(1)}, bf16[96,768]{1,0:T(8,128)(2,1)S(1)}, u32[]{:S(2)}, u32[]{:S(2)}) collective-permute-start(bf16[96,768]{1,0:T(8,128)(2,1)S(1)} %get-tuple-element.258), channel_id=1, source_target_pairs={{0,2},{1,3},{2,0},{3,1},{4,6},{5,7},{6,4},{7,5},{8,10},{9,11},{10,... | collective-permute-start | bytes 442376 | tf_op jit(solution)/shard_map/ppermute | solution.py:504
  11.2 21.5 %collective-permute-start.48 = (bf16[96,768]{1,0:T(8,128)(2,1)S(1)}, bf16[96,768]{1,0:T(8,128)(2,1)S(1)}, u32[]{:S(2)}, u32[]{:S(2)}) collective-permute-start(bf16[96,768]{1,0:T(8,128)(2,1)S(1)} %get-tuple-element.253), channel_id=1, source_target_pairs={{0,2},{1,3},{2,0},{3,1},{4,6},{5,7},{6,4},{7,5},{8,10},{9,11},{10,... | collective-permute-start | bytes 442376 | tf_op jit(solution)/shard_map/ppermute | solution.py:504
  24.4 14.7 %collective-permute-start.1 = (bf16[96,1536]{1,0:T(8,128)(2,1)S(1)}, bf16[96,1536]{1,0:T(8,128)(2,1)S(1)}, u32[]{:S(2)}, u32[]{:S(2)}) collective-permute-start(bf16[96,1536]{1,0:T(8,128)(2,1)S(1)} %concatenate.131), channel_id=1, source_target_pairs={{0,1},{1,0},{2,3},{3,2},{4,5},{5,4},{6,7},{7,6},{8,9},{9,8},{10,11... | collective-permute-start | bytes 884744 | tf_op jit(solution)/shard_map/ppermute | solution.py:504
  27.3 18.2 %collective-permute-start.31 = (bf16[2,96,768]{2,1,0:T(8,128)(2,1)S(1)}, bf16[2,96,768]{2,1,0:T(8,128)(2,1)}, u32[]{:S(2)}, u32[]{:S(2)}) collective-permute-start(bf16[2,96,768]{2,1,0:T(8,128)(2,1)S(1)} %pad_maximum_fusion.4), channel_id=1, source_target_pairs={{0,1},{1,0},{2,3},{3,2},{4,5},{5,4},{6,7},{7,6},{8,9},{9,8},{10,11... | collective-permute-start | bytes 884744 | tf_op jit(solution)/shard_map/ppermute | solution.py:504
  31.2 20.6 %collective-permute-start.40 = (bf16[2,96,768]{2,1,0:T(8,128)(2,1)}, bf16[2,96,768]{2,1,0:T(8,128)(2,1)}, u32[]{:S(2)}, u32[]{:S(2)}) collective-permute-start(bf16[2,96,768]{2,1,0:T(8,128)(2,1)} %pad_maximum_fusion.5), channel_id=1, source_target_pairs={{0,1},{1,0},{2,3},{3,2},{4,5},{5,4},{6,7},{7,6},{8,9},{9,8},{10,11... | collective-permute-start | bytes 884744 | tf_op jit(solution)/shard_map/ppermute | solution.py:504
  33.5 24.5 %collective-permute-start.49 = (bf16[2,96,768]{2,1,0:T(8,128)(2,1)}, bf16[2,96,768]{2,1,0:T(8,128)(2,1)}, u32[]{:S(2)}, u32[]{:S(2)}) collective-permute-start(bf16[2,96,768]{2,1,0:T(8,128)(2,1)} %pad_maximum_fusion.6), channel_id=1, source_target_pairs={{0,1},{1,0},{2,3},{3,2},{4,5},{5,4},{6,7},{7,6},{8,9},{9,8},{10,11... | collective-permute-start | bytes 884744 | tf_op jit(solution)/shard_map/ppermute | solution.py:504
  40.6 21.5 %collective-permute-start.2 = (bf16[96,768]{1,0:T(8,128)(2,1)S(1)}, bf16[96,768]{1,0:T(8,128)(2,1)}, u32[]{:S(2)}, u32[]{:S(2)}) collective-permute-start(bf16[96,768]{1,0:T(8,128)(2,1)S(1)} %concatenate.132.rest_0_), channel_id=1, source_target_pairs={{0,4},{4,0},{8,12},{12,8},{16,20},{20,16},{24,28},{28,24},{1,5},{5... | collective-permute-start | bytes 442376 | tf_op jit(solution)/shard_map/ppermute | solution.py:504
  40.7 23.0 %collective-permute-start.3 = (bf16[96,768]{1,0:T(8,128)(2,1)S(1)}, bf16[96,768]{1,0:T(8,128)(2,1)}, u32[]{:S(2)}, u32[]{:S(2)}) collective-permute-start(bf16[96,768]{1,0:T(8,128)(2,1)S(1)} %concatenate.132.rest_0_), channel_id=1, source_target_pairs={{0,8},{4,12},{8,0},{12,4},{16,24},{20,28},{24,16},{28,20},{1,9},{5... | collective-permute-start | bytes 442376 | tf_op jit(solution)/shard_map/ppermute | solution.py:504
  45.5 18.2 %collective-permute-start.5 = (bf16[96,768]{1,0:T(8,128)(2,1)S(1)}, bf16[96,768]{1,0:T(8,128)(2,1)S(1)}, u32[]{:S(2)}, u32[]{:S(2)}) collective-permute-start(bf16[96,768]{1,0:T(8,128)(2,1)S(1)} %concatenate.132.rest_0_), channel_id=1, source_target_pairs={{0,16},{4,20},{8,24},{12,28},{16,0},{20,4},{24,8},{28,12},{1,17},{... | collective-permute-start | bytes 442376 | tf_op jit(solution)/shard_map/ppermute | solution.py:504
  51.8 12.5 %collective-permute-start.9 = (bf16[96,768]{1,0:T(8,128)(2,1)S(1)}, bf16[96,768]{1,0:T(8,128)(2,1)S(1)}, u32[]{:S(2)}, u32[]{:S(2)}) collective-permute-start(bf16[96,768]{1,0:T(8,128)(2,1)S(1)} %concatenate.133.rest_0_), channel_id=1, source_target_pairs={{0,4},{4,0},{8,12},{12,8},{16,20},{20,16},{24,28},{28,24},{1,5},{5... | collective-permute-start | bytes 442376 | tf_op jit(solution)/shard_map/ppermute | solution.py:504
  74.5 14.6 %collective-permute-start.13 = (bf16[96,768]{1,0:T(8,128)(2,1)}, bf16[96,768]{1,0:T(8,128)(2,1)}, u32[]{:S(2)}, u32[]{:S(2)}) collective-permute-start(bf16[96,768]{1,0:T(8,128)(2,1)} %copy-done.67), channel_id=1, source_target_pairs={{0,4},{4,0},{8,12},{12,8},{16,20},{20,16},{24,28},{28,24},{1,5},{5... | collective-permute-start | bytes 442376 | tf_op jit(solution)/shard_map/ppermute | solution.py:504
  74.7 14.5 %collective-permute-start.14 = (bf16[96,768]{1,0:T(8,128)(2,1)}, bf16[96,768]{1,0:T(8,128)(2,1)}, u32[]{:S(2)}, u32[]{:S(2)}) collective-permute-start(bf16[96,768]{1,0:T(8,128)(2,1)} %copy-done.67), channel_id=1, source_target_pairs={{0,8},{4,12},{8,0},{12,4},{16,24},{20,28},{24,16},{28,20},{1,9},{5... | collective-permute-start | bytes 442376 | tf_op jit(solution)/shard_map/ppermute | solution.py:504
  76.7 9.7 %collective-permute-start.11 = (bf16[96,768]{1,0:T(8,128)(2,1)}, bf16[96,768]{1,0:T(8,128)(2,1)}, u32[]{:S(2)}, u32[]{:S(2)}) collective-permute-start(bf16[96,768]{1,0:T(8,128)(2,1)} %collective-permute-done.10.rest_2_), channel_id=1, source_target_pairs={{0,4},{4,0},{8,12},{12,8},{16,20},{20,16},{24,28},{28,24},{1,5},{5... | collective-permute-start | bytes 442376 | tf_op jit(solution)/shard_map/ppermute | solution.py:504
  76.7 13.6 %collective-permute-start.18 = (bf16[96,768]{1,0:T(8,128)(2,1)}, bf16[96,768]{1,0:T(8,128)(2,1)}, u32[]{:S(2)}, u32[]{:S(2)}) collective-permute-start(bf16[96,768]{1,0:T(8,128)(2,1)} %copy-done.65), channel_id=1, source_target_pairs={{0,4},{4,0},{8,12},{12,8},{16,20},{20,16},{24,28},{28,24},{1,5},{5... | collective-permute-start | bytes 442376 | tf_op jit(solution)/shard_map/ppermute | solution.py:504
  77.2 13.1 %collective-permute-start.20 = (bf16[96,768]{1,0:T(8,128)(2,1)}, bf16[96,768]{1,0:T(8,128)(2,1)}, u32[]{:S(2)}, u32[]{:S(2)}) collective-permute-start(bf16[96,768]{1,0:T(8,128)(2,1)} %copy-done.68), channel_id=1, source_target_pairs={{0,4},{4,0},{8,12},{12,8},{16,20},{20,16},{24,28},{28,24},{1,5},{5... | collective-permute-start | bytes 442376 | tf_op jit(solution)/shard_map/ppermute | solution.py:504
  93.5 20.3 %collective-permute-start.32 = (bf16[4,96,768]{2,1,0:T(8,128)(2,1)S(1)}, bf16[4,96,768]{2,1,0:T(8,128)(2,1)S(1)}, u32[]{:S(2)}, u32[]{:S(2)}) collective-permute-start(bf16[4,96,768]{2,1,0:T(8,128)(2,1)S(1)} %pad_maximum_fusion.rest_0_), channel_id=1, source_target_pairs={{0,4},{4,0},{8,12},{12,8},{16,20},{20,16},{24,28},{28,24},{1,5},{5... | collective-permute-start | bytes 1769480 | tf_op jit(solution)/shard_map/ppermute | solution.py:504
  93.5 21.2 %collective-permute-start.33 = (bf16[4,96,768]{2,1,0:T(8,128)(2,1)S(1)}, bf16[4,96,768]{2,1,0:T(8,128)(2,1)S(1)}, u32[]{:S(2)}, u32[]{:S(2)}) collective-permute-start(bf16[4,96,768]{2,1,0:T(8,128)(2,1)S(1)} %pad_maximum_fusion.rest_0_), channel_id=1, source_target_pairs={{0,8},{4,12},{8,0},{12,4},{16,24},{20,28},{24,16},{28,20},{1,9},{5... | collective-permute-start | bytes 1769480 | tf_op jit(solution)/shard_map/ppermute | solution.py:504
  94.7 16.6 %collective-permute-start.15 = (bf16[96,768]{1,0:T(8,128)(2,1)}, bf16[96,768]{1,0:T(8,128)(2,1)S(1)}, u32[]{:S(2)}, u32[]{:S(2)}) collective-permute-start(bf16[96,768]{1,0:T(8,128)(2,1)} %collective-permute-done.14.rest_6_), channel_id=1, source_target_pairs={{0,4},{4,0},{8,12},{12,8},{16,20},{20,16},{24,28},{28,24},{1,5},{5... | collective-permute-start | bytes 442376 | tf_op jit(solution)/shard_map/ppermute | solution.py:504
  95.5 17.2 %collective-permute-start.22 = (bf16[96,768]{1,0:T(8,128)(2,1)S(1)}, bf16[96,768]{1,0:T(8,128)(2,1)S(1)}, u32[]{:S(2)}, u32[]{:S(2)}) collective-permute-start(bf16[96,768]{1,0:T(8,128)(2,1)S(1)} %collective-permute-done.21.rest_6_), channel_id=1, source_target_pairs={{0,4},{4,0},{8,12},{12,8},{16,20},{20,16},{24,28},{28,24},{1,5},{5... | collective-permute-start | bytes 442376 | tf_op jit(solution)/shard_map/ppermute | solution.py:504
  95.5 17.2 %collective-permute-start.29 = (bf16[96,768]{1,0:T(8,128)(2,1)S(1)}, bf16[96,768]{1,0:T(8,128)(2,1)S(1)}, u32[]{:S(2)}, u32[]{:S(2)}) collective-permute-start(bf16[96,768]{1,0:T(8,128)(2,1)S(1)} %collective-permute-done.28.rest_9_), channel_id=1, source_target_pairs={{0,4},{4,0},{8,12},{12,8},{16,20},{20,16},{24,28},{28,24},{1,5},{5... | collective-permute-start | bytes 442376 | tf_op jit(solution)/shard_map/ppermute | solution.py:504
  111.3 19.4 %collective-permute-start.35 = (bf16[4,96,768]{2,1,0:T(8,128)(2,1)S(1)}, bf16[4,96,768]{2,1,0:T(8,128)(2,1)S(1)}, u32[]{:S(2)}, u32[]{:S(2)}) collective-permute-start(bf16[4,96,768]{2,1,0:T(8,128)(2,1)S(1)} %pad_maximum_fusion.rest_0_), channel_id=1, source_target_pairs={{0,16},{4,20},{8,24},{12,28},{16,0},{20,4},{24,8},{28,12},{1,17},{... | collective-permute-start | bytes 1769480 | tf_op jit(solution)/shard_map/ppermute | solution.py:504
  112.8 19.2 %collective-permute-start.41 = (bf16[4,96,768]{2,1,0:T(8,128)(2,1)S(1)}, bf16[4,96,768]{2,1,0:T(8,128)(2,1)S(1)}, u32[]{:S(2)}, u32[]{:S(2)}) collective-permute-start(bf16[4,96,768]{2,1,0:T(8,128)(2,1)S(1)} %pad_maximum_fusion.1.rest_1_.rest_0_), channel_id=1, source_target_pairs={{0,4},{4,0},{8,12},{12,8},{16,20},{20,16},{24,28},{28,24},{1,5},{5... | collective-permute-start | bytes 1769480 | tf_op jit(solution)/shard_map/ppermute | solution.py:504
  112.8 19.2 %collective-permute-start.42 = (bf16[4,96,768]{2,1,0:T(8,128)(2,1)S(1)}, bf16[4,96,768]{2,1,0:T(8,128)(2,1)S(1)}, u32[]{:S(2)}, u32[]{:S(2)}) collective-permute-start(bf16[4,96,768]{2,1,0:T(8,128)(2,1)S(1)} %pad_maximum_fusion.1.rest_1_.rest_0_), channel_id=1, source_target_pairs={{0,8},{4,12},{8,0},{12,4},{16,24},{20,28},{24,16},{28,20},{1,9},{5... | collective-permute-start | bytes 1769480 | tf_op jit(solution)/shard_map/ppermute | solution.py:504
  113.8 26.4 %collective-permute-start.44 = (bf16[4,96,768]{2,1,0:T(8,128)(2,1)S(1)}, bf16[4,96,768]{2,1,0:T(8,128)(2,1)S(1)}, u32[]{:S(2)}, u32[]{:S(2)}) collective-permute-start(bf16[4,96,768]{2,1,0:T(8,128)(2,1)S(1)} %pad_maximum_fusion.1.rest_1_.rest_0_), channel_id=1, source_target_pairs={{0,16},{4,20},{8,24},{12,28},{16,0},{20,4},{24,8},{28,12},{1,17},{... | collective-permute-start | bytes 1769480 | tf_op jit(solution)/shard_map/ppermute | solution.py:504
  114.7 37.6 %collective-permute-start.37 = (bf16[4,96,768]{2,1,0:T(8,128)(2,1)S(1)}, bf16[4,96,768]{2,1,0:T(8,128)(2,1)S(1)}, u32[]{:S(2)}, u32[]{:S(2)}) collective-permute-start(bf16[4,96,768]{2,1,0:T(8,128)(2,1)S(1)} %collective-permute-done.33.rest_2_), channel_id=1, source_target_pairs={{0,16},{4,20},{8,24},{12,28},{16,0},{20,4},{24,8},{28,12},{1,17},{... | collective-permute-start | bytes 1769480 | tf_op jit(solution)/shard_map/ppermute | solution.py:504
  130.8 44.4 %collective-permute-start.51 = (bf16[4,96,768]{2,1,0:T(8,128)(2,1)S(1)}, bf16[4,96,768]{2,1,0:T(8,128)(2,1)S(1)}, u32[]{:S(2)}, u32[]{:S(2)}) collective-permute-start(bf16[4,96,768]{2,1,0:T(8,128)(2,1)S(1)} %pad_maximum_fusion.2.rest_1_.rest_0_), channel_id=1, source_target_pairs={{0,8},{4,12},{8,0},{12,4},{16,24},{20,28},{24,16},{28,20},{1,9},{5... | collective-permute-start | bytes 1769480 | tf_op jit(solution)/shard_map/ppermute | solution.py:504
  131.9 44.4 %collective-permute-start.34 = (bf16[4,96,768]{2,1,0:T(8,128)(2,1)S(1)}, bf16[4,96,768]{2,1,0:T(8,128)(2,1)S(1)}, u32[]{:S(2)}, u32[]{:S(2)}) collective-permute-start(bf16[4,96,768]{2,1,0:T(8,128)(2,1)S(1)} %collective-permute-done.33.rest_2_), channel_id=1, source_target_pairs={{0,4},{4,0},{8,12},{12,8},{16,20},{20,16},{24,28},{28,24},{1,5},{5... | collective-permute-start | bytes 1769480 | tf_op jit(solution)/shard_map/ppermute | solution.py:504
  132.0 44.6 %collective-permute-start.36 = (bf16[4,96,768]{2,1,0:T(8,128)(2,1)S(1)}, bf16[4,96,768]{2,1,0:T(8,128)(2,1)S(1)}, u32[]{:S(2)}, u32[]{:S(2)}) collective-permute-start(bf16[4,96,768]{2,1,0:T(8,128)(2,1)S(1)} %collective-permute-done.35.rest_4_), channel_id=1, source_target_pairs={{0,4},{4,0},{8,12},{12,8},{16,20},{20,16},{24,28},{28,24},{1,5},{5... | collective-permute-start | bytes 1769480 | tf_op jit(solution)/shard_map/ppermute | solution.py:504
  140.1 36.8 %collective-permute-start.46 = (bf16[4,96,768]{2,1,0:T(8,128)(2,1)S(1)}, bf16[4,96,768]{2,1,0:T(8,128)(2,1)S(1)}, u32[]{:S(2)}, u32[]{:S(2)}) collective-permute-start(bf16[4,96,768]{2,1,0:T(8,128)(2,1)S(1)} %collective-permute-done.44.rest_5_.rest_4_), channel_id=1, source_target_pairs={{0,8},{4,12},{8,0},{12,4},{16,24},{20,28},{24,16},{28,20},{1,9},{5... | collective-permute-start | bytes 1769480 | tf_op jit(solution)/shard_map/ppermute | solution.py:504
  152.4 25.6 %collective-permute-start.38 = (bf16[4,96,768]{2,1,0:T(8,128)(2,1)S(1)}, bf16[4,96,768]{2,1,0:T(8,128)(2,1)S(1)}, u32[]{:S(2)}, u32[]{:S(2)}) collective-permute-start(bf16[4,96,768]{2,1,0:T(8,128)(2,1)S(1)} %collective-permute-done.37.rest_6_), channel_id=1, source_target_pairs={{0,4},{4,0},{8,12},{12,8},{16,20},{20,16},{24,28},{28,24},{1,5},{5... | collective-permute-start | bytes 1769480 | tf_op jit(solution)/shard_map/ppermute | solution.py:504
  175.2 19.8 %collective-permute-start.53 = (bf16[4,96,768]{2,1,0:T(8,128)(2,1)S(1)}, bf16[4,96,768]{2,1,0:T(8,128)(2,1)S(1)}, u32[]{:S(2)}, u32[]{:S(2)}) collective-permute-start(bf16[4,96,768]{2,1,0:T(8,128)(2,1)S(1)} %pad_maximum_fusion.2.rest_1_.rest_0_), channel_id=1, source_target_pairs={{0,16},{4,20},{8,24},{12,28},{16,0},{20,4},{24,8},{28,12},{1,17},{... | collective-permute-start | bytes 1769480 | tf_op jit(solution)/shard_map/ppermute | solution.py:504
  176.3 19.3 %collective-permute-start.45 = (bf16[4,96,768]{2,1,0:T(8,128)(2,1)S(1)}, bf16[4,96,768]{2,1,0:T(8,128)(2,1)S(1)}, u32[]{:S(2)}, u32[]{:S(2)}) collective-permute-start(bf16[4,96,768]{2,1,0:T(8,128)(2,1)S(1)} %collective-permute-done.44.rest_5_.rest_4_), channel_id=1, source_target_pairs={{0,4},{4,0},{8,12},{12,8},{16,20},{20,16},{24,28},{28,24},{1,5},{5... | collective-permute-start | bytes 1769480 | tf_op jit(solution)/shard_map/ppermute | solution.py:504
  176.6 18.5 %collective-permute-start.43 = (bf16[4,96,768]{2,1,0:T(8,128)(2,1)S(1)}, bf16[4,96,768]{2,1,0:T(8,128)(2,1)S(1)}, u32[]{:S(2)}, u32[]{:S(2)}) collective-permute-start(bf16[4,96,768]{2,1,0:T(8,128)(2,1)S(1)} %collective-permute-done.42.rest_3_.rest_2_), channel_id=1, source_target_pairs={{0,4},{4,0},{8,12},{12,8},{16,20},{20,16},{24,28},{28,24},{1,5},{5... | collective-permute-start | bytes 1769480 | tf_op jit(solution)/shard_map/ppermute | solution.py:504
  177.0 26.6 %collective-permute-start.55 = (bf16[4,96,768]{2,1,0:T(8,128)(2,1)S(1)}, bf16[4,96,768]{2,1,0:T(8,128)(2,1)S(1)}, u32[]{:S(2)}, u32[]{:S(2)}) collective-permute-start(bf16[4,96,768]{2,1,0:T(8,128)(2,1)S(1)} %collective-permute-done.51.rest_3_.rest_2_), channel_id=1, source_target_pairs={{0,16},{4,20},{8,24},{12,28},{16,0},{20,4},{24,8},{28,12},{1,17},{... | collective-permute-start | bytes 1769480 | tf_op jit(solution)/shard_map/ppermute | solution.py:504
  177.9 25.7 %collective-permute-start.47 = (bf16[4,96,768]{2,1,0:T(8,128)(2,1)S(1)}, bf16[4,96,768]{2,1,0:T(8,128)(2,1)S(1)}, u32[]{:S(2)}, u32[]{:S(2)}) collective-permute-start(bf16[4,96,768]{2,1,0:T(8,128)(2,1)S(1)} %collective-permute-done.46.rest_7_.rest_6_), channel_id=1, source_target_pairs={{0,4},{4,0},{8,12},{12,8},{16,20},{20,16},{24,28},{28,24},{1,5},{5... | collective-permute-start | bytes 1769480 | tf_op jit(solution)/shard_map/ppermute | solution.py:504
  195.0 27.0 %collective-permute-start.50 = (bf16[4,96,768]{2,1,0:T(8,128)(2,1)S(1)}, bf16[4,96,768]{2,1,0:T(8,128)(2,1)S(1)}, u32[]{:S(2)}, u32[]{:S(2)}) collective-permute-start(bf16[4,96,768]{2,1,0:T(8,128)(2,1)S(1)} %pad_maximum_fusion.2.rest_1_.rest_0_), channel_id=1, source_target_pairs={{0,4},{4,0},{8,12},{12,8},{16,20},{20,16},{24,28},{28,24},{1,5},{5... | collective-permute-start | bytes 1769480 | tf_op jit(solution)/shard_map/ppermute | solution.py:504
  195.1 26.9 %collective-permute-start.52 = (bf16[4,96,768]{2,1,0:T(8,128)(2,1)S(1)}, bf16[4,96,768]{2,1,0:T(8,128)(2,1)S(1)}, u32[]{:S(2)}, u32[]{:S(2)}) collective-permute-start(bf16[4,96,768]{2,1,0:T(8,128)(2,1)S(1)} %collective-permute-done.51.rest_3_.rest_2_), channel_id=1, source_target_pairs={{0,4},{4,0},{8,12},{12,8},{16,20},{20,16},{24,28},{28,24},{1,5},{5... | collective-permute-start | bytes 1769480 | tf_op jit(solution)/shard_map/ppermute | solution.py:504
  195.6 26.3 %collective-permute-start.54 = (bf16[4,96,768]{2,1,0:T(8,128)(2,1)S(1)}, bf16[4,96,768]{2,1,0:T(8,128)(2,1)S(1)}, u32[]{:S(2)}, u32[]{:S(2)}) collective-permute-start(bf16[4,96,768]{2,1,0:T(8,128)(2,1)S(1)} %collective-permute-done.53.rest_5_.rest_4_), channel_id=1, source_target_pairs={{0,4},{4,0},{8,12},{12,8},{16,20},{20,16},{24,28},{28,24},{1,5},{5... | collective-permute-start | bytes 1769480 | tf_op jit(solution)/shard_map/ppermute | solution.py:504
  203.6 18.4 %collective-permute-start.56 = (bf16[4,96,768]{2,1,0:T(8,128)(2,1)S(1)}, bf16[4,96,768]{2,1,0:T(8,128)(2,1)S(1)}, u32[]{:S(2)}, u32[]{:S(2)}) collective-permute-start(bf16[4,96,768]{2,1,0:T(8,128)(2,1)S(1)} %collective-permute-done.55.rest_7_.rest_6_), channel_id=1, source_target_pairs={{0,4},{4,0},{8,12},{12,8},{16,20},{20,16},{24,28},{28,24},{1,5},{5... | collective-permute-start | bytes 1769480 | tf_op jit(solution)/shard_map/ppermute | solution.py:504
  401.3 18.2 %collective-permute-start.67 = (bf16[4,96,768]{2,1,0:T(8,128)(2,1)}, bf16[4,96,768]{2,1,0:T(8,128)(2,1)S(1)}, u32[]{:S(2)}, u32[]{:S(2)}) collective-permute-start(bf16[4,96,768]{2,1,0:T(8,128)(2,1)} %get-tuple-element.111), channel_id=1, source_target_pairs={{0,4},{4,0},{8,12},{12,8},{16,20},{20,16},{24,28},{28,24},{1,5},{5... | collective-permute-start | bytes 1769480 | tf_op jit(solution)/shard_map/ppermute | solution.py:504
  401.4 20.4 %collective-permute-start.62 = (bf16[4,96,768]{2,1,0:T(8,128)(2,1)S(1)}, bf16[4,96,768]{2,1,0:T(8,128)(2,1)S(1)}, u32[]{:S(2)}, u32[]{:S(2)}) collective-permute-start(bf16[4,96,768]{2,1,0:T(8,128)(2,1)S(1)} %copy-done.41), channel_id=1, source_target_pairs={{0,4},{4,0},{8,12},{12,8},{16,20},{20,16},{24,28},{28,24},{1,5},{5... | collective-permute-start | bytes 1769480 | tf_op jit(solution)/shard_map/ppermute | solution.py:504
  403.1 17.1 %collective-permute-start.57 = (bf16[4,96,768]{2,1,0:T(8,128)(2,1)S(1)}, bf16[4,96,768]{2,1,0:T(8,128)(2,1)S(1)}, u32[]{:S(2)}, u32[]{:S(2)}) collective-permute-start(bf16[4,96,768]{2,1,0:T(8,128)(2,1)S(1)} %copy-done.42), channel_id=1, source_target_pairs={{0,4},{4,0},{8,12},{12,8},{16,20},{20,16},{24,28},{28,24},{1,5},{5... | collective-permute-start | bytes 1769480 | tf_op jit(solution)/shard_map/ppermute | solution.py:504
  409.7 13.3 %collective-permute-start.77 = (bf16[4,96,768]{2,1,0:T(8,128)(2,1)S(1)}, bf16[4,96,768]{2,1,0:T(8,128)(2,1)S(1)}, u32[]{:S(2)}, u32[]{:S(2)}) collective-permute-start(bf16[4,96,768]{2,1,0:T(8,128)(2,1)S(1)} %copy-done.38), channel_id=1, source_target_pairs={{0,4},{4,0},{8,12},{12,8},{16,20},{20,16},{24,28},{28,24},{1,5},{5... | collective-permute-start | bytes 1769480 | tf_op jit(solution)/shard_map/ppermute | solution.py:504
  418.2 54.7 %collective-permute-start.92 = (bf16[4,4,96,768]{3,2,1,0:T(8,128)(2,1)S(1)}, bf16[4,4,96,768]{3,2,1,0:T(8,128)(2,1)S(1)}, u32[]{:S(2)}, u32[]{:S(2)}) collective-permute-start(bf16[4,4,96,768]{3,2,1,0:T(8,128)(2,1)S(1)} %copy-done.37), channel_id=1, source_target_pairs={{0,4},{4,0},{8,12},{12,8},{16,20},{20,16},{24,28},{28,24},{1,5},{5... | collective-permute-start | bytes 7077896 | tf_op jit(solution)/shard_map/ppermute | solution.py:504
  419.5 57.0 %collective-permute-start.87 = (bf16[4,4,96,768]{3,2,1,0:T(8,128)(2,1)S(1)}, bf16[4,4,96,768]{3,2,1,0:T(8,128)(2,1)S(1)}, u32[]{:S(2)}, u32[]{:S(2)}) collective-permute-start(bf16[4,4,96,768]{3,2,1,0:T(8,128)(2,1)S(1)} %copy-done.36), channel_id=1, source_target_pairs={{0,4},{4,0},{8,12},{12,8},{16,20},{20,16},{24,28},{28,24},{1,5},{5... | collective-permute-start | bytes 7077896 | tf_op jit(solution)/shard_map/ppermute | solution.py:504
  421.7 57.7 %collective-permute-start.82 = (bf16[4,4,96,768]{3,2,1,0:T(8,128)(2,1)S(1)}, bf16[4,4,96,768]{3,2,1,0:T(8,128)(2,1)S(1)}, u32[]{:S(2)}, u32[]{:S(2)}) collective-permute-start(bf16[4,4,96,768]{3,2,1,0:T(8,128)(2,1)S(1)} %copy-done.35), channel_id=1, source_target_pairs={{0,4},{4,0},{8,12},{12,8},{16,20},{20,16},{24,28},{28,24},{1,5},{5... | collective-permute-start | bytes 7077896 | tf_op jit(solution)/shard_map/ppermute | solution.py:504
  421.8 9.5 %collective-permute-start.68 = (bf16[2,96,768]{2,1,0:T(8,128)(2,1)S(1)}, bf16[2,96,768]{2,1,0:T(8,128)(2,1)S(1)}, u32[]{:S(2)}, u32[]{:S(2)}) collective-permute-start(bf16[2,96,768]{2,1,0:T(8,128)(2,1)S(1)} %add_convert_fusion.14), channel_id=1, source_target_pairs={{0,8},{4,12},{8,0},{12,4},{16,24},{20,28},{24,16},{28,20},{1,9},{5... | collective-permute-start | bytes 884744 | tf_op jit(solution)/shard_map/ppermute | solution.py:504
  423.1 9.3 %collective-permute-start.63 = (bf16[2,96,768]{2,1,0:T(8,128)(2,1)S(1)}, bf16[2,96,768]{2,1,0:T(8,128)(2,1)S(1)}, u32[]{:S(2)}, u32[]{:S(2)}) collective-permute-start(bf16[2,96,768]{2,1,0:T(8,128)(2,1)S(1)} %get-tuple-element.176), channel_id=1, source_target_pairs={{0,16},{4,20},{8,24},{12,28},{16,0},{20,4},{24,8},{28,12},{1,17},{... | collective-permute-start | bytes 884744 | tf_op jit(solution)/shard_map/ppermute | solution.py:504
  431.3 9.9 %collective-permute-start.58 = (bf16[2,96,768]{2,1,0:T(8,128)(2,1)S(1)}, bf16[2,96,768]{2,1,0:T(8,128)(2,1)S(1)}, u32[]{:S(2)}, u32[]{:S(2)}) collective-permute-start(bf16[2,96,768]{2,1,0:T(8,128)(2,1)S(1)} %add_convert_fusion.18), channel_id=1, source_target_pairs={{0,8},{4,12},{8,0},{12,4},{16,24},{20,28},{24,16},{28,20},{1,9},{5... | collective-permute-start | bytes 884744 | tf_op jit(solution)/shard_map/ppermute | solution.py:504
  432.4 13.9 %collective-permute-start.78 = (bf16[2,96,768]{2,1,0:T(8,128)(2,1)S(1)}, bf16[2,96,768]{2,1,0:T(8,128)(2,1)S(1)}, u32[]{:S(2)}, u32[]{:S(2)}) collective-permute-start(bf16[2,96,768]{2,1,0:T(8,128)(2,1)S(1)} %add_convert_fusion.12), channel_id=1, source_target_pairs={{0,8},{4,12},{8,0},{12,4},{16,24},{20,28},{24,16},{28,20},{1,9},{5... | collective-permute-start | bytes 884744 | tf_op jit(solution)/shard_map/ppermute | solution.py:504
  468.1 14.8 %collective-permute-start.61 = (bf16[96,192]{1,0:T(8,128)(2,1)S(1)}, bf16[96,192]{1,0:T(8,128)(2,1)S(1)}, u32[]{:S(2)}, u32[]{:S(2)}) collective-permute-start(bf16[96,192]{1,0:T(8,128)(2,1)S(1)} %pad_maximum_fusion.16), channel_id=1, source_target_pairs={{0,2},{1,3},{2,0},{3,1},{4,6},{5,7},{6,4},{7,5},{8,10},{9,11},{10,... | collective-permute-start | bytes 110600 | tf_op jit(solution)/shard_map/ppermute | solution.py:504
  471.2 14.0 %collective-permute-start.81 = (bf16[96,192]{1,0:T(8,128)(2,1)S(1)}, bf16[96,192]{1,0:T(8,128)(2,1)S(1)}, u32[]{:S(2)}, u32[]{:S(2)}) collective-permute-start(bf16[96,192]{1,0:T(8,128)(2,1)S(1)} %pad_maximum_fusion.19), channel_id=1, source_target_pairs={{0,2},{1,3},{2,0},{3,1},{4,6},{5,7},{6,4},{7,5},{8,10},{9,11},{10,... | collective-permute-start | bytes 110600 | tf_op jit(solution)/shard_map/ppermute | solution.py:504
  475.5 29.2 %collective-permute-start.93 = (bf16[2,4,96,768]{3,2,1,0:T(8,128)(2,1)}, bf16[2,4,96,768]{3,2,1,0:T(8,128)(2,1)}, u32[]{:S(2)}, u32[]{:S(2)}) collective-permute-start(bf16[2,4,96,768]{3,2,1,0:T(8,128)(2,1)} %add_convert_fusion), channel_id=1, source_target_pairs={{0,8},{4,12},{8,0},{12,4},{16,24},{20,28},{24,16},{28,20},{1,9},{5... | collective-permute-start | bytes 3538952 | tf_op jit(solution)/shard_map/ppermute | solution.py:504
  478.3 29.5 %collective-permute-start.88 = (bf16[2,4,96,768]{3,2,1,0:T(8,128)(2,1)}, bf16[2,4,96,768]{3,2,1,0:T(8,128)(2,1)}, u32[]{:S(2)}, u32[]{:S(2)}) collective-permute-start(bf16[2,4,96,768]{3,2,1,0:T(8,128)(2,1)} %get-tuple-element.158), channel_id=1, source_target_pairs={{0,16},{4,20},{8,24},{12,28},{16,0},{20,4},{24,8},{28,12},{1,17},{... | collective-permute-start | bytes 3538952 | tf_op jit(solution)/shard_map/ppermute | solution.py:504
  481.9 47.9 %collective-permute-start.83 = (bf16[2,4,96,768]{3,2,1,0:T(8,128)(2,1)}, bf16[2,4,96,768]{3,2,1,0:T(8,128)(2,1)}, u32[]{:S(2)}, u32[]{:S(2)}) collective-permute-start(bf16[2,4,96,768]{3,2,1,0:T(8,128)(2,1)} %add_convert_fusion.4), channel_id=1, source_target_pairs={{0,8},{4,12},{8,0},{12,4},{16,24},{20,28},{24,16},{28,20},{1,9},{5... | collective-permute-start | bytes 3538952 | tf_op jit(solution)/shard_map/ppermute | solution.py:504
  506.7 28.9 %collective-permute-start.94 = (bf16[4,96,768]{2,1,0:T(8,128)(2,1)}, bf16[4,96,768]{2,1,0:T(8,128)(2,1)}, u32[]{:S(2)}, u32[]{:S(2)}) collective-permute-start(bf16[4,96,768]{2,1,0:T(8,128)(2,1)} %fusion.8), channel_id=1, source_target_pairs={{0,16},{4,20},{8,24},{12,28},{16,0},{20,4},{24,8},{28,12},{1,17},{... | collective-permute-start | bytes 1769480 | tf_op jit(solution)/shard_map/ppermute | solution.py:504
  509.9 29.3 %collective-permute-start.89 = (bf16[4,96,768]{2,1,0:T(8,128)(2,1)}, bf16[4,96,768]{2,1,0:T(8,128)(2,1)}, u32[]{:S(2)}, u32[]{:S(2)}) collective-permute-start(bf16[4,96,768]{2,1,0:T(8,128)(2,1)} %fusion.6), channel_id=1, source_target_pairs={{0,8},{4,12},{8,0},{12,4},{16,24},{20,28},{24,16},{28,20},{1,9},{5... | collective-permute-start | bytes 1769480 | tf_op jit(solution)/shard_map/ppermute | solution.py:504
  532.0 10.2 %collective-permute-start.84 = (bf16[4,96,768]{2,1,0:T(8,128)(2,1)}, bf16[4,96,768]{2,1,0:T(8,128)(2,1)}, u32[]{:S(2)}, u32[]{:S(2)}) collective-permute-start(bf16[4,96,768]{2,1,0:T(8,128)(2,1)} %fusion.4), channel_id=1, source_target_pairs={{0,16},{4,20},{8,24},{12,28},{16,0},{20,4},{24,8},{28,12},{1,17},{... | collective-permute-start | bytes 1769480 | tf_op jit(solution)/shard_map/ppermute | solution.py:504
  537.1 9.5 %collective-permute-start.95 = (bf16[2,96,768]{2,1,0:T(8,128)(2,1)S(1)}, bf16[2,96,768]{2,1,0:T(8,128)(2,1)S(1)}, u32[]{:S(2)}, u32[]{:S(2)}) collective-permute-start(bf16[2,96,768]{2,1,0:T(8,128)(2,1)S(1)} %slice.990), channel_id=1, source_target_pairs={{0,1},{1,0},{2,3},{3,2},{4,5},{5,4},{6,7},{7,6},{8,9},{9,8},{10,11... | collective-permute-start | bytes 884744 | tf_op jit(solution)/shard_map/ppermute | solution.py:504
  540.6 12.3 %collective-permute-start.90 = (bf16[2,96,768]{2,1,0:T(8,128)(2,1)S(1)}, bf16[2,96,768]{2,1,0:T(8,128)(2,1)S(1)}, u32[]{:S(2)}, u32[]{:S(2)}) collective-permute-start(bf16[2,96,768]{2,1,0:T(8,128)(2,1)S(1)} %slice.976), channel_id=1, source_target_pairs={{0,1},{1,0},{2,3},{3,2},{4,5},{5,4},{6,7},{7,6},{8,9},{9,8},{10,11... | collective-permute-start | bytes 884744 | tf_op jit(solution)/shard_map/ppermute | solution.py:504
  543.6 12.5 %collective-permute-start.85 = (bf16[2,96,768]{2,1,0:T(8,128)(2,1)S(1)}, bf16[2,96,768]{2,1,0:T(8,128)(2,1)S(1)}, u32[]{:S(2)}, u32[]{:S(2)}) collective-permute-start(bf16[2,96,768]{2,1,0:T(8,128)(2,1)S(1)} %slice.966), channel_id=1, source_target_pairs={{0,1},{1,0},{2,3},{3,2},{4,5},{5,4},{6,7},{7,6},{8,9},{9,8},{10,11... | collective-permute-start | bytes 884744 | tf_op jit(solution)/shard_map/ppermute | solution.py:504
  546.7 9.6 %collective-permute-start.96 = (bf16[96,768]{1,0:T(8,128)(2,1)S(1)}, bf16[96,768]{1,0:T(8,128)(2,1)S(1)}, u32[]{:S(2)}, u32[]{:S(2)}) collective-permute-start(bf16[96,768]{1,0:T(8,128)(2,1)S(1)} %fusion.26), channel_id=1, source_target_pairs={{0,2},{1,3},{2,0},{3,1},{4,6},{5,7},{6,4},{7,5},{8,10},{9,11},{10,... | collective-permute-start | bytes 442376 | tf_op jit(solution)/shard_map/ppermute | solution.py:504
  (111 other events, 1359.2 us)

commit v3 on v2

v3 whole, which is shorter than its diff:
```python
import functools
import math

import jax
import jax.numpy as jnp
from jax import lax
from jax.experimental import pallas as pl
from jax.experimental.pallas import tpu as pltpu
from jax.sharding import PartitionSpec as P

HEAD = 64
SEQ = 1024
GROUP = 4
QB = 256
AB = 512
FEED_ROWS = 1024
BLOCKS = 8
LOG2E = 1.4426950408889634
INV_ROOT_HEAD = 1.0 / math.sqrt(HEAD)
SCALE = LOG2E * INV_ROOT_HEAD
NORM_EPS = 1e-12
INV_ROOT_TWO = 0.7071067811865476
INV_ROOT_TWO_PI = 0.3989422804014327
FF_CHUNKS = 3
NT = (((1,), (1,)), ((), ()))
NN = (((1,), (0,)), ((), ()))
BF16 = jnp.bfloat16
F32 = jnp.float32


def mm(left, right, dims=NN):
    return lax.dot_general(left, right, dims, preferred_element_type=F32)


def params(**more):
    return pltpu.CompilerParams(vmem_limit_bytes=56 << 20, **more)


BRIEF = pl.CostEstimate(flops=1 << 20, bytes_accessed=1 << 16, transcendentals=0)


SMEM = pl.BlockSpec(memory_space=pltpu.SMEM)


def whole(*shape):
    return pl.BlockSpec(shape, lambda *_: (0,) * len(shape))


def shaped(dtype, *shape):
    return jax.ShapeDtypeStruct(shape, dtype)


def assemble(place_ref, piece_refs, full_ref):
    at = 0
    for piece_ref in piece_refs:
        for i in range(piece_ref.shape[0]):
            rows = piece_ref.shape[1]
            start = pl.multiple_of(place_ref[at] * rows, rows)
            full_ref[pl.ds(start, rows), :] = piece_ref[i]
            at += 1


def deal(place_ref, full_ref, even_ref, odd_ref):
    rows = full_ref.shape[0] // BLOCKS
    for at in range(BLOCKS):
        start = pl.multiple_of(place_ref[at] * rows, rows)
        target = odd_ref if at >= BLOCKS // 2 else even_ref
        target[at % (BLOCKS // 2)] = full_ref[pl.ds(start, rows), :]


def piece_specs(pieces):
    arrays, column = pieces
    specs = []
    for array in arrays:
        if column is None:
            specs.append(whole(*array.shape))
        else:
            count, _, rows, lanes = array.shape
            at = (lambda m: (0, m, 0, 0)) if column == "grid" else (lambda _: (0, column, 0, 0))
            specs.append(pl.BlockSpec((count, None, rows, lanes), at))
    return specs


def fill_row_distance(dist_ref):
    row = lax.broadcasted_iota(jnp.int32, dist_ref.shape, 0)
    col = lax.broadcasted_iota(jnp.int32, dist_ref.shape, 1)
    dist_ref[...] = jnp.abs(row - col + (SEQ - AB)).astype(F32) * LOG2E


def fill_distance(dist_ref):
    row = lax.broadcasted_iota(jnp.int32, dist_ref.shape, 0)
    col = lax.broadcasted_iota(jnp.int32, dist_ref.shape, 1)
    dist_ref[...] = jnp.abs(row - col - (SEQ - AB)).astype(F32) * LOG2E


def attend_kernel(base, count, place_ref, slope_ref, x_ref, bias_ref, *rest):
    piece_refs = rest[:count]
    qkv_ref, ctx_ref, lse_ref, full_ref, dist_ref = rest[count:]
    width = GROUP * HEAD
    assemble(place_ref, piece_refs, full_ref)
    fill_row_distance(dist_ref)
    for block in range(SEQ // AB):
        rows = slice(block * AB, (block + 1) * AB)
        qkv_ref[rows, :] = (mm(x_ref[rows, :], full_ref[...]) + bias_ref[...]).astype(BF16)
    lane = lax.broadcasted_iota(jnp.int32, (1, 128), 1)
    for pair in range(GROUP // 2):
        keys = qkv_ref[:, width + 128 * pair : width + 128 * pair + 128]
        values = qkv_ref[:, 2 * width + 128 * pair : 2 * width + 128 * pair + 128]
        for block in range(SEQ // AB):
            rows = slice(block * AB, (block + 1) * AB)
            start = SEQ - AB - block * AB
            q = qkv_ref[rows, 128 * pair : 128 * pair + 128]
            parts = []
            stats = []
            for side in range(2):
                own = (lane < HEAD) if side == 0 else (lane >= HEAD)
                slope = slope_ref[base + 2 * pair + side]
                s = mm(jnp.where(own, q, jnp.zeros_like(q)), keys, NT) * SCALE
                s = s - slope * dist_ref[:, start : start + SEQ]
                top = jnp.max(s, axis=1, keepdims=True)
                w = jnp.exp2(s - top)
                total = jnp.sum(w, axis=1, keepdims=True)
                p = (w * (1.0 / total)).astype(BF16)
                parts.append(mm(p, values))
                stats.append(top + jnp.log2(total))
            ctx = jnp.where(lane < HEAD, parts[0], parts[1])
            ctx_ref[rows, 128 * pair : 128 * pair + 128] = ctx.astype(BF16)
            flipped = jnp.where(lane < HEAD, stats[0], stats[1]).T
            lse_ref[2 * pair : 2 * pair + 1, rows] = flipped[0:1, :]
            lse_ref[2 * pair + 1 : 2 * pair + 2, rows] = flipped[HEAD : HEAD + 1, :]


def attend_forward(group, place, slopes, x, bias, pieces):
    width = GROUP * HEAD
    depth = x.shape[1]
    return pl.pallas_call(
        functools.partial(attend_kernel, group * GROUP, len(pieces[0])),
        grid=(1,),
        in_specs=[SMEM, SMEM, whole(SEQ, depth), whole(1, 3 * width)]
        + piece_specs(pieces),
        out_specs=[whole(SEQ, 3 * width), whole(SEQ, width), whole(GROUP, SEQ)],
        out_shape=[
            shaped(BF16, SEQ, 3 * width),
            shaped(BF16, SEQ, width),
            shaped(F32, GROUP, SEQ),
        ],
        scratch_shapes=[
            pltpu.VMEM((depth, 3 * width), BF16),
            pltpu.VMEM((AB, 2 * SEQ - AB), F32),
        ],
        compiler_params=params(),
        cost_estimate=BRIEF,
        name="attend_forward",
    )(place, slopes, x, bias, *pieces[0])


def attend_back_pair(pair, slopes, qkv_ref, lse_ref, dctx_ref, dist_ref, acc_ref, dqt_ref, sums_ref):
    width = GROUP * HEAD
    lane = lax.broadcasted_iota(jnp.int32, (1, 128), 1)
    cols = slice(128 * pair, 128 * pair + 128)
    keys = qkv_ref[:, width + 128 * pair : width + 128 * pair + 128]
    values = qkv_ref[:, 2 * width + 128 * pair : 2 * width + 128 * pair + 128]
    keys_t = keys.T
    for side in range(2):
        own = (lane < HEAD) if side == 0 else (lane >= HEAD)
        own_rows = slice(HEAD * side, HEAD * side + HEAD)
        for block in range(SEQ // AB):
            rows = slice(block * AB, (block + 1) * AB)
            start = SEQ - AB - block * AB
            q = qkv_ref[rows, cols]
            q = jnp.where(own, q, jnp.zeros_like(q))
            do = dctx_ref[rows, cols]
            do = jnp.where(own, do, jnp.zeros_like(do))
            s = mm(keys, q, NT) * SCALE
            s = s - slopes[side] * dist_ref[start : start + SEQ, :]
            p = jnp.exp2(s - lse_ref[2 * pair + side : 2 * pair + side + 1, rows])
            dp = mm(values, do, NT)
            inner = jnp.sum(p * dp, axis=0, keepdims=True)
            ds = (p * (dp - inner)).astype(BF16)
            p = p.astype(BF16)
            dv = mm(p, do)
            dk = mm(ds, q)
            if block == 0 and side == 0:
                acc_ref[:, 0:128] = dk
                acc_ref[:, 128:256] = dv
            else:
                acc_ref[:, 0:128] += dk
                acc_ref[:, 128:256] += dv
            dqt_ref[own_rows, rows] = mm(keys_t[own_rows], ds)
    dq = dqt_ref[...].T * INV_ROOT_HEAD
    dk = acc_ref[:, 0:128] * INV_ROOT_HEAD
    dv = acc_ref[:, 128:256]
    sums_ref[0:1, :] = jnp.sum(dq, axis=0, keepdims=True)
    sums_ref[1:2, :] = jnp.sum(dv, axis=0, keepdims=True)
    return dq.astype(BF16), dk.astype(BF16), dv.astype(BF16)


def attend_back_first(
    base, slope_ref, qkv_ref, lse_ref, dctx_ref, dqkv_ref, sums_ref, dist_ref, acc_ref, dqt_ref
):
    fill_distance(dist_ref)
    slopes = [slope_ref[base], slope_ref[base + 1]]
    got = attend_back_pair(
        0, slopes, qkv_ref, lse_ref, dctx_ref, dist_ref, acc_ref, dqt_ref, sums_ref
    )
    for i, value in enumerate(got):
        dqkv_ref[:, 128 * i : 128 * i + 128] = value


def attend_back_second(
    base, count, place_ref, slope_ref, qkv_ref, lse_ref, dctx_ref, x_t_ref, acc_in_ref, pair_ref, *rest
):
    piece_refs = rest[:count]
    (even_ref, odd_ref, sums_ref, acc_out_ref, full_ref, dist_ref, acc_ref, dqt_ref, dqkv_ref) = rest[
        count:
    ]
    width = GROUP * HEAD
    fill_distance(dist_ref)
    assemble(place_ref, piece_refs, full_ref)
    slopes = [slope_ref[base + 2], slope_ref[base + 3]]
    got = attend_back_pair(
        1, slopes, qkv_ref, lse_ref, dctx_ref, dist_ref, acc_ref, dqt_ref, sums_ref
    )
    for i, value in enumerate(got):
        dqkv_ref[:, width * i : width * i + 128] = pair_ref[:, 128 * i : 128 * i + 128]
        dqkv_ref[:, width * i + 128 : width * i + 256] = value
    for block in range(SEQ // AB):
        rows = slice(block * AB, (block + 1) * AB)
        d_rows = acc_in_ref[rows, :] + mm(dqkv_ref[rows, :], full_ref[...], NT)
        acc_out_ref[rows, :] = d_rows.astype(acc_out_ref.dtype)
    full_ref[...] = mm(x_t_ref[...], dqkv_ref[...]).astype(BF16)
    deal(place_ref, full_ref, even_ref, odd_ref)


def attend_scratch():
    return [
        pltpu.VMEM((2 * SEQ - AB, AB), F32),
        pltpu.VMEM((SEQ, 256), F32),
        pltpu.VMEM((128, SEQ), F32),
    ]


def attend_backward_first(group, slopes, qkv, lse, d_context):
    width = GROUP * HEAD
    return pl.pallas_call(
        functools.partial(attend_back_first, group * GROUP),
        grid=(1,),
        in_specs=[
            SMEM,
            whole(SEQ, 3 * width),
            whole(GROUP, SEQ),
            pl.BlockSpec((SEQ, width), lambda _: (0, group)),
        ],
        out_specs=[whole(SEQ, 3 * 128), whole(2, 128)],
        out_shape=[shaped(BF16, SEQ, 3 * 128), shaped(F32, 2, 128)],
        scratch_shapes=attend_scratch(),
        compiler_params=params(),
        cost_estimate=BRIEF,
        name="attend_backward_first",
    )(slopes, qkv, lse, d_context)


def attend_backward_second(
    group, last, place, slopes, qkv, lse, d_context, x_t, d_tokens, pair, pieces
):
    width = GROUP * HEAD
    depth = x_t.shape[0]
    rows = depth // BLOCKS
    return pl.pallas_call(
        functools.partial(attend_back_second, group * GROUP, len(pieces[0])),
        grid=(1,),
        in_specs=[
            SMEM,
            SMEM,
            whole(SEQ, 3 * width),
            whole(GROUP, SEQ),
            pl.BlockSpec((SEQ, width), lambda _: (0, group)),
            whole(depth, SEQ),
            whole(SEQ, depth),
            whole(SEQ, 3 * 128),
        ]
        + piece_specs(pieces),
        out_specs=[
            whole(BLOCKS // 2, rows, 3 * width),
            whole(BLOCKS // 2, rows, 3 * width),
            whole(2, 128),
            whole(SEQ, depth),
        ],
        out_shape=[
            shaped(BF16, BLOCKS // 2, rows, 3 * width),
            shaped(BF16, BLOCKS // 2, rows, 3 * width),
            shaped(F32, 2, 128),
            shaped(BF16 if last else F32, SEQ, depth),
        ],
        scratch_shapes=[pltpu.VMEM((depth, 3 * width), BF16)]
        + attend_scratch()
        + [pltpu.VMEM((SEQ, 3 * width), BF16)],
        compiler_params=params(),
        cost_estimate=BRIEF,
        name="attend_backward_second",
    )(place, slopes, qkv, lse, d_context, x_t, d_tokens, pair, *pieces[0])


def row_mean(value):
    return jnp.mean(value, axis=1, keepdims=True)


def normalize(resid):
    center = resid - row_mean(resid)
    inverse = lax.rsqrt(row_mean(center * center) + NORM_EPS)
    return center * inverse, inverse


def norm_pull(grad_rows, normed, inverse, gain):
    scaled = grad_rows * gain
    return inverse * (scaled - row_mean(scaled) - normed * row_mean(scaled * normed))


def add_sums(sums_ref, values, first):
    for place, value in enumerate(values):
        row = jnp.sum(value, axis=0, keepdims=True)
        if first:
            sums_ref[place : place + 1, :] = row
        else:
            sums_ref[place : place + 1, :] += row


def join_kernel(count, place_ref, x_ref, vec_ref, *rest):
    ctx_refs = rest[:3]
    piece_refs = rest[3 : 3 + count]
    normed_ref, inverse_ref, low_ref, low_t_ref, full_ref = rest[3 + count :]
    assemble(place_ref, piece_refs, full_ref)
    width = ctx_refs[0].shape[1]
    for block in range(SEQ // QB):
        rows = slice(block * QB, (block + 1) * QB)
        total = x_ref[rows, :].astype(F32) + vec_ref[0:1, :]
        for g, ctx_ref in enumerate(ctx_refs):
            total += mm(ctx_ref[rows, :], full_ref[:, g * width : (g + 1) * width], NT)
        normed, inverse = normalize(total)
        normed_ref[rows, :] = normed
        inverse_ref[rows, :] = jnp.broadcast_to(inverse, (QB, 128))
        low = normed * vec_ref[1:2, :] + vec_ref[2:3, :]
        low_ref[rows, :] = low.astype(BF16)
        low_t_ref[:, rows] = low.astype(BF16).T


def join(place, x, vec, ctx, pieces):
    depth = x.shape[1]
    rows = depth // BLOCKS
    return pl.pallas_call(
        functools.partial(join_kernel, len(pieces[0])),
        grid=(1,),
        in_specs=[SMEM, whole(SEQ, depth), whole(8, depth)]
        + [whole(SEQ, ctx[0].shape[1])] * 3
        + piece_specs(pieces),
        out_specs=[whole(SEQ, depth), whole(SEQ, 128), whole(SEQ, depth), whole(depth, SEQ)],
        out_shape=[
            shaped(F32, SEQ, depth),
            shaped(F32, SEQ, 128),
            shaped(BF16, SEQ, depth),
            shaped(BF16, depth, SEQ),
        ],
        scratch_shapes=[pltpu.VMEM((depth, depth), BF16)],
        compiler_params=params(),
        cost_estimate=BRIEF,
        name="join",
    )(place, x, vec, *ctx, *pieces[0])


def turn_kernel(ffn_ref, normed1_ref, cot_ref, vec_ref, out_ref, d_ref, low_ref, low_t_ref, sums_ref):
    for block in range(SEQ // QB):
        rows = slice(block * QB, (block + 1) * QB)
        hidden = normed1_ref[rows, :] * vec_ref[1:2, :] + vec_ref[2:3, :]
        normed, inverse = normalize(hidden + ffn_ref[rows, :] + vec_ref[3:4, :])
        out_ref[rows, :] = (normed * vec_ref[4:5, :] + vec_ref[5:6, :]).astype(BF16)
        grad = cot_ref[rows, :].astype(F32)
        d_resid = norm_pull(grad, normed, inverse, vec_ref[4:5, :])
        d_ref[rows, :] = d_resid
        low_ref[rows, :] = d_resid.astype(BF16)
        low_t_ref[:, rows] = d_resid.astype(BF16).T
        add_sums(sums_ref, (grad * normed, grad, d_resid), block == 0)


def turn(ffn, normed1, cot, vec):
    depth = cot.shape[1]
    return pl.pallas_call(
        turn_kernel,
        grid=(1,),
        in_specs=[whole(SEQ, depth)] * 3 + [whole(8, depth)],
        out_specs=[whole(SEQ, depth)] * 3 + [whole(depth, SEQ), whole(3, depth)],
        out_shape=[
            shaped(BF16, SEQ, depth),
            shaped(F32, SEQ, depth),
            shaped(BF16, SEQ, depth),
            shaped(BF16, depth, SEQ),
            shaped(F32, 3, depth),
        ],
        compiler_params=params(),
        cost_estimate=BRIEF,
        name="turn",
    )(ffn, normed1, cot, vec)


def rejoin_kernel(count, place_ref, d_hidden_ref, normed_ref, inverse_ref, vec_ref, *rest):
    ctx_refs = rest[:3]
    piece_refs = rest[3 : 3 + count]
    d_ref, dctx_ref, even_ref, odd_ref, sums_ref, full_ref, low_t_ref = rest[3 + count :]
    width = ctx_refs[0].shape[1]
    assemble(place_ref, piece_refs, full_ref)
    for block in range(SEQ // QB):
        rows = slice(block * QB, (block + 1) * QB)
        normed = normed_ref[rows, :]
        grad = d_hidden_ref[rows, :]
        d_resid = norm_pull(grad, normed, inverse_ref[rows, 0:1], vec_ref[1:2, :])
        d_ref[rows, :] = d_resid
        low = d_resid.astype(BF16)
        low_t_ref[:, rows] = d_resid.astype(BF16).T
        dctx_ref[rows, :] = mm(low, full_ref[...]).astype(BF16)
        add_sums(sums_ref, (grad * normed, grad, d_resid), block == 0)
    for g, ctx_ref in enumerate(ctx_refs):
        full_ref[:, g * width : (g + 1) * width] = mm(low_t_ref[...], ctx_ref[...]).astype(BF16)
    deal(place_ref, full_ref, even_ref, odd_ref)


def rejoin(place, d_hidden, normed, inverse, vec, ctx, pieces):
    depth = d_hidden.shape[1]
    rows = depth // BLOCKS
    return pl.pallas_call(
        functools.partial(rejoin_kernel, len(pieces[0])),
        grid=(1,),
        in_specs=[SMEM, whole(SEQ, depth), whole(SEQ, depth), whole(SEQ, 128), whole(8, depth)]
        + [whole(SEQ, ctx[0].shape[1])] * 3
        + piece_specs(pieces),
        out_specs=[
            whole(SEQ, depth),
            whole(SEQ, depth),
            whole(BLOCKS // 2, rows, depth),
            whole(BLOCKS // 2, rows, depth),
            whole(3, depth),
        ],
        out_shape=[
            shaped(F32, SEQ, depth),
            shaped(BF16, SEQ, depth),
            shaped(BF16, BLOCKS // 2, rows, depth),
            shaped(BF16, BLOCKS // 2, rows, depth),
            shaped(F32, 3, depth),
        ],
        scratch_shapes=[pltpu.VMEM((depth, depth), BF16), pltpu.VMEM((depth, SEQ), BF16)],
        compiler_params=params(),
        cost_estimate=BRIEF,
        name="rejoin",
    )(place, d_hidden, normed, inverse, vec, *ctx, *pieces[0])


def gelu_parts(gate):
    normal_cdf = 0.5 * (1.0 + lax.erf(gate * INV_ROOT_TWO))
    density = jnp.exp(-0.5 * gate * gate) * INV_ROOT_TWO_PI
    return gate * normal_cdf, normal_cdf + gate * density


def feed_kernel(first, count, place_ref, low_ref, *rest):
    if not first:
        acc_in_ref, *rest = rest
    piece_refs = rest[:count]
    acc_ref, gated_ref, slope_ref, active_ref, full_ref = rest[count:]
    part = gated_ref.shape[1]
    assemble(place_ref, piece_refs, full_ref)

    @pl.when(pl.program_id(0) == 0)
    def _():
        acc_ref[...] = jnp.zeros_like(acc_ref) if first else acc_in_ref[...]

    for block in range(SEQ // FEED_ROWS):
        rows = slice(block * FEED_ROWS, (block + 1) * FEED_ROWS)
        both = mm(low_ref[rows, :], full_ref[:, : 2 * part])
        up = both[:, part:]
        active, slope = gelu_parts(both[:, :part])
        gated = (active * up).astype(BF16)
        gated_ref[rows, :] = gated
        slope_ref[rows, :] = (slope * up).astype(BF16)
        active_ref[rows, :] = active.astype(BF16)
        acc_ref[rows, :] += mm(gated, full_ref[:, 2 * part :], NT)


def feed(place, low, acc, pieces):
    depth = low.shape[1]
    _, steps, rows, lanes = pieces[0][0].shape
    part = lanes // 3
    columns = pl.BlockSpec((SEQ, part), lambda m: (0, m))
    first = acc is None
    return pl.pallas_call(
        functools.partial(feed_kernel, first, len(pieces[0])),
        grid=(steps,),
        in_specs=[SMEM, whole(SEQ, depth)]
        + ([] if first else [whole(SEQ, depth)])
        + piece_specs(pieces),
        out_specs=[whole(SEQ, depth), columns, columns, columns],
        out_shape=[shaped(F32, SEQ, depth)] + [shaped(BF16, SEQ, steps * part)] * 3,
        scratch_shapes=[pltpu.VMEM((depth, lanes), BF16)],
        compiler_params=params(),
        cost_estimate=BRIEF,
        name="feed",
    )(place, low, *([] if first else [acc]), *pieces[0])


def feed_back_kernel(
    count, place_ref, d_ref, d_t_ref, low_t_ref, acc_in_ref, gated_ref, slope_ref, active_ref, *rest
):
    piece_refs = rest[:count]
    acc_ref, even_ref, odd_ref, full_ref, gate_up_ref, keep_ref = rest[count:]
    part = gated_ref.shape[1]
    assemble(place_ref, piece_refs, full_ref)
    step = pl.program_id(0)
    at = pl.ds(pl.multiple_of(step * 2 * part, part), 2 * part)
    keep_ref[:, at] = full_ref[:, : 2 * part]
    for block in range(SEQ // QB):
        rows = slice(block * QB, (block + 1) * QB)
        d_gated = mm(d_ref[rows, :], full_ref[:, 2 * part :])
        d_gate = (d_gated * slope_ref[rows, :].astype(F32)).astype(BF16)
        d_up = (d_gated * active_ref[rows, :].astype(F32)).astype(BF16)
        gate_up_ref[rows, at] = jnp.concatenate([d_gate, d_up], axis=1)
    full_ref[:, : 2 * part] = mm(low_t_ref[...], gate_up_ref[:, at]).astype(BF16)
    full_ref[:, 2 * part :] = mm(d_t_ref[...], gated_ref[...]).astype(BF16)
    deal(place_ref, full_ref, even_ref, odd_ref)

    @pl.when(step == pl.num_programs(0) - 1)
    def _():
        for block in range(SEQ // QB):
            rows = slice(block * QB, (block + 1) * QB)
            acc_ref[rows, :] = acc_in_ref[rows, :] + mm(gate_up_ref[rows, :], keep_ref[...], NT)


def feed_back(place, d_low, d_low_t, low_t, acc, gated, slope, active, pieces):
    depth = d_low.shape[1]
    _, steps, rows, lanes = pieces[0][0].shape
    part = lanes // 3
    columns = pl.BlockSpec((SEQ, part), lambda m: (0, m))
    dealt = pl.BlockSpec((BLOCKS // 2, None, rows, lanes), lambda m: (0, m, 0, 0))
    return pl.pallas_call(
        functools.partial(feed_back_kernel, len(pieces[0])),
        grid=(steps,),
        in_specs=[SMEM, whole(SEQ, depth), whole(depth, SEQ), whole(depth, SEQ), whole(SEQ, depth)]
        + [columns] * 3
        + piece_specs(pieces),
        out_specs=[whole(SEQ, depth), dealt, dealt],
        out_shape=[shaped(F32, SEQ, depth)] + [shaped(BF16, BLOCKS // 2, steps, rows, lanes)] * 2,
        scratch_shapes=[
            pltpu.VMEM((depth, lanes), BF16),
            pltpu.VMEM((SEQ, 2 * steps * part), BF16),
            pltpu.VMEM((depth, 2 * steps * part), BF16),
        ],
        compiler_params=params(),
        cost_estimate=BRIEF,
        name="feed_back",
    )(place, d_low, d_low_t, low_t, acc, gated, slope, active, *pieces[0])


def halves(value, size):
    blocks = [value[:, i : i + size] for i in range(0, value.shape[1], size)]
    return jnp.concatenate(blocks[1::2], axis=1), jnp.concatenate(blocks[0::2], axis=1)


def four(mine, first, second, both):
    values = [item.astype(F32) for item in (mine, first, second, both)]
    return (values[0] + values[1]) + (values[2] + values[3])


def after(value, *earlier):
    earlier = [item for item in jax.tree.leaves(earlier) if item is not value]
    if not earlier:
        return value
    return lax.optimization_barrier((value, *earlier))[0]


def after_all(values, tie):
    return [after(value, tie) for value in values]


def add_three(*values):
    values = [value.astype(F32) for value in values]
    return (values[0] + values[1] + values[2]).astype(BF16)


def add_low(left, right):
    return (left.astype(F32) + right.astype(F32)).astype(BF16)


def interleave(parts, size):
    lanes = parts[0].shape[1]
    return jnp.concatenate(
        [part[:, i : i + size] for i in range(0, lanes, size) for part in parts], axis=1
    )


def pick(value, size, at):
    return jnp.concatenate(
        [value[:, i : i + size] for i in range(at * size, value.shape[1], 4 * size)], axis=1
    )


class Layer:
    def __init__(self, values, order, places):
        (
            self.tokens,
            self.qkv_weight,
            qv_bias,
            self.out_weight,
            out_bias,
            norm1_gain,
            norm1_shift,
            self.in_weight,
            self.down_weight,
            down_bias,
            norm2_gain,
            norm2_shift,
            self.cotangent,
        ) = values
        self.depth = self.tokens.shape[1]
        self.rows = self.qkv_weight.shape[0]
        self.groups = self.qkv_weight.shape[2] // HEAD
        self.part = self.in_weight.shape[2] // FF_CHUNKS
        self.n_tensor = order.shape[0]
        self.places = places
        groups = self.groups
        head_ids = (order[None, :] * groups + jnp.arange(groups, dtype=jnp.int32)[:, None]).reshape(-1)
        powers = jnp.where(head_ids < 8, -(head_ids + 1).astype(F32), 7.5 - head_ids.astype(F32))
        self.slopes = jnp.exp2(powers)
        bias = qv_bias.reshape(2, self.n_tensor, groups, HEAD)[:, order].transpose(2, 0, 1, 3)
        bias = bias.reshape(groups, 2, self.n_tensor * HEAD)
        self.bias = jnp.concatenate([bias[:, 0], jnp.zeros_like(bias[:, 0]), bias[:, 1]], axis=1)
        self.vec = jnp.stack(
            [out_bias, norm1_gain, norm1_shift, down_bias, norm2_gain, norm2_shift, out_bias, out_bias]
        )
        self.tokens_t = self.tokens.T
        self.done = []
        self.kept = []
        self.bias_grads = []
        self.pieces = {}
        self.acc = None

    def head_columns(self, g):
        return [self.qkv_weight[:, c, g * HEAD : (g + 1) * HEAD] for c in range(3)]

    def unit_columns(self, c):
        cols = slice(c * self.part, (c + 1) * self.part)
        return jnp.concatenate(
            [self.in_weight[:, 0, cols], self.in_weight[:, 1, cols], self.down_weight[:, cols]], axis=1
        )

    def attend(self, g, *ready):
        got = attend_forward(
            g,
            self.places[g],
            self.slopes,
            after(self.tokens, *ready),
            self.bias[g : g + 1],
            self.pieces[g],
        )
        self.done.append(got)
        return got[2]

    def join(self, *ready):
        self.qkv, self.ctx, self.lse = zip(*self.done)
        tokens = after(self.tokens, *ready)
        self.normed1, self.inverse1, self.low, self.low_t = join(
            self.places["o"], tokens, self.vec, self.ctx, self.pieces["o"]
        )
        return self.inverse1

    def feed(self, c, *ready):
        low = after(self.low, *ready)
        name = f"u{c}"
        self.acc, *saved = feed(self.places[name], low, self.acc, self.pieces[name])
        self.kept.append(saved)
        return self.acc

    def turn(self):
        self.result, self.d_hidden, self.d_low, self.d_low_t, self.sums2 = turn(
            self.acc, self.normed1, self.cotangent, self.vec
        )

    def feed_back(self, c, *ready):
        d_hidden = after(self.d_hidden, *ready)
        name = f"u{c}"
        self.d_hidden, even, odd = feed_back(
            self.places[name],
            self.d_low,
            self.d_low_t,
            self.low_t,
            d_hidden,
            *self.kept[c],
            self.pieces[name],
        )
        return even, odd, self.d_hidden

    def rejoin(self, *ready):
        d_hidden = after(self.d_hidden, *ready)
        self.d_tokens, self.d_context, even, odd, self.sums1 = rejoin(
            self.places["o"],
            d_hidden,
            self.normed1,
            self.inverse1,
            self.vec,
            self.ctx,
            self.pieces["o"],
        )
        return even, odd, self.d_tokens

    def attend_back_first(self, g, *ready):
        self.d_context = after(self.d_context, *ready)
        self.pair, self.pair_sums = attend_backward_first(
            g, self.slopes, self.qkv[g], self.lse[g], self.d_context
        )
        return self.pair

    def attend_back_second(self, g, *ready):
        d_tokens = after(self.d_tokens, *ready)
        even, odd, sums, self.d_tokens = attend_backward_second(
            g,
            g == self.groups - 1,
            self.places[g],
            self.slopes,
            self.qkv[g],
            self.lse[g],
            self.d_context,
            self.tokens_t,
            d_tokens,
            self.pair,
            self.pieces[g],
        )
        sums = jnp.concatenate([self.pair_sums, sums], axis=1)
        self.bias_grads.append(sums.reshape(2, self.n_tensor, HEAD))
        return even, odd, self.d_tokens

    def small_sums(self, back):
        qv_grad = jnp.stack(self.bias_grads, axis=2)[:, back].reshape(2, self.depth)
        return jnp.concatenate([self.sums1, self.sums2, qv_grad])

    def outputs(self, grads, sums):
        part = self.part
        units = [grads[f"u{c}"] for c in range(FF_CHUNKS)]
        qkv = [grads[g].reshape(self.rows, 3, HEAD) for g in range(self.groups)]
        in_grad = jnp.stack(
            [
                jnp.concatenate([unit[:, i * part : (i + 1) * part] for unit in units], axis=1)
                for i in range(2)
            ],
            axis=1,
        )
        return (
            self.result,
            self.d_tokens,
            jnp.concatenate(qkv, axis=2),
            sums[6:],
            grads["o"],
            sums[2],
            sums[0],
            sums[1],
            in_grad,
            jnp.concatenate([unit[:, 2 * part :] for unit in units], axis=1),
            sums[5],
            sums[3],
            sums[4],
        )


def plain(*values):
    n_tensor = lax.axis_size("tensor")
    index = jnp.arange(n_tensor, dtype=jnp.int32)
    place = jnp.arange(BLOCKS, dtype=jnp.int32)
    names = [0, 1, 2, "o"] + [f"u{c}" for c in range(FF_CHUNKS)]
    layer = Layer(values, index, {name: place for name in names})
    depth = layer.depth

    def heads(piece):
        rows, lanes = piece.shape
        columns = lax.all_gather(
            piece.reshape(rows, lanes // HEAD, 1, HEAD), "tensor", axis=2, tiled=True
        )
        columns = lax.all_gather(columns.reshape(rows, -1), "dp", axis=0, tiled=True)
        return ([columns.reshape(BLOCKS, depth // BLOCKS, -1)], None)

    def units(piece):
        columns = lax.all_gather(lax.all_gather(piece, "tensor", axis=0), "dp", axis=1, tiled=True)
        blocks = columns.reshape(n_tensor, BLOCKS, depth // BLOCKS, -1)
        return ([jnp.moveaxis(blocks, 0, 1)], "grid")

    def total_rows(even, odd):
        blocks = jnp.concatenate([even, odd]).astype(F32)
        blocks = jnp.moveaxis(blocks, 0, -3)
        blocks = blocks.reshape(blocks.shape[:-3] + (-1, blocks.shape[-1]))
        return lax.psum_scatter(blocks, "dp", scatter_dimension=blocks.ndim - 2, tiled=True)

    def total_heads(even, odd):
        mine = total_rows(even, odd)
        rows = mine.shape[0]
        mine = mine.reshape(rows, -1, n_tensor, HEAD)
        mine = lax.psum_scatter(mine, "tensor", scatter_dimension=2, tiled=True)
        return mine.reshape(rows, -1)

    def total_units(even, odd):
        return lax.psum_scatter(total_rows(even, odd), "tensor", scatter_dimension=0, tiled=False)

    for g in range(layer.groups):
        layer.pieces[g] = heads(jnp.concatenate(layer.head_columns(g), axis=1))
        layer.attend(g)
    layer.pieces["o"] = heads(layer.out_weight)
    layer.join()
    for c in range(FF_CHUNKS):
        layer.pieces[f"u{c}"] = units(layer.unit_columns(c))
        layer.feed(c)
    layer.turn()
    grads = {}
    for c in range(FF_CHUNKS):
        grads[f"u{c}"] = total_units(*layer.feed_back(c)[:2])
    grads["o"] = total_heads(*layer.rejoin()[:2])
    for g in range(layer.groups):
        layer.attend_back_first(g)
        grads[g] = total_heads(*layer.attend_back_second(g)[:2])
    return layer.outputs(grads, lax.psum(layer.small_sums(index), ("dp", "tensor")))


def paired(*values):
    me = lax.axis_index("dp")
    at = lax.axis_index("tensor")

    def dp(value, bit):
        return lax.ppermute(value, "dp", [(i, i ^ bit) for i in range(8)])

    def tp(value, bit):
        return lax.ppermute(value, "tensor", [(i, i ^ bit) for i in range(4)])

    def stacked(left, right):
        return jnp.stack([left, right])

    x, y, core = 2, 4, 1
    order = jnp.array([0, 2, 1, 3], jnp.int32) ^ at
    back = jnp.arange(4, dtype=jnp.int32) ^ at
    back = (back & 1) * 2 + (back >> 1)
    place = jnp.array([0, x, y, x | y, 1, x | 1, y | 1, x | y | 1], jnp.int32) ^ me
    names = [0, 1, 2, "o"] + [f"u{c}" for c in range(FF_CHUNKS)]
    layer = Layer(values, order, {name: place for name in names})

    own = jnp.concatenate(layer.head_columns(0), axis=1)
    others = jnp.concatenate(layer.head_columns(1) + layer.head_columns(2) + [layer.out_weight], axis=1)
    units = [layer.unit_columns(c) for c in range(FF_CHUNKS)]
    got = [tp(own, 2), tp(own, 1), tp(own, 3)]
    u2_x, u2_y = dp(units[2], x), dp(units[2], y)
    q0 = interleave([own, *got], HEAD)[None]
    q0_got = [dp(q0, x), dp(q0, y), dp(q0, x | y)]
    others = after(others, q0)
    others = interleave([others, tp(others, 2)], HEAD)
    q0 = [q0, *q0_got]
    q0_core = [dp(value, core) for value in q0]
    others = interleave([others, tp(others, 1)], 128)
    layer.pieces[0] = (q0 + q0_core, None)
    q = jnp.stack([others[:, i * layer.depth : (i + 1) * layer.depth] for i in range(3)])
    q_x, q_y, q1_xy = dp(q, x), dp(q, y), dp(q[:1], x | y)
    u0 = after(units[0], others)
    u0 = stacked(u0, tp(u0, 2))
    u0_near = tp(u0, 1)
    u1_far = tp(after(units[1], u0), 2)

    tie = layer.attend(0, q, u0, u2_x, u2_y, layer.tokens_t)
    q_x, q_y, q1_xy = after(q_x, tie), after(q_y, tie), after(q1_xy, tie)
    q1 = [q[:1], q_x[:1], q_y[:1], q1_xy]
    layer.pieces[1] = (q1 + [dp(value, core) for value in q1], None)
    qo_xy = dp(q_x[1:], y)
    u0 = jnp.concatenate([u0, after(u0_near, tie)])
    u0_x = dp(u0, x)
    u1 = stacked(units[1], after(u1_far, tie))
    u1_near = tp(u1, 1)
    u2_left = stacked(units[2], u2_x)
    u2_xy = dp(after(u2_x, tie), y)
    u2_left_near = tp(after(u2_left, tie), 1)

    tie = layer.attend(1, u0, u1, u2_left)
    qo = [q[1:], q_x[1:], q_y[1:], after(qo_xy, tie)]
    qo = qo + [dp(value, core) for value in qo]
    qo = [value[None] for value in qo]
    layer.pieces[2], layer.pieces["o"] = (qo, 0), (qo, 1)
    u0_x = after(u0_x, tie)
    u0_y = dp(after(u0, u0_x), y)
    u0_core = [dp(after(u0, u0_x), core)]
    u1 = jnp.concatenate([u1, after(u1_near, tie)])
    u1_x = dp(u1, x)
    u2_right = stacked(u2_y, after(u2_xy, tie))
    u2_left_near = after(u2_left_near, tie)
    u2_left_far = tp(after(u2_left, u2_left_near), 2)

    tie = layer.attend(2, u0_x, u1, u2_right, u2_left_near)
    u0_y, u0_core[0] = after(u0_y, tie), after(u0_core[0], tie)
    u0_xy = dp(u0_y, x)
    u0_core += [dp(after(u0_x, tie), core), dp(u0_y, core)]
    u1_x = after(u1_x, tie)
    u1_y = dp(after(u1, u1_x), y)
    u2_left_far = after(u2_left_far, tie)
    u2_right_near = tp(after(u2_right, tie), 1)

    tie = layer.join(u0_y, u1_x, u2_left_far)
    u0_xy = after(u0_xy, tie)
    u0_core = [u0_core[0], *after_all(u0_core[1:], tie), dp(u0_xy, core)]
    layer.pieces["u0"] = ([value[None] for value in [u0, u0_x, u0_y, u0_xy, *u0_core]], "grid")
    u1_y = after(u1_y, tie)
    u1_xy = dp(after(u1_x, u1_y), y)
    u1_core = [dp(after(u1, u1_y), core), dp(after(u1_x, u1_y), core)]
    u2_right_near = after(u2_right_near, tie)
    u2_right_far = tp(after(u2_right, u2_right_near), 2)
    u2_left_both = tp(u2_left_far, 1)

    tie = layer.feed(0, u1_y, u2_right_near)
    u1_xy = after(u1_xy, tie)
    u1_core = after_all(u1_core, tie) + [dp(u1_y, core), dp(u1_xy, core)]
    layer.pieces["u1"] = ([value[None] for value in [u1, u1_x, u1_y, u1_xy, *u1_core]], "grid")
    u2_right_far = after(u2_right_far, tie)
    u2_right_both = tp(u2_right_far, 1)
    u2_left = [u2_left, u2_left_far, u2_left_near, after(u2_left_both, tie)]
    u2_left = jnp.stack(u2_left, axis=1)
    u2_left_core = dp(u2_left, core)

    tie = layer.feed(1, u2_right_far, u2_left)
    u2_right = [u2_right, u2_right_far, u2_right_near, after(u2_right_both, tie)]
    u2_right = jnp.stack(u2_right, axis=1)
    u2_core = [after(u2_left_core, tie), dp(u2_right, core)]
    layer.pieces["u2"] = ([u2_left, u2_right, *u2_core], "grid")
    layer.feed(2)
    layer.turn()

    grads = {}

    def add_core(even, odd, tie, blocks):
        odd = after(odd, tie)
        return [add_low(even[i], odd[i]) for i in blocks]

    even0, odd0, _ = layer.feed_back(0)
    odd0 = dp(odd0, core)

    even1, odd1, tie = layer.feed_back(1)
    f0 = add_core(even0, odd0, tie, range(4))
    f0_first = dp(f0[3], y)
    odd1 = dp(odd1, core)

    even2, odd2, tie = layer.feed_back(2, *f0)
    f0[1] = add_low(f0[1], after(f0_first, tie))
    f0_second = [dp(f0[2], y), dp(f0[1], x)]
    f1 = add_core(even1, odd1, tie, range(4))
    odd2 = dp(odd2, core)

    even_o, odd_o, tie = layer.rejoin(f0[1], *f1)
    f0_second = after_all(f0_second, tie)
    sent = add_three(f0[0][2:], f0_second[0][2:], f0_second[1][2:])
    f0 = add_three(f0[0][:2], f0_second[0][:2], f0_second[1][:2])
    f0_near = tp(sent, 1)
    odd2 = after(odd2, tie)
    f2_sent = [add_low(even2[i : i + 2, 2:], odd2[i : i + 2, 2:]) for i in (0, 2)]
    f2 = [add_low(even2[i : i + 2, :2], odd2[i : i + 2, :2]) for i in (0, 2)]
    f2_left = tp(f2_sent[0], 1)
    odd_o = dp(odd_o, core)

    tie = layer.attend_back_first(0, f0, sent, *f2, *f2_sent)
    f0_near = after(f0_near, tie)
    sent, f0 = add_low(f0[1], f0_near[1]), add_low(f0[0], f0_near[0])
    f0_far = tp(sent, 2)
    f1_first = dp(after(f1[3], tie), x)
    f2_left = after(f2_left, tie)
    f2_left_sent, f2_left = add_low(f2[0][:, 1], f2_left[:, 1]), add_low(f2[0][:, 0], f2_left[:, 0])
    f2_right = tp(after(f2_sent[1], tie), 1)
    o = add_core(even_o, odd_o, tie, range(4))
    o_sent = stacked(o[2], o[3])
    o_first = dp(o_sent, y)

    even_q0, odd_q0, tie = layer.attend_back_second(0, f0, sent, f2_left, f2_left_sent, o_sent, o[0], o[1])
    grads["u0"] = f0.astype(F32) + after(f0_far, tie).astype(F32)
    f1[2] = add_low(f1[2], after(f1_first, tie))
    f1_second = [dp(after(f1[1], tie), x), dp(f1[2], y)]
    f2_right = after(f2_right, tie)
    f2_right_sent, f2_right = add_low(f2[1][:, 1], f2_right[:, 1]), add_low(f2[1][:, 0], f2_right[:, 0])
    f2_left_far = tp(after(f2_left_sent, tie), 2)
    o_first = after(o_first, tie)
    o = [add_low(o[0], o_first[0]), add_low(o[1], o_first[1])]
    o_second = dp(o[1], x)
    odd_q0 = dp(odd_q0, core)

    tie = layer.attend_back_first(1, grads["u0"], f1[2], f2_right, f2_right_sent, *o)
    f1_second = after_all(f1_second, tie)
    sent = add_three(f1[0][2:], f1_second[0][2:], f1_second[1][2:])
    f1 = add_three(f1[0][:2], f1_second[0][:2], f1_second[1][:2])
    f1_near = tp(sent, 1)
    f2_left = add_low(f2_left, after(f2_left_far, tie))
    f2_right_far = tp(after(f2_right_sent, tie), 2)
    o_sent, o = halves(add_low(o[0], after(o_second, tie)), 128)
    o_near = tp(o_sent, 1)
    q0 = add_core(even_q0, odd_q0, tie, range(4))
    q0_sent = stacked(q0[1], q0[3])
    q0_first = dp(q0_sent, x)

    even_q1, odd_q1, tie = layer.attend_back_second(1, f1, sent, f2_left, o, o_sent, q0_sent, q0[0], q0[2])
    f1_near = after(f1_near, tie)
    sent, f1 = add_low(f1[1], f1_near[1]), add_low(f1[0], f1_near[0])
    f1_far = tp(sent, 2)
    f2_right = add_low(f2_right, after(f2_right_far, tie))
    f2_first = dp(f2_right, y)
    o_sent, o = halves(add_low(o, after(o_near, tie)), HEAD)
    o_far = tp(o_sent, 2)
    q0_first = after(q0_first, tie)
    q0 = [add_low(q0[0], q0_first[0]), add_low(q0[2], q0_first[1])]
    q0_second = dp(q0[1], y)
    odd_q1 = dp(odd_q1, core)

    tie = layer.attend_back_first(2, f1, sent, f2_right, o, o_sent, *q0)
    grads["u1"] = f1.astype(F32) + after(f1_far, tie).astype(F32)
    f2_first = after(f2_first, tie)
    f2 = [add_low(f2_left[0], f2_first[0]), add_low(f2_left[1], f2_first[1])]
    f2_second = dp(f2[1], x)
    grads["o"] = o.astype(F32) + after(o_far, tie).astype(F32)
    q0_sent, q0 = halves(add_low(q0[0], after(q0_second, tie)), 128)
    q0_near = tp(q0_sent, 1)
    q1 = add_core(even_q1, odd_q1, tie, range(4))
    q1_sent = stacked(q1[2], q1[3])
    q1_first = dp(q1_sent, y)

    even_q2, odd_q2, tie = layer.attend_back_second(
        2, grads["u1"], grads["o"], *f2, q0, q0_sent, q1_sent, q1[0], q1[1]
    )
    odd_q2 = dp(odd_q2, core)
    sums = layer.small_sums(back)
    sums_got = dp(sums, core)
    q0_sent, q0 = halves(add_low(q0, after(q0_near, tie)), HEAD)
    q0_far = tp(q0_sent, 2)
    q1_first = after(q1_first, tie)
    q1 = [add_low(q1[0], q1_first[0]), add_low(q1[1], q1_first[1])]
    q1_second = dp(q1[1], x)
    grads["u2"] = f2[0].astype(F32) + after(f2_second, tie).astype(F32)

    tie = q1
    q2 = add_core(even_q2, odd_q2, tie, range(4))
    q2_got = [dp(q2[1], x), dp(q2[2], y), dp(q2[3], x | y)]
    sums = sums + after(sums_got, tie)
    sums_got = dp(sums, x)
    q1_sent, q1 = halves(add_low(q1[0], after(q1_second, tie)), 128)
    q1_near = tp(q1_sent, 1)
    tie = [q1, sums]
    grads[0] = q0.astype(F32) + after(q0_far, tie).astype(F32)
    sums = sums + after(sums_got, tie)
    sums_got = dp(sums, y)
    q1_sent, q1 = halves(add_low(q1, after(q1_near, tie)), HEAD)
    q1_far = tp(q1_sent, 2)
    tie = [q1, sums]
    q2 = four(q2[0], *after_all(q2_got, tie)).astype(BF16)
    q2 = [pick(q2, HEAD, i) for i in range(4)]
    q2_got = [tp(q2[1], 2), tp(q2[2], 1), tp(q2[3], 3)]
    sums = sums + after(sums_got, tie)
    sums_got = tp(sums, 1)
    tie = [sums, *q2]
    grads[1] = q1.astype(F32) + after(q1_far, tie).astype(F32)
    sums = sums + after(sums_got, tie)
    sums_got = tp(sums, 2)
    grads[2] = four(q2[0], q2_got[1], q2_got[0], q2_got[2])
    return layer.outputs(grads, sums + sums_got)


def local(suits, *values):
    return paired(*values) if suits else plain(*values)


def solution(mesh):
    rows_all = P(("dp", "tensor"), None)
    columns_3d = P("dp", None, "tensor")
    columns_2d = P("dp", "tensor")
    return jax.shard_map(
        functools.partial(local, dict(mesh.shape) == {"dp": 8, "tensor": 4}),
        mesh=mesh,
        in_specs=(
            rows_all,
            columns_3d,
            P(),
            columns_2d,
            P(),
            P(),
            P(),
            columns_3d,
            columns_2d,
            P(),
            P(),
            P(),
            rows_all,
        ),
        out_specs=(
            rows_all,
            rows_all,
            columns_3d,
            P(),
            columns_2d,
            P(),
            P(),
            P(),
            columns_3d,
            columns_2d,
            P(),
            P(),
            P(),
        ),
        check_vma=False,
    )
```

time: 570 us -> 463 us (0.81)
  waiting for transfers between devices: 157 us -> 83.1 us
  Pallas kernels: 260 us -> 220 us
  other arithmetic: 28.6 us -> 35.4 us
    ppermute x97 -> x99, waiting for transfers between devices: 157 us -> 83.1 us  [the longest x65 41.8 us: dp(): return lax.ppermute(value, 'dp', [(i, i ^ bit) for i in range(8)])]
    pallas_call x14 -> x17, Pallas kernels: 250 us -> 211 us  [the longest x3 56.9 us: feed_back(): pl.pallas_call(functools.partial(feed_back_kernel, len(pieces[0])), grid=...]
    another operation x10 -> x17, other arithmetic: 1.67 us -> 8.7 us  [the longest x2 2.94 us: paired(): u2_right = jnp.stack(u2_right, axis=1)]
    ppermute x97 -> x99, starting transfers between devices: 79.5 us -> 84.1 us  [the longest x65 43.2 us: dp(): return lax.ppermute(value, 'dp', [(i, i ^ bit) for i in range(8)])]
    convert_element_type x33 -> x27, other arithmetic: 18.2 us -> 15.1 us  [add_low(): return (left.astype(F32) + right.astype(F32)).astype(BF16)]
  transfers between devices with their start and end apart: 97 -> 99, of which waited for: 40 -> 21; matrix products, arithmetic and copies ran while one was open for 10% -> 13% of each run, Pallas kernels for 15% -> 39%
where the time goes in v3:
time: 463 us; the launch traced here: 459 us
  Pallas kernels  220 us (48%)
  starting transfers between devices  84.1 us (18%)
  waiting for transfers between devices  83.1 us (18%)
  other arithmetic  35.4 us (8%)
  local copies, waits for them, and re-layouts  33.8 us (7%)
    pallas_call x3, Pallas kernels, feed_back(): pl.pallas_call(functools.partial(feed_back_kernel, len(pieces[0])), grid=...  56.9 us
    ppermute x65, starting transfers between devices, dp(): return lax.ppermute(value, 'dp', [(i, i ^ bit) for i in range(8)])  43.2 us
    ppermute x65, waiting for transfers between devices, dp(): return lax.ppermute(value, 'dp', [(i, i ^ bit) for i in range(8)])  41.8 us
    ppermute x34, waiting for transfers between devices, tp(): return lax.ppermute(value, 'tensor', [(i, i ^ bit) for i in range(4)])  41.3 us
    ppermute x34, starting transfers between devices, tp(): return lax.ppermute(value, 'tensor', [(i, i ^ bit) for i in range(4)])  40.9 us
    pallas_call x3, Pallas kernels, attend_backward_second(): pl.pallas_call(functools.partial(attend_back_second, group * GROUP, len(p...  40.3 us
    pallas_call x3, Pallas kernels, feed(): pl.pallas_call(functools.partial(feed_kernel, first, len(pieces[0])), gri...  35.3 us
    pallas_call x3, Pallas kernels, attend_forward(): pl.pallas_call(functools.partial(attend_kernel, group * GROUP, len(pieces...  34.2 us
  transfers between devices with their start and end apart: 99, of which 21 were waited for; matrix products, arithmetic and copies ran while one was open for 13% of the time, Pallas kernels for 39%

profile of v3, /device:TPU:0, one launch (start us, length us, event | category | flops | bytes accessed | tf_op | source)
XLA Modules:
  0.0 458.9 jit_solution(9498261238687363694)
XLA Ops:
  1.8 4.1 collective-permute-start.2
  5.9 1.6 collective-permute-start.3
  8.8 2.0 collective-permute-start
  16.9 1.6 collective-permute-start.10
  18.5 5.5 %collective-permute-done.5 = bf16[96,576]{1,0:T(8,128)(2,1)S(1)} collective-permute-done((bf16[96,576]{1,0:T(8,128)(2,1)S(1)}, bf16[96,576]{1,0:T(8,128)(2,1)S(1)}, u32[]{:S(2)}, u32[]{:S(2)}) %collective-permute-start.5) | collective-permute-done | bytes 110624 | tf_op jit(solution)/shard_map/ppermute | solution.py:831
  30.2 1.7 collective-permute-done.6
  36.7 2.5 collective-permute-start.17
  39.2 1.6 collective-permute-start.18
  43.4 2.1 copy.59
  46.9 11.2 %attend_forward.3 = (bf16[1024,768]{1,0:T(8,128)(2,1)}, bf16[1024,256]{1,0:T(8,128)(2,1)}, f32[4,1024]{1,0:T(4,128)}) custom-call(s32[8]{0:T(128)} %broadcast_xor_fusion.place_ref, f32[12]{0:T(128)} %reshape.245.slope_ref, bf16[1024,768]{1,0:T(8,128)(2,1)} %x_ref.3, f32[1,768]{1,0:T(1,128)} %get-tuple-element.544.bias_ref, bf16[1,96,768]{2,1,0:T(8,128)(2,1)} %bitcast.269, ...), custom_call_target="tpu_custom_call" | custom-call | flops 1048576 | bytes 65536 | tf_op jit(solution)/shard_map/attend_forward/pallas_call | solution.py:136
  58.3 2.1 fusion.51
  64.7 1.7 fusion.53
  68.7 1.8 collective-permute-start.28
  71.1 11.4 %attend_forward.4 = (bf16[1024,768]{1,0:T(8,128)(2,1)}, bf16[1024,256]{1,0:T(8,128)(2,1)}, f32[4,1024]{1,0:T(4,128)}) custom-call(s32[8]{0:T(128)} %broadcast_xor_fusion.place_ref, f32[12]{0:T(128)} %reshape.245.slope_ref, bf16[1024,768]{1,0:T(8,128)(2,1)} %x_ref.3, f32[1,768]{1,0:T(1,128)} %get-tuple-element.543.bias_ref, bf16[1,96,768]{2,1,0:T(8,128)(2,1)} %bitcast.257, ...), custom_call_target="tpu_custom_call" | custom-call | flops 1048576 | bytes 65536 | tf_op jit(solution)/shard_map/attend_forward/pallas_call | solution.py:136
  86.3 1.7 fusion.52
  88.0 14.4 %collective-permute-done.27 = bf16[96,768]{1,0:T(8,128)(2,1)S(1)} collective-permute-done((bf16[96,768]{1,0:T(8,128)(2,1)S(1)}, bf16[96,768]{1,0:T(8,128)(2,1)S(1)}, u32[]{:S(2)}, u32[]{:S(2)}) %collective-permute-start.27) | collective-permute-done | bytes 147488 | tf_op jit(solution)/shard_map/ppermute | solution.py:828
  103.8 1.8 fusion.48
  106.5 11.5 %attend_forward.5 = (bf16[1024,768]{1,0:T(8,128)(2,1)}, bf16[1024,256]{1,0:T(8,128)(2,1)}, f32[4,1024]{1,0:T(4,128)}) custom-call(s32[8]{0:T(128)} %broadcast_xor_fusion.place_ref, f32[12]{0:T(128)} %reshape.245.slope_ref, bf16[1024,768]{1,0:T(8,128)(2,1)} %x_ref.3, f32[1,768]{1,0:T(1,128)} %get-tuple-element.542.bias_ref, ...), custom_call_target="tpu_custom_call" | custom-call | flops 1048576 | bytes 65536 | tf_op jit(solution)/shard_map/attend_forward/pallas_call | solution.py:136
  118.1 1.6 collective-permute-start.39
  120.5 1.7 collective-permute-start.36
  124.8 11.3 %collective-permute-done.35 = bf16[2,96,768]{2,1,0:T(8,128)(2,1)} collective-permute-done((bf16[2,96,768]{2,1,0:T(8,128)(2,1)}, bf16[2,96,768]{2,1,0:T(8,128)(2,1)}, u32[]{:S(2)}, u32[]{:S(2)}) %collective-permute-start.35) | collective-permute-done | bytes 294944 | tf_op jit(solution)/shard_map/ppermute | solution.py:831
  136.1 7.2 %join.1 = (f32[1024,768]{1,0:T(8,128)}, f32[1024,128]{1,0:T(8,128)}, bf16[1024,768]{1,0:T(8,128)(2,1)}, bf16[768,1024]{1,0:T(8,128)(2,1)}) custom-call(s32[8]{0:T(128)} %broadcast_xor_fusion.place_ref, bf16[1024,768]{1,0:T(8,128)(2,1)} %x_ref.3, f32[8,768]{1,0:T(8,128)} %stack.153.vec_ref, bf16[1024,256]{1,0:T(8,128)(2,1)} %get-tuple-element.200.rest_0_, ...), custom_call_target="tpu_custom_call" | custom-call | flops 1048576 | bytes 65536 | tf_op jit(solution)/shard_map/join/pallas_call | solution.py:350
  147.3 11.1 %feed.3 = (f32[1024,768]{1,0:T(8,128)}, bf16[1024,1024]{1,0:T(8,128)(2,1)}, bf16[1024,1024]{1,0:T(8,128)(2,1)}, bf16[1024,1024]{1,0:T(8,128)(2,1)}) custom-call(s32[8]{0:T(128)} %broadcast_xor_fusion.place_ref, bf16[1024,768]{1,0:T(8,128)(2,1)} %get-tuple-element.219.low_ref, bf16[1,4,96,768]{3,2,1,0:T(8,128)(2,1)} %get-tuple-element.409.rest_0_, ...), custom_call_target="tpu_custom_call" | custom-call | flops 1048576 | bytes 65536 | tf_op jit(solution)/shard_map/feed/pallas_call | solution.py:491
  161.2 9.2 %collective-permute-done.44 = bf16[2,96,768]{2,1,0:T(8,128)(2,1)S(1)} collective-permute-done((bf16[2,96,768]{2,1,0:T(8,128)(2,1)}, bf16[2,96,768]{2,1,0:T(8,128)(2,1)S(1)}, u32[]{:S(2)}, u32[]{:S(2)}) %collective-permute-start.44) | collective-permute-done | bytes 294944 | tf_op jit(solution)/shard_map/ppermute | solution.py:831
  173.2 12.1 %feed.4 = (f32[1024,768]{1,0:T(8,128)}, bf16[1024,1024]{1,0:T(8,128)(2,1)}, bf16[1024,1024]{1,0:T(8,128)(2,1)}, bf16[1024,1024]{1,0:T(8,128)(2,1)}) custom-call(s32[8]{0:T(128)} %broadcast_xor_fusion.place_ref, bf16[1024,768]{1,0:T(8,128)(2,1)} %get-tuple-element.219.low_ref, f32[1024,768]{1,0:T(8,128)} %get-tuple-element.216.rest_0_, ...), custom_call_target="tpu_custom_call" | custom-call | flops 1048576 | bytes 65536 | tf_op jit(solution)/shard_map/feed/pallas_call | solution.py:491
  188.0 2.4 copy.70.rest_3_.rest_2_
  191.4 12.2 %feed.5 = (f32[1024,768]{1,0:T(8,128)}, bf16[1024,1024]{1,0:T(8,128)(2,1)}, bf16[1024,1024]{1,0:T(8,128)(2,1)}, bf16[1024,1024]{1,0:T(8,128)(2,1)}) custom-call(s32[8]{0:T(128)} %broadcast_xor_fusion.place_ref, bf16[1024,768]{1,0:T(8,128)(2,1)} %get-tuple-element.219.low_ref, f32[1024,768]{1,0:T(8,128)} %get-tuple-element.225.rest_0_, ...), custom_call_target="tpu_custom_call" | custom-call | flops 1048576 | bytes 65536 | tf_op jit(solution)/shard_map/feed/pallas_call | solution.py:491
  203.5 9.1 %turn.1 = (bf16[1024,768]{1,0:T(8,128)(2,1)}, f32[1024,768]{1,0:T(8,128)}, bf16[1024,768]{1,0:T(8,128)(2,1)}, bf16[768,1024]{1,0:T(8,128)(2,1)}, f32[3,768]{1,0:T(4,128)}) custom-call(f32[1024,768]{1,0:T(8,128)} %get-tuple-element.228.ffn_ref, f32[1024,768]{1,0:T(8,128)} %get-tuple-element.229.normed1_ref.normed_ref, bf16[1024,768]{1,0:T(8,128)(2,1)} %cot_ref.1, ...), custom_call_target="tpu_custom_call" | custom-call | flops 1048576 | bytes 65536 | tf_op jit(solution)/shard_map/turn/pallas_call | solution.py:386
  212.6 18.9 %feed_back.3 = (f32[1024,768]{1,0:T(8,128)}, bf16[4,4,96,768]{3,2,1,0:T(8,128)(2,1)}, bf16[4,4,96,768]{3,2,1,0:T(8,128)(2,1)}) custom-call(s32[8]{0:T(128)} %broadcast_xor_fusion.place_ref, bf16[1024,768]{1,0:T(8,128)(2,1)} %get-tuple-element.232.d_ref, bf16[768,1024]{1,0:T(8,128)(2,1)} %get-tuple-element.233.d_t_ref, ...), custom_call_target="tpu_custom_call" | custom-call | flops 1048576 | bytes 65536 | tf_op jit(solution)/shard_map/feed_back/pallas_call | solution.py:539
  231.8 19.2 %feed_back.4 = (f32[1024,768]{1,0:T(8,128)}, bf16[4,4,96,768]{3,2,1,0:T(8,128)(2,1)}, bf16[4,4,96,768]{3,2,1,0:T(8,128)(2,1)}) custom-call(s32[8]{0:T(128)} %broadcast_xor_fusion.place_ref, bf16[1024,768]{1,0:T(8,128)(2,1)} %get-tuple-element.232.d_ref, bf16[768,1024]{1,0:T(8,128)(2,1)} %get-tuple-element.233.d_t_ref, ...), custom_call_target="tpu_custom_call" | custom-call | flops 1048576 | bytes 65536 | tf_op jit(solution)/shard_map/feed_back/pallas_call | solution.py:539
  251.4 1.7 add_convert_fusion.6
  253.1 18.8 %feed_back.5 = (f32[1024,768]{1,0:T(8,128)}, bf16[4,4,96,768]{3,2,1,0:T(8,128)(2,1)}, bf16[4,4,96,768]{3,2,1,0:T(8,128)(2,1)}) custom-call(s32[8]{0:T(128)} %broadcast_xor_fusion.place_ref, bf16[1024,768]{1,0:T(8,128)(2,1)} %get-tuple-element.232.d_ref, bf16[768,1024]{1,0:T(8,128)(2,1)} %get-tuple-element.233.d_t_ref, ...), custom_call_target="tpu_custom_call" | custom-call | flops 1048576 | bytes 65536 | tf_op jit(solution)/shard_map/feed_back/pallas_call | solution.py:539
  274.3 14.1 %collective-permute-done.54 = bf16[4,96,768]{2,1,0:T(8,128)(2,1)S(1)} collective-permute-done((bf16[4,96,768]{2,1,0:T(8,128)(2,1)S(1)}, bf16[4,96,768]{2,1,0:T(8,128)(2,1)S(1)}, u32[]{:S(2)}, u32[]{:S(2)}) %collective-permute-start.54) | collective-permute-done | bytes 589856 | tf_op jit(solution)/shard_map/ppermute | solution.py:828
  290.7 8.8 %rejoin.1 = (f32[1024,768]{1,0:T(8,128)}, bf16[1024,768]{1,0:T(8,128)(2,1)}, bf16[4,96,768]{2,1,0:T(8,128)(2,1)}, bf16[4,96,768]{2,1,0:T(8,128)(2,1)}, f32[3,768]{1,0:T(4,128)}) custom-call(s32[8]{0:T(128)} %broadcast_xor_fusion.place_ref, f32[1024,768]{1,0:T(8,128)} %get-tuple-element.256.d_hidden_ref, ...), custom_call_target="tpu_custom_call" | custom-call | flops 1048576 | bytes 65536 | tf_op jit(solution)/shard_map/rejoin/pallas_call | solution.py:428
  300.5 3.2 collective-permute-done.57
  303.7 1.6 fusion.12
  305.3 1.8 collective-permute-start.59
  307.1 2.7 add_convert_fusion.3
  311.4 9.5 %attend_backward_first.3 = (bf16[1024,384]{1,0:T(8,128)(2,1)}, f32[2,128]{1,0:T(2,128)}) custom-call(f32[12]{0:T(128)} %reshape.245.slope_ref, bf16[1024,768]{1,0:T(8,128)(2,1)} %get-tuple-element.265.qkv_ref, f32[4,1024]{1,0:T(4,128)} %get-tuple-element.176.lse_ref, bf16[1024,768]{1,0:T(8,128)(2,1)} %get-tuple-element.299.dctx_ref), custom_call_target="tpu_custom_call" | custom-call | flops 1048576 | bytes 65536 | tf_op jit(solution)/shard_map/attend_backward_first/pallas_call | solution.py:245
  322.0 2.5 collective-permute-start.60
  326.4 3.1 collective-permute-done.61
  329.5 1.9 fusion.16
  331.4 13.3 %attend_backward_second.3 = (bf16[4,96,768]{2,1,0:T(8,128)(2,1)}, bf16[4,96,768]{2,1,0:T(8,128)(2,1)}, f32[2,128]{1,0:T(2,128)}, f32[1024,768]{1,0:T(8,128)}) custom-call(s32[8]{0:T(128)} %broadcast_xor_fusion.place_ref, f32[12]{0:T(128)} %reshape.245.slope_ref, bf16[1024,768]{1,0:T(8,128)(2,1)} %get-tuple-element.265.qkv_ref, ...), custom_call_target="tpu_custom_call" | custom-call | flops 1048576 | bytes 65536 | tf_op jit(solution)/shard_map/attend_backward_second/pallas_call | solution.py:269
  347.4 1.7 collective-permute-start.66
  349.6 9.3 %attend_backward_first.4 = (bf16[1024,384]{1,0:T(8,128)(2,1)}, f32[2,128]{1,0:T(2,128)}) custom-call(f32[12]{0:T(128)} %reshape.245.slope_ref, bf16[1024,768]{1,0:T(8,128)(2,1)} %get-tuple-element.282.qkv_ref, f32[4,1024]{1,0:T(4,128)} %get-tuple-element.184.lse_ref, bf16[1024,768]{1,0:T(8,128)(2,1)} %get-tuple-element.299.dctx_ref), custom_call_target="tpu_custom_call" | custom-call | flops 1048576 | bytes 65536 | tf_op jit(solution)/shard_map/attend_backward_first/pallas_call | solution.py:245
  359.7 2.4 collective-permute-start.72
  365.8 2.1 collective-permute-start.68
  368.5 13.5 %attend_backward_second.4 = (bf16[4,96,768]{2,1,0:T(8,128)(2,1)}, bf16[4,96,768]{2,1,0:T(8,128)(2,1)}, f32[2,128]{1,0:T(2,128)}, f32[1024,768]{1,0:T(8,128)}) custom-call(s32[8]{0:T(128)} %broadcast_xor_fusion.place_ref, f32[12]{0:T(128)} %reshape.245.slope_ref, bf16[1024,768]{1,0:T(8,128)(2,1)} %get-tuple-element.282.qkv_ref, ...), custom_call_target="tpu_custom_call" | custom-call | flops 1048576 | bytes 65536 | tf_op jit(solution)/shard_map/attend_backward_second/pallas_call | solution.py:269
  385.5 2.1 collective-permute-start.75
  388.3 9.1 %attend_backward_first.5 = (bf16[1024,384]{1,0:T(8,128)(2,1)}, f32[2,128]{1,0:T(2,128)}) custom-call(f32[12]{0:T(128)} %reshape.245.slope_ref, bf16[1024,768]{1,0:T(8,128)(2,1)} %get-tuple-element.231.qkv_ref, f32[4,1024]{1,0:T(4,128)} %get-tuple-element.194.lse_ref, bf16[1024,768]{1,0:T(8,128)(2,1)} %get-tuple-element.299.dctx_ref), custom_call_target="tpu_custom_call" | custom-call | flops 1048576 | bytes 65536 | tf_op jit(solution)/shard_map/attend_backward_first/pallas_call | solution.py:245
  397.5 1.7 collective-permute-start.98
  401.2 1.6 collective-permute-start.82
  402.8 13.6 %attend_backward_second.5 = (bf16[4,96,768]{2,1,0:T(8,128)(2,1)}, bf16[4,96,768]{2,1,0:T(8,128)(2,1)}, f32[2,128]{1,0:T(2,128)}, bf16[1024,768]{1,0:T(8,128)(2,1)}) custom-call(s32[8]{0:T(128)} %broadcast_xor_fusion.place_ref, f32[12]{0:T(128)} %reshape.245.slope_ref, bf16[1024,768]{1,0:T(8,128)(2,1)} %get-tuple-element.231.qkv_ref, ...), custom_call_target="tpu_custom_call" | custom-call | flops 1048576 | bytes 65536 | tf_op jit(solution)/shard_map/attend_backward_second/pallas_call | solution.py:269
  418.7 2.9 collective-permute-start.81
  424.3 1.8 collective-permute-start.87
  426.1 3.7 collective-permute-done.83
  430.7 3.6 collective-permute-done.85
  436.3 1.7 collective-permute-start.90
  438.1 2.6 collective-permute-done.92
  443.9 3.0 collective-permute-start.93
  447.0 1.9 collective-permute-start.96
  449.5 2.5 collective-permute-done.86
  452.3 1.5 collective-permute-start.97
  454.7 2.5 collective-permute-done.97
  (475 shorter events, 92.4 us)
Async XLA Ops:
  1.8 12.8 %collective-permute-start.2 = (bf16[96,192]{1,0:T(8,128)(2,1)S(1)}, bf16[96,192]{1,0:T(8,128)(2,1)S(1)}, u32[]{:S(2)}, u32[]{:S(2)}) collective-permute-start(bf16[96,192]{1,0:T(8,128)(2,1)S(1)} %pad_maximum_fusion.25), channel_id=1, source_target_pairs={{0,2},{1,3},{2,0},{3,1},{4,6},{5,7},{6,4},{7,5},{8,10},{9,11},{10,... | collective-permute-start | bytes 110600 | tf_op jit(solution)/shard_map/ppermute | solution.py:831
  8.8 17.1 %collective-permute-start = (bf16[96,768]{1,0:T(8,128)(2,1)S(1)}, bf16[96,768]{1,0:T(8,128)(2,1)S(1)}, u32[]{:S(2)}, u32[]{:S(2)}) collective-permute-start(bf16[96,768]{1,0:T(8,128)(2,1)S(1)} %pad_maximum_fusion.16), channel_id=1, source_target_pairs={{0,2},{1,3},{2,0},{3,1},{4,6},{5,7},{6,4},{7,5},{8,10},{9,11},{10,... | collective-permute-start | bytes 442376 | tf_op jit(solution)/shard_map/ppermute | solution.py:831
  11.5 16.7 %collective-permute-start.7 = (bf16[96,768]{1,0:T(8,128)(2,1)}, bf16[96,768]{1,0:T(8,128)(2,1)S(1)}, u32[]{:S(2)}, u32[]{:S(2)}) collective-permute-start(bf16[96,768]{1,0:T(8,128)(2,1)} %get-tuple-element.482), channel_id=1, source_target_pairs={{0,8},{4,12},{8,0},{12,4},{16,24},{20,28},{24,16},{28,20},{1,9},{5... | collective-permute-start | bytes 442376 | tf_op jit(solution)/shard_map/ppermute | solution.py:828
  16.4 13.3 %collective-permute-start.9 = (bf16[1,96,768]{2,1,0:T(8,128)(2,1)S(1)}, bf16[1,96,768]{2,1,0:T(8,128)(2,1)S(1)}, u32[]{:S(2)}, u32[]{:S(2)}) collective-permute-start(bf16[1,96,768]{2,1,0:T(8,128)(2,1)S(1)} %bitcast.265), channel_id=1, source_target_pairs={{0,8},{4,12},{8,0},{12,4},{16,24},{20,28},{24,16},{28,20},{1,9},{5... | collective-permute-start | bytes 442376 | tf_op jit(solution)/shard_map/ppermute | solution.py:828
  16.9 12.8 %collective-permute-start.10 = (bf16[1,96,768]{2,1,0:T(8,128)(2,1)S(1)}, bf16[1,96,768]{2,1,0:T(8,128)(2,1)S(1)}, u32[]{:S(2)}, u32[]{:S(2)}) collective-permute-start(bf16[1,96,768]{2,1,0:T(8,128)(2,1)S(1)} %bitcast.266), channel_id=1, source_target_pairs={{0,16},{4,20},{8,24},{12,28},{16,0},{20,4},{24,8},{28,12},{1,17},{... | collective-permute-start | bytes 442376 | tf_op jit(solution)/shard_map/ppermute | solution.py:828
  36.2 22.1 %collective-permute-start.1 = (bf16[2,96,768]{2,1,0:T(8,128)(2,1)}, bf16[2,96,768]{2,1,0:T(8,128)(2,1)}, u32[]{:S(2)}, u32[]{:S(2)}) collective-permute-start(bf16[2,96,768]{2,1,0:T(8,128)(2,1)} %pad_maximum_fusion.6), channel_id=1, source_target_pairs={{0,1},{1,0},{2,3},{3,2},{4,5},{5,4},{6,7},{7,6},{8,9},{9,8},{10,11... | collective-permute-start | bytes 884744 | tf_op jit(solution)/shard_map/ppermute | solution.py:831
  36.7 21.5 %collective-permute-start.17 = (bf16[96,768]{1,0:T(8,128)(2,1)}, bf16[96,768]{1,0:T(8,128)(2,1)S(1)}, u32[]{:S(2)}, u32[]{:S(2)}) collective-permute-start(bf16[96,768]{1,0:T(8,128)(2,1)} %get-tuple-element.178), channel_id=1, source_target_pairs={{0,2},{1,3},{2,0},{3,1},{4,6},{5,7},{6,4},{7,5},{8,10},{9,11},{10,... | collective-permute-start | bytes 442376 | tf_op jit(solution)/shard_map/ppermute | solution.py:831
  39.2 22.9 %collective-permute-start.18 = (bf16[3,96,768]{2,1,0:T(8,128)(2,1)}, bf16[3,96,768]{2,1,0:T(8,128)(2,1)}, u32[]{:S(2)}, u32[]{:S(2)}) collective-permute-start(bf16[3,96,768]{2,1,0:T(8,128)(2,1)} %pad_maximum_fusion.5), channel_id=1, source_target_pairs={{0,8},{4,12},{8,0},{12,4},{16,24},{20,28},{24,16},{28,20},{1,9},{5... | collective-permute-start | bytes 1327112 | tf_op jit(solution)/shard_map/ppermute | solution.py:828
  40.8 22.2 %collective-permute-start.19 = (bf16[3,96,768]{2,1,0:T(8,128)(2,1)}, bf16[3,96,768]{2,1,0:T(8,128)(2,1)}, u32[]{:S(2)}, u32[]{:S(2)}) collective-permute-start(bf16[3,96,768]{2,1,0:T(8,128)(2,1)} %pad_maximum_fusion.5), channel_id=1, source_target_pairs={{0,16},{4,20},{8,24},{12,28},{16,0},{20,4},{24,8},{28,12},{1,17},{... | collective-permute-start | bytes 1327112 | tf_op jit(solution)/shard_map/ppermute | solution.py:828
  46.3 15.4 %collective-permute-start.20 = (bf16[1,96,768]{2,1,0:T(8,128)(2,1)S(1)}, bf16[1,96,768]{2,1,0:T(8,128)(2,1)S(1)}, u32[]{:S(2)}, u32[]{:S(2)}) collective-permute-start(bf16[1,96,768]{2,1,0:T(8,128)(2,1)S(1)} %bitcast.255), channel_id=1, source_target_pairs={{0,24},{4,28},{8,16},{12,20},{16,8},{20,12},{24,0},{28,4},{1,25},{... | collective-permute-start | bytes 442376 | tf_op jit(solution)/shard_map/ppermute | solution.py:828
  60.3 23.9 %collective-permute-start.16 = (bf16[4,96,768]{2,1,0:T(8,128)(2,1)}, bf16[4,96,768]{2,1,0:T(8,128)(2,1)S(1)}, u32[]{:S(2)}, u32[]{:S(2)}) collective-permute-start(bf16[4,96,768]{2,1,0:T(8,128)(2,1)} %get-tuple-element.186), channel_id=1, source_target_pairs={{0,8},{4,12},{8,0},{12,4},{16,24},{20,28},{24,16},{28,20},{1,9},{5... | collective-permute-start | bytes 1769480 | tf_op jit(solution)/shard_map/ppermute | solution.py:828
  61.7 20.8 %collective-permute-start.26 = (bf16[2,96,768]{2,1,0:T(8,128)(2,1)S(1)}, bf16[2,96,768]{2,1,0:T(8,128)(2,1)S(1)}, u32[]{:S(2)}, u32[]{:S(2)}) collective-permute-start(bf16[2,96,768]{2,1,0:T(8,128)(2,1)S(1)} %pad_maximum_fusion.7), channel_id=1, source_target_pairs={{0,1},{1,0},{2,3},{3,2},{4,5},{5,4},{6,7},{7,6},{8,9},{9,8},{10,11... | collective-permute-start | bytes 884744 | tf_op jit(solution)/shard_map/ppermute | solution.py:831
  66.4 18.5 %collective-permute-start.29 = (bf16[2,96,768]{2,1,0:T(8,128)(2,1)S(1)}, bf16[2,96,768]{2,1,0:T(8,128)(2,1)S(1)}, u32[]{:S(2)}, u32[]{:S(2)}) collective-permute-start(bf16[2,96,768]{2,1,0:T(8,128)(2,1)S(1)} %get-tuple-element.413), channel_id=1, source_target_pairs={{0,16},{4,20},{8,24},{12,28},{16,0},{20,4},{24,8},{28,12},{1,17},{... | collective-permute-start | bytes 884744 | tf_op jit(solution)/shard_map/ppermute | solution.py:828
  68.7 33.8 %collective-permute-start.28 = (bf16[2,96,768]{2,1,0:T(8,128)(2,1)}, bf16[2,96,768]{2,1,0:T(8,128)(2,1)S(1)}, u32[]{:S(2)}, u32[]{:S(2)}) collective-permute-start(bf16[2,96,768]{2,1,0:T(8,128)(2,1)} %get-tuple-element.197), channel_id=1, source_target_pairs={{0,1},{1,0},{2,3},{3,2},{4,5},{5,4},{6,7},{7,6},{8,9},{9,8},{10,11... | collective-permute-start | bytes 884744 | tf_op jit(solution)/shard_map/ppermute | solution.py:831
  70.5 33.2 %collective-permute-start.30 = (bf16[2,96,768]{2,1,0:T(8,128)(2,1)S(1)}, bf16[2,96,768]{2,1,0:T(8,128)(2,1)S(1)}, u32[]{:S(2)}, u32[]{:S(2)}) collective-permute-start(bf16[2,96,768]{2,1,0:T(8,128)(2,1)S(1)} %get-tuple-element.434), channel_id=1, source_target_pairs={{0,4},{4,0},{8,12},{12,8},{16,20},{20,16},{24,28},{28,24},{1,5},{5... | collective-permute-start | bytes 884744 | tf_op jit(solution)/shard_map/ppermute | solution.py:828
  83.7 34.4 %collective-permute-start.34 = (bf16[4,96,768]{2,1,0:T(8,128)(2,1)}, bf16[4,96,768]{2,1,0:T(8,128)(2,1)S(1)}, u32[]{:S(2)}, u32[]{:S(2)}) collective-permute-start(bf16[4,96,768]{2,1,0:T(8,128)(2,1)} %get-tuple-element.222), channel_id=1, source_target_pairs={{0,8},{4,12},{8,0},{12,4},{16,24},{20,28},{24,16},{28,20},{1,9},{5... | collective-permute-start | bytes 1769480 | tf_op jit(solution)/shard_map/ppermute | solution.py:828
  84.2 33.8 %collective-permute-start.25 = (bf16[4,96,768]{2,1,0:T(8,128)(2,1)}, bf16[4,96,768]{2,1,0:T(8,128)(2,1)S(1)}, u32[]{:S(2)}, u32[]{:S(2)}) collective-permute-start(bf16[4,96,768]{2,1,0:T(8,128)(2,1)} %get-tuple-element.186), channel_id=1, source_target_pairs={{0,16},{4,20},{8,24},{12,28},{16,0},{20,4},{24,8},{28,12},{1,17},{... | collective-permute-start | bytes 1769480 | tf_op jit(solution)/shard_map/ppermute | solution.py:828
  84.9 17.5 %collective-permute-start.27 = (bf16[96,768]{1,0:T(8,128)(2,1)S(1)}, bf16[96,768]{1,0:T(8,128)(2,1)S(1)}, u32[]{:S(2)}, u32[]{:S(2)}) collective-permute-start(bf16[96,768]{1,0:T(8,128)(2,1)S(1)} %copy-done.67), channel_id=1, source_target_pairs={{0,16},{4,20},{8,24},{12,28},{16,0},{20,4},{24,8},{28,12},{1,17},{... | collective-permute-start | bytes 442376 | tf_op jit(solution)/shard_map/ppermute | solution.py:828
  118.1 25.3 %collective-permute-start.39 = (bf16[4,96,768]{2,1,0:T(8,128)(2,1)S(1)}, bf16[4,96,768]{2,1,0:T(8,128)(2,1)S(1)}, u32[]{:S(2)}, u32[]{:S(2)}) collective-permute-start(bf16[4,96,768]{2,1,0:T(8,128)(2,1)S(1)} %collective-permute-done.25), channel_id=1, source_target_pairs={{0,8},{4,12},{8,0},{12,4},{16,24},{20,28},{24,16},{28,20},{1,9},{5... | collective-permute-start | bytes 1769480 | tf_op jit(solution)/shard_map/ppermute | solution.py:828
  119.6 24.3 %collective-permute-start.38 = (bf16[4,96,768]{2,1,0:T(8,128)(2,1)}, bf16[4,96,768]{2,1,0:T(8,128)(2,1)S(1)}, u32[]{:S(2)}, u32[]{:S(2)}) collective-permute-start(bf16[4,96,768]{2,1,0:T(8,128)(2,1)} %get-tuple-element.222), channel_id=1, source_target_pairs={{0,16},{4,20},{8,24},{12,28},{16,0},{20,4},{24,8},{28,12},{1,17},{... | collective-permute-start | bytes 1769480 | tf_op jit(solution)/shard_map/ppermute | solution.py:828
  120.2 16.0 %collective-permute-start.35 = (bf16[2,96,768]{2,1,0:T(8,128)(2,1)}, bf16[2,96,768]{2,1,0:T(8,128)(2,1)}, u32[]{:S(2)}, u32[]{:S(2)}) collective-permute-start(bf16[2,96,768]{2,1,0:T(8,128)(2,1)} %get-tuple-element.197), channel_id=1, source_target_pairs={{0,2},{1,3},{2,0},{3,1},{4,6},{5,7},{6,4},{7,5},{8,10},{9,11},{10,... | collective-permute-start | bytes 884744 | tf_op jit(solution)/shard_map/ppermute | solution.py:831
  120.5 23.6 %collective-permute-start.36 = (bf16[2,96,768]{2,1,0:T(8,128)(2,1)}, bf16[2,96,768]{2,1,0:T(8,128)(2,1)S(1)}, u32[]{:S(2)}, u32[]{:S(2)}) collective-permute-start(bf16[2,96,768]{2,1,0:T(8,128)(2,1)} %get-tuple-element.207), channel_id=1, source_target_pairs={{0,1},{1,0},{2,3},{3,2},{4,5},{5,4},{6,7},{7,6},{8,9},{9,8},{10,11... | collective-permute-start | bytes 884744 | tf_op jit(solution)/shard_map/ppermute | solution.py:831
  122.2 23.4 %collective-permute-start.40 = (bf16[4,96,768]{2,1,0:T(8,128)(2,1)}, bf16[4,96,768]{2,1,0:T(8,128)(2,1)}, u32[]{:S(2)}, u32[]{:S(2)}) collective-permute-start(bf16[4,96,768]{2,1,0:T(8,128)(2,1)} %get-tuple-element.186), channel_id=1, source_target_pairs={{0,4},{4,0},{8,12},{12,8},{16,20},{20,16},{24,28},{28,24},{1,5},{5... | collective-permute-start | bytes 1769480 | tf_op jit(solution)/shard_map/ppermute | solution.py:828
  144.1 15.7 %collective-permute-start.45 = (bf16[4,96,768]{2,1,0:T(8,128)(2,1)S(1)}, bf16[4,96,768]{2,1,0:T(8,128)(2,1)S(1)}, u32[]{:S(2)}, u32[]{:S(2)}) collective-permute-start(bf16[4,96,768]{2,1,0:T(8,128)(2,1)S(1)} %collective-permute-done.34), channel_id=1, source_target_pairs={{0,16},{4,20},{8,24},{12,28},{16,0},{20,4},{24,8},{28,12},{1,17},{... | collective-permute-start | bytes 1769480 | tf_op jit(solution)/shard_map/ppermute | solution.py:828
  145.6 15.5 %collective-permute-start.37 = (bf16[2,96,768]{2,1,0:T(8,128)(2,1)}, bf16[2,96,768]{2,1,0:T(8,128)(2,1)}, u32[]{:S(2)}, u32[]{:S(2)}) collective-permute-start(bf16[2,96,768]{2,1,0:T(8,128)(2,1)} %get-tuple-element.207), channel_id=1, source_target_pairs={{0,2},{1,3},{2,0},{3,1},{4,6},{5,7},{6,4},{7,5},{8,10},{9,11},{10,... | collective-permute-start | bytes 884744 | tf_op jit(solution)/shard_map/ppermute | solution.py:831
  145.6 26.2 %collective-permute-start.47 = (bf16[4,96,768]{2,1,0:T(8,128)(2,1)S(1)}, bf16[4,96,768]{2,1,0:T(8,128)(2,1)S(1)}, u32[]{:S(2)}, u32[]{:S(2)}) collective-permute-start(bf16[4,96,768]{2,1,0:T(8,128)(2,1)S(1)} %collective-permute-done.34), channel_id=1, source_target_pairs={{0,4},{4,0},{8,12},{12,8},{16,20},{20,16},{24,28},{28,24},{1,5},{5... | collective-permute-start | bytes 1769480 | tf_op jit(solution)/shard_map/ppermute | solution.py:828
  145.9 26.0 %collective-permute-start.48 = (bf16[4,96,768]{2,1,0:T(8,128)(2,1)S(1)}, bf16[4,96,768]{2,1,0:T(8,128)(2,1)S(1)}, u32[]{:S(2)}, u32[]{:S(2)}) collective-permute-start(bf16[4,96,768]{2,1,0:T(8,128)(2,1)S(1)} %collective-permute-done.38), channel_id=1, source_target_pairs={{0,4},{4,0},{8,12},{12,8},{16,20},{20,16},{24,28},{28,24},{1,5},{5... | collective-permute-start | bytes 1769480 | tf_op jit(solution)/shard_map/ppermute | solution.py:828
  146.4 25.3 %collective-permute-start.46 = (bf16[4,96,768]{2,1,0:T(8,128)(2,1)}, bf16[4,96,768]{2,1,0:T(8,128)(2,1)S(1)}, u32[]{:S(2)}, u32[]{:S(2)}) collective-permute-start(bf16[4,96,768]{2,1,0:T(8,128)(2,1)} %get-tuple-element.222), channel_id=1, source_target_pairs={{0,4},{4,0},{8,12},{12,8},{16,20},{20,16},{24,28},{28,24},{1,5},{5... | collective-permute-start | bytes 1769480 | tf_op jit(solution)/shard_map/ppermute | solution.py:828
  159.7 12.1 %collective-permute-start.49 = (bf16[4,96,768]{2,1,0:T(8,128)(2,1)S(1)}, bf16[4,96,768]{2,1,0:T(8,128)(2,1)S(1)}, u32[]{:S(2)}, u32[]{:S(2)}) collective-permute-start(bf16[4,96,768]{2,1,0:T(8,128)(2,1)S(1)} %collective-permute-done.45), channel_id=1, source_target_pairs={{0,4},{4,0},{8,12},{12,8},{16,20},{20,16},{24,28},{28,24},{1,5},{5... | collective-permute-start | bytes 1769480 | tf_op jit(solution)/shard_map/ppermute | solution.py:828
  170.3 14.9 %collective-permute-start.50 = (bf16[2,96,768]{2,1,0:T(8,128)(2,1)}, bf16[2,96,768]{2,1,0:T(8,128)(2,1)S(1)}, u32[]{:S(2)}, u32[]{:S(2)}) collective-permute-start(bf16[2,96,768]{2,1,0:T(8,128)(2,1)} %collective-permute-done.37), channel_id=1, source_target_pairs={{0,1},{1,0},{2,3},{3,2},{4,5},{5,4},{6,7},{7,6},{8,9},{9,8},{10,11... | collective-permute-start | bytes 884744 | tf_op jit(solution)/shard_map/ppermute | solution.py:831
  171.7 16.2 %collective-permute-start.51 = (bf16[2,4,96,768]{3,2,0,1:T(8,128)(2,1)S(1)}, bf16[2,4,96,768]{3,2,0,1:T(8,128)(2,1)}, u32[]{:S(2)}, u32[]{:S(2)}) collective-permute-start(bf16[2,4,96,768]{3,2,0,1:T(8,128)(2,1)S(1)} %pad_maximum_fusion), channel_id=1, source_target_pairs={{0,4},{4,0},{8,12},{12,8},{16,20},{20,16},{24,28},{28,24},{1,5},{5... | collective-permute-start | bytes 3538952 | tf_op jit(solution)/shard_map/ppermute | solution.py:828
  231.5 19.9 %collective-permute-start.53 = (bf16[4,4,96,768]{3,2,1,0:T(8,128)(2,1)}, bf16[4,4,96,768]{3,2,1,0:T(8,128)(2,1)S(1)}, u32[]{:S(2)}, u32[]{:S(2)}) collective-permute-start(bf16[4,4,96,768]{3,2,1,0:T(8,128)(2,1)} %get-tuple-element.245), channel_id=1, source_target_pairs={{0,4},{4,0},{8,12},{12,8},{16,20},{20,16},{24,28},{28,24},{1,5},{5... | collective-permute-start | bytes 7077896 | tf_op jit(solution)/shard_map/ppermute | solution.py:828
  251.0 39.0 %collective-permute-start.55 = (bf16[4,4,96,768]{3,2,1,0:T(8,128)(2,1)}, bf16[4,4,96,768]{3,2,1,0:T(8,128)(2,1)S(1)}, u32[]{:S(2)}, u32[]{:S(2)}) collective-permute-start(bf16[4,4,96,768]{3,2,1,0:T(8,128)(2,1)} %get-tuple-element.254), channel_id=1, source_target_pairs={{0,4},{4,0},{8,12},{12,8},{16,20},{20,16},{24,28},{28,24},{1,5},{5... | collective-permute-start | bytes 7077896 | tf_op jit(solution)/shard_map/ppermute | solution.py:828
  271.9 35.2 %collective-permute-start.58 = (bf16[4,4,96,768]{3,2,1,0:T(8,128)(2,1)}, bf16[4,4,96,768]{3,2,1,0:T(8,128)(2,1)}, u32[]{:S(2)}, u32[]{:S(2)}) collective-permute-start(bf16[4,4,96,768]{3,2,1,0:T(8,128)(2,1)} %get-tuple-element.262), channel_id=1, source_target_pairs={{0,4},{4,0},{8,12},{12,8},{16,20},{20,16},{24,28},{28,24},{1,5},{5... | collective-permute-start | bytes 7077896 | tf_op jit(solution)/shard_map/ppermute | solution.py:828
  272.3 16.2 %collective-permute-start.54 = (bf16[4,96,768]{2,1,0:T(8,128)(2,1)S(1)}, bf16[4,96,768]{2,1,0:T(8,128)(2,1)S(1)}, u32[]{:S(2)}, u32[]{:S(2)}) collective-permute-start(bf16[4,96,768]{2,1,0:T(8,128)(2,1)S(1)} %copy-done.31), channel_id=1, source_target_pairs={{0,16},{4,20},{8,24},{12,28},{16,0},{20,4},{24,8},{28,12},{1,17},{... | collective-permute-start | bytes 1769480 | tf_op jit(solution)/shard_map/ppermute | solution.py:828
  272.9 27.6 %collective-permute-start.56 = (bf16[4,96,768]{2,1,0:T(8,128)(2,1)S(1)}, bf16[4,96,768]{2,1,0:T(8,128)(2,1)}, u32[]{:S(2)}, u32[]{:S(2)}) collective-permute-start(bf16[4,96,768]{2,1,0:T(8,128)(2,1)S(1)} %copy-done.30), channel_id=1, source_target_pairs={{0,16},{4,20},{8,24},{12,28},{16,0},{20,4},{24,8},{28,12},{1,17},{... | collective-permute-start | bytes 1769480 | tf_op jit(solution)/shard_map/ppermute | solution.py:828
  289.4 14.4 %collective-permute-start.57 = (bf16[4,96,768]{2,1,0:T(8,128)(2,1)}, bf16[4,96,768]{2,1,0:T(8,128)(2,1)}, u32[]{:S(2)}, u32[]{:S(2)}) collective-permute-start(bf16[4,96,768]{2,1,0:T(8,128)(2,1)} %add_convert_fusion.10), channel_id=1, source_target_pairs={{0,8},{4,12},{8,0},{12,4},{16,24},{20,28},{24,16},{28,20},{1,9},{5... | collective-permute-start | bytes 1769480 | tf_op jit(solution)/shard_map/ppermute | solution.py:828
  300.5 24.1 %collective-permute-start.62 = (bf16[4,96,768]{2,1,0:T(8,128)(2,1)}, bf16[4,96,768]{2,1,0:T(8,128)(2,1)S(1)}, u32[]{:S(2)}, u32[]{:S(2)}) collective-permute-start(bf16[4,96,768]{2,1,0:T(8,128)(2,1)} %get-tuple-element.270), channel_id=1, source_target_pairs={{0,4},{4,0},{8,12},{12,8},{16,20},{20,16},{24,28},{28,24},{1,5},{5... | collective-permute-start | bytes 1769480 | tf_op jit(solution)/shard_map/ppermute | solution.py:828
  305.3 15.6 %collective-permute-start.59 = (bf16[2,96,768]{2,1,0:T(8,128)(2,1)S(1)}, bf16[2,96,768]{2,1,0:T(8,128)(2,1)}, u32[]{:S(2)}, u32[]{:S(2)}) collective-permute-start(bf16[2,96,768]{2,1,0:T(8,128)(2,1)S(1)} %get-tuple-element.382), channel_id=1, source_target_pairs={{0,1},{1,0},{2,3},{3,2},{4,5},{5,4},{6,7},{7,6},{8,9},{9,8},{10,11... | collective-permute-start | bytes 884744 | tf_op jit(solution)/shard_map/ppermute | solution.py:831
  309.9 19.6 %collective-permute-start.61 = (bf16[2,2,96,768]{3,2,0,1:T(8,128)(2,1)}, bf16[2,2,96,768]{3,2,0,1:T(8,128)(2,1)}, u32[]{:S(2)}, u32[]{:S(2)}) collective-permute-start(bf16[2,2,96,768]{3,2,0,1:T(8,128)(2,1)} %get-tuple-element.373), channel_id=1, source_target_pairs={{0,1},{1,0},{2,3},{3,2},{4,5},{5,4},{6,7},{7,6},{8,9},{9,8},{10,11... | collective-permute-start | bytes 1769480 | tf_op jit(solution)/shard_map/ppermute | solution.py:831
  322.0 22.7 %collective-permute-start.60 = (bf16[96,768]{1,0:T(8,128)(2,1)S(1)}, bf16[96,768]{1,0:T(8,128)(2,1)S(1)}, u32[]{:S(2)}, u32[]{:S(2)}) collective-permute-start(bf16[96,768]{1,0:T(8,128)(2,1)S(1)} %get-tuple-element.406), channel_id=1, source_target_pairs={{0,2},{1,3},{2,0},{3,1},{4,6},{5,7},{6,4},{7,5},{8,10},{9,11},{10,... | collective-permute-start | bytes 442376 | tf_op jit(solution)/shard_map/ppermute | solution.py:831
  324.5 21.0 %collective-permute-start.63 = (bf16[4,96,768]{2,1,0:T(8,128)(2,1)S(1)}, bf16[4,96,768]{2,1,0:T(8,128)(2,1)S(1)}, u32[]{:S(2)}, u32[]{:S(2)}) collective-permute-start(bf16[4,96,768]{2,1,0:T(8,128)(2,1)S(1)} %get-tuple-element.275), channel_id=1, source_target_pairs={{0,8},{4,12},{8,0},{12,4},{16,24},{20,28},{24,16},{28,20},{1,9},{5... | collective-permute-start | bytes 1769480 | tf_op jit(solution)/shard_map/ppermute | solution.py:828
  325.1 19.6 %collective-permute-start.64 = (bf16[2,2,96,768]{3,2,1,0:T(8,128)(2,1)S(1)}, bf16[2,2,96,768]{3,2,1,0:T(8,128)(2,1)S(1)}, u32[]{:S(2)}, u32[]{:S(2)}) collective-permute-start(bf16[2,2,96,768]{3,2,1,0:T(8,128)(2,1)S(1)} %add_convert_fusion.2), channel_id=1, source_target_pairs={{0,1},{1,0},{2,3},{3,2},{4,5},{5,4},{6,7},{7,6},{8,9},{9,8},{10,11... | collective-permute-start | bytes 1769480 | tf_op jit(solution)/shard_map/ppermute | solution.py:831
  325.6 20.1 %collective-permute-start.65 = (bf16[2,96,768]{2,1,0:T(8,128)(2,1)S(1)}, bf16[2,96,768]{2,1,0:T(8,128)(2,1)S(1)}, u32[]{:S(2)}, u32[]{:S(2)}) collective-permute-start(bf16[2,96,768]{2,1,0:T(8,128)(2,1)S(1)} %pad_maximum_fusion.11), channel_id=1, source_target_pairs={{0,16},{4,20},{8,24},{12,28},{16,0},{20,4},{24,8},{28,12},{1,17},{... | collective-permute-start | bytes 884744 | tf_op jit(solution)/shard_map/ppermute | solution.py:828
  346.5 17.8 %collective-permute-start.67 = (bf16[4,96,768]{2,1,0:T(8,128)(2,1)S(1)}, bf16[4,96,768]{2,1,0:T(8,128)(2,1)}, u32[]{:S(2)}, u32[]{:S(2)}) collective-permute-start(bf16[4,96,768]{2,1,0:T(8,128)(2,1)S(1)} %add_convert_fusion.1), channel_id=1, source_target_pairs={{0,16},{4,20},{8,24},{12,28},{16,0},{20,4},{24,8},{28,12},{1,17},{... | collective-permute-start | bytes 1769480 | tf_op jit(solution)/shard_map/ppermute | solution.py:828
  347.0 12.7 %collective-permute-start.70 = (bf16[96,768]{1,0:T(8,128)(2,1)}, bf16[96,768]{1,0:T(8,128)(2,1)}, u32[]{:S(2)}, u32[]{:S(2)}) collective-permute-start(bf16[96,768]{1,0:T(8,128)(2,1)} %get-tuple-element.428), channel_id=1, source_target_pairs={{0,8},{4,12},{8,0},{12,4},{16,24},{20,28},{24,16},{28,20},{1,9},{5... | collective-permute-start | bytes 442376 | tf_op jit(solution)/shard_map/ppermute | solution.py:828
  347.4 16.9 %collective-permute-start.66 = (bf16[4,96,768]{2,1,0:T(8,128)(2,1)S(1)}, bf16[4,96,768]{2,1,0:T(8,128)(2,1)}, u32[]{:S(2)}, u32[]{:S(2)}) collective-permute-start(bf16[4,96,768]{2,1,0:T(8,128)(2,1)S(1)} %get-tuple-element.281), channel_id=1, source_target_pairs={{0,8},{4,12},{8,0},{12,4},{16,24},{20,28},{24,16},{28,20},{1,9},{5... | collective-permute-start | bytes 1769480 | tf_op jit(solution)/shard_map/ppermute | solution.py:828
  349.1 14.1 %collective-permute-start.69 = (bf16[2,96,768]{2,1,0:T(8,128)(2,1)}, bf16[2,96,768]{2,1,0:T(8,128)(2,1)}, u32[]{:S(2)}, u32[]{:S(2)}) collective-permute-start(bf16[2,96,768]{2,1,0:T(8,128)(2,1)} %get-tuple-element.286), channel_id=1, source_target_pairs={{0,2},{1,3},{2,0},{3,1},{4,6},{5,7},{6,4},{7,5},{8,10},{9,11},{10,... | collective-permute-start | bytes 884744 | tf_op jit(solution)/shard_map/ppermute | solution.py:831
  349.6 18.3 %collective-permute-start.71 = (bf16[4,96,768]{2,1,0:T(8,128)(2,1)}, bf16[4,96,768]{2,1,0:T(8,128)(2,1)S(1)}, u32[]{:S(2)}, u32[]{:S(2)}) collective-permute-start(bf16[4,96,768]{2,1,0:T(8,128)(2,1)} %get-tuple-element.290), channel_id=1, source_target_pairs={{0,4},{4,0},{8,12},{12,8},{16,20},{20,16},{24,28},{28,24},{1,5},{5... | collective-permute-start | bytes 1769480 | tf_op jit(solution)/shard_map/ppermute | solution.py:828
  359.7 22.3 %collective-permute-start.72 = (bf16[2,96,768]{2,1,0:T(8,128)(2,1)}, bf16[2,96,768]{2,1,0:T(8,128)(2,1)S(1)}, u32[]{:S(2)}, u32[]{:S(2)}) collective-permute-start(bf16[2,96,768]{2,1,0:T(8,128)(2,1)} %fusion.18), channel_id=1, source_target_pairs={{0,2},{1,3},{2,0},{3,1},{4,6},{5,7},{6,4},{7,5},{8,10},{9,11},{10,... | collective-permute-start | bytes 884744 | tf_op jit(solution)/shard_map/ppermute | solution.py:831
  363.2 19.0 %collective-permute-start.73 = (bf16[96,384]{1,0:T(8,128)(2,1)S(1)}, bf16[96,384]{1,0:T(8,128)(2,1)S(1)}, u32[]{:S(2)}, u32[]{:S(2)}) collective-permute-start(bf16[96,384]{1,0:T(8,128)(2,1)S(1)} %pad_maximum_fusion.20), channel_id=1, source_target_pairs={{0,1},{1,0},{2,3},{3,2},{4,5},{5,4},{6,7},{7,6},{8,9},{9,8},{10,11... | collective-permute-start | bytes 221192 | tf_op jit(solution)/shard_map/ppermute | solution.py:831
  365.8 19.6 %collective-permute-start.68 = (bf16[2,96,768]{2,1,0:T(8,128)(2,1)S(1)}, bf16[2,96,768]{2,1,0:T(8,128)(2,1)S(1)}, u32[]{:S(2)}, u32[]{:S(2)}) collective-permute-start(bf16[2,96,768]{2,1,0:T(8,128)(2,1)S(1)} %get-tuple-element.380), channel_id=1, source_target_pairs={{0,1},{1,0},{2,3},{3,2},{4,5},{5,4},{6,7},{7,6},{8,9},{9,8},{10,11... | collective-permute-start | bytes 884744 | tf_op jit(solution)/shard_map/ppermute | solution.py:831
  368.1 17.3 %collective-permute-start.74 = (bf16[2,96,768]{2,1,0:T(8,128)(2,1)S(1)}, bf16[2,96,768]{2,1,0:T(8,128)(2,1)S(1)}, u32[]{:S(2)}, u32[]{:S(2)}) collective-permute-start(bf16[2,96,768]{2,1,0:T(8,128)(2,1)S(1)} %pad_maximum_fusion.12), channel_id=1, source_target_pairs={{0,8},{4,12},{8,0},{12,4},{16,24},{20,28},{24,16},{28,20},{1,9},{5... | collective-permute-start | bytes 884744 | tf_op jit(solution)/shard_map/ppermute | solution.py:828
  383.0 14.4 %collective-permute-start.76 = (bf16[96,192]{1,0:T(8,128)(2,1)}, bf16[96,192]{1,0:T(8,128)(2,1)}, u32[]{:S(2)}, u32[]{:S(2)}) collective-permute-start(bf16[96,192]{1,0:T(8,128)(2,1)} %pad_maximum_fusion.27), channel_id=1, source_target_pairs={{0,2},{1,3},{2,0},{3,1},{4,6},{5,7},{6,4},{7,5},{8,10},{9,11},{10,... | collective-permute-start | bytes 110600 | tf_op jit(solution)/shard_map/ppermute | solution.py:831
  384.0 13.4 %collective-permute-start.77 = (bf16[2,96,768]{2,1,0:T(8,128)(2,1)S(1)}, bf16[2,96,768]{2,1,0:T(8,128)(2,1)S(1)}, u32[]{:S(2)}, u32[]{:S(2)}) collective-permute-start(bf16[2,96,768]{2,1,0:T(8,128)(2,1)S(1)} %add_convert_fusion.14), channel_id=1, source_target_pairs={{0,16},{4,20},{8,24},{12,28},{16,0},{20,4},{24,8},{28,12},{1,17},{... | collective-permute-start | bytes 884744 | tf_op jit(solution)/shard_map/ppermute | solution.py:828
  385.3 15.7 %collective-permute-start.79 = (bf16[4,96,768]{2,1,0:T(8,128)(2,1)}, bf16[4,96,768]{2,1,0:T(8,128)(2,1)S(1)}, u32[]{:S(2)}, u32[]{:S(2)}) collective-permute-start(bf16[4,96,768]{2,1,0:T(8,128)(2,1)} %get-tuple-element.306), channel_id=1, source_target_pairs={{0,4},{4,0},{8,12},{12,8},{16,20},{20,16},{24,28},{28,24},{1,5},{5... | collective-permute-start | bytes 1769480 | tf_op jit(solution)/shard_map/ppermute | solution.py:828
  385.5 15.3 %collective-permute-start.75 = (bf16[96,768]{1,0:T(8,128)(2,1)S(1)}, bf16[96,768]{1,0:T(8,128)(2,1)S(1)}, u32[]{:S(2)}, u32[]{:S(2)}) collective-permute-start(bf16[96,768]{1,0:T(8,128)(2,1)S(1)} %get-tuple-element.403), channel_id=1, source_target_pairs={{0,2},{1,3},{2,0},{3,1},{4,6},{5,7},{6,4},{7,5},{8,10},{9,11},{10,... | collective-permute-start | bytes 442376 | tf_op jit(solution)/shard_map/ppermute | solution.py:831
  387.6 13.1 %collective-permute-start.78 = (bf16[96,768]{1,0:T(8,128)(2,1)S(1)}, bf16[96,768]{1,0:T(8,128)(2,1)S(1)}, u32[]{:S(2)}, u32[]{:S(2)}) collective-permute-start(bf16[96,768]{1,0:T(8,128)(2,1)S(1)} %get-tuple-element.426), channel_id=1, source_target_pairs={{0,16},{4,20},{8,24},{12,28},{16,0},{20,4},{24,8},{28,12},{1,17},{... | collective-permute-start | bytes 442376 | tf_op jit(solution)/shard_map/ppermute | solution.py:828
  397.5 24.2 %collective-permute-start.98 = (bf16[96,768]{1,0:T(8,128)(2,1)S(1)}, bf16[96,768]{1,0:T(8,128)(2,1)S(1)}, u32[]{:S(2)}, u32[]{:S(2)}) collective-permute-start(bf16[96,768]{1,0:T(8,128)(2,1)S(1)} %get-tuple-element.401), channel_id=1, source_target_pairs={{0,8},{4,12},{8,0},{12,4},{16,24},{20,28},{24,16},{28,20},{1,9},{5... | collective-permute-start | bytes 442376 | tf_op jit(solution)/shard_map/ppermute | solution.py:828
  400.9 17.7 %collective-permute-start.80 = (bf16[96,384]{1,0:T(8,128)(2,1)S(1)}, bf16[96,384]{1,0:T(8,128)(2,1)S(1)}, u32[]{:S(2)}, u32[]{:S(2)}) collective-permute-start(bf16[96,384]{1,0:T(8,128)(2,1)S(1)} %pad_maximum_fusion.22), channel_id=1, source_target_pairs={{0,1},{1,0},{2,3},{3,2},{4,5},{5,4},{6,7},{7,6},{8,9},{9,8},{10,11... | collective-permute-start | bytes 221192 | tf_op jit(solution)/shard_map/ppermute | solution.py:831
  401.2 22.6 %collective-permute-start.82 = (bf16[2,96,768]{2,1,0:T(8,128)(2,1)S(1)}, bf16[2,96,768]{2,1,0:T(8,128)(2,1)S(1)}, u32[]{:S(2)}, u32[]{:S(2)}) collective-permute-start(bf16[2,96,768]{2,1,0:T(8,128)(2,1)S(1)} %pad_maximum_fusion.13), channel_id=1, source_target_pairs={{0,16},{4,20},{8,24},{12,28},{16,0},{20,4},{24,8},{28,12},{1,17},{... | collective-permute-start | bytes 884744 | tf_op jit(solution)/shard_map/ppermute | solution.py:828
  416.4 17.9 %collective-permute-start.89 = (bf16[4,96,768]{2,1,0:T(8,128)(2,1)}, bf16[4,96,768]{2,1,0:T(8,128)(2,1)S(1)}, u32[]{:S(2)}, u32[]{:S(2)}) collective-permute-start(bf16[4,96,768]{2,1,0:T(8,128)(2,1)} %get-tuple-element.327), channel_id=1, source_target_pairs={{0,4},{4,0},{8,12},{12,8},{16,20},{20,16},{24,28},{28,24},{1,5},{5... | collective-permute-start | bytes 1769480 | tf_op jit(solution)/shard_map/ppermute | solution.py:828
  418.7 11.8 %collective-permute-start.81 = (bf16[96,192]{1,0:T(8,128)(2,1)S(1)}, bf16[96,192]{1,0:T(8,128)(2,1)S(1)}, u32[]{:S(2)}, u32[]{:S(2)}) collective-permute-start(bf16[96,192]{1,0:T(8,128)(2,1)S(1)} %pad_maximum_fusion.28), channel_id=1, source_target_pairs={{0,2},{1,3},{2,0},{3,1},{4,6},{5,7},{6,4},{7,5},{8,10},{9,11},{10,... | collective-permute-start | bytes 110600 | tf_op jit(solution)/shard_map/ppermute | solution.py:831
  430.0 17.0 %collective-permute-start.88 = (f32[8,768]{1,0:T(8,128)S(1)}, f32[8,768]{1,0:T(8,128)S(1)}, u32[]{:S(2)}, u32[]{:S(2)}) collective-permute-start(f32[8,768]{1,0:T(8,128)S(1)} %add.383), channel_id=1, source_target_pairs={{0,16},{4,20},{8,24},{12,28},{16,0},{20,4},{24,8},{28,12},{1,17},{... | collective-permute-start | bytes 73736 | tf_op jit(solution)/shard_map/ppermute | solution.py:828
  (120 other events, 948.5 us)
